TPU v7x, 128 devices: a whole 4x4x4 slice. The times are simulated.
128 devices in a mesh: wide: 16 (over z, y), narrow: 8 (over x, core).
Axes of the slice: x: 4, y: 4, z: 4, core: 2. Of those that a mesh axis runs over, the one named last changes fastest.
Arguments:
- hidden_in: bfloat16 [2048, 2048], P('wide'), may hold values from -6 to 6
- attn_gain: float32 [2048], replicated, may hold values from 0.1 to 1.9
- w_qkv: bfloat16 [2048, 4096], P('wide', 'narrow'), may hold values from -0.125 to 0.125
- q_gain: float32 [128], replicated, may hold values from 0.5 to 10
- k_gain: float32 [128], replicated, may hold values from 0.1 to 1.9
- w_out: bfloat16 [2048, 2048], P('narrow', 'wide'), may hold values from -0.125 to 0.125
- prefix_cache: bfloat16 [2, 64, 4096, 1024], P(None, 'wide', None, 'narrow'), may hold values from -150 to 150
- tail_cache: bfloat16 [2, 1024, 256, 1024], P(None, 'wide', None, 'narrow'), may hold values from -150 to 150
- prompt_lens: int32 [64], replicated, may hold values from 1 to 4096
- tail_lens: int32 [1024], P('wide'), may hold values from 1 to 256
- slot_prompt: int32 [64], replicated, may hold values from 0 to 63, each once
Outputs:
- hidden_out: bfloat16 [2048, 2048], P('wide')
- scores: float32 [2048, 16], P('wide', 'narrow')
- new_cache: bfloat16 [2, 2048, 1024], P(None, 'wide', 'narrow')
Inputs may be any that keep to these rules, and one draw needn't show every extreme that they name: `slot_prompt`: each prompt is held in exactly one slot.
All inputs are finite; a program needn't handle non-finite values.
Results may differ from a plain program's by a relative error of at most 0.007.
Values may be sent and summed in bfloat16 or wider, within the bound.
No kernel may reach another device: no remote copies, remote signals or barrier semaphores. Data moves between devices by JAX's collectives and lax.ppermute only.
A program may use at most 128 MiB of HBM per device.

v0:
```python
import math

import jax
import jax.numpy as jnp
from jax import lax
from jax.sharding import PartitionSpec as P

HEADS = 16
KVH = 8
HD = 128
CONT = 16
NEW = 2
PLEN = 4096
TLEN = 256


epsilon = 1e-06
rope_base = 1000000.0
negative_fill = -1e30


def rms_norm(values, norm_gain):
    mean_square = jnp.mean(values * values, axis=-1, keepdims=True)
    return values * lax.rsqrt(mean_square + epsilon) * norm_gain


def rotate(values, position):
    half_width = values.shape[-1] // 2
    channel = jnp.arange(half_width, dtype=jnp.float32)
    inverse_freq = jnp.exp(channel * (-2.0 / values.shape[-1]) * math.log(rope_base))
    angles = position[..., None] * inverse_freq
    cosine = jnp.cos(angles)
    sines = jnp.sin(angles)
    leading = values[..., :half_width]
    trailing = values[..., half_width:]
    return jnp.concatenate(
        [leading * cosine - trailing * sines, trailing * cosine + leading * sines], axis=-1
    )


def lookup(indices, lookup_table):
    entries = jnp.arange(lookup_table.shape[0], dtype=jnp.int32)
    return jnp.sum(
        jnp.where(indices[:, None] == entries[None, :], lookup_table[None, :], 0), axis=1
    )


def combine_parts(prefix_out, prefix_lse, tail_out, tail_lse):
    highest = jnp.maximum(prefix_lse, tail_lse)
    prefix_share = jnp.exp(prefix_lse - highest)
    tail_share = jnp.exp(tail_lse - highest)
    merged = (prefix_share[..., None] * prefix_out + tail_share[..., None] * tail_out) / (
        prefix_share + tail_share
    )[..., None]
    return (merged.astype(jnp.bfloat16), highest + jnp.log(prefix_share + tail_share))


def body(
    hidden_in,
    attn_gain,
    w_qkv,
    q_gain,
    k_gain,
    w_out,
    prefix_cache,
    tail_cache,
    prompt_lens,
    tail_lens,
    slot_prompt,
):
    group_size = HEADS // KVH
    per_prompt = CONT * NEW
    scaling = HD ** (-0.5)
    wide_index = lax.axis_index("wide")
    rows_dev = hidden_in.shape[0]
    conts_dev = tail_cache.shape[1]
    slot_count = prefix_cache.shape[1]
    groups = prefix_cache.shape[3] // HD
    heads_dev = groups * group_size
    residual = hidden_in.astype(jnp.float32)
    normed = rms_norm(residual, attn_gain).astype(jnp.bfloat16)
    regrouped = lax.all_to_all(normed, "wide", split_axis=1, concat_axis=0, tiled=True)
    projected = lax.psum_scatter(
        jnp.dot(regrouped, w_qkv, preferred_element_type=jnp.float32),
        "wide",
        scatter_dimension=0,
        tiled=True,
    )
    projected = projected.reshape(rows_dev, groups, group_size + 2, HD)
    row_index = wide_index * rows_dev + jnp.arange(rows_dev, dtype=jnp.int32)
    continuation = row_index // NEW
    prompt_index = continuation // CONT
    step_index = row_index % NEW
    local_cont = continuation - wide_index * conts_dev
    position = (
        lookup(prompt_index, prompt_lens) + lookup(local_cont, tail_lens) + step_index
    ).astype(jnp.float32)
    queries = rotate(
        rms_norm(projected[:, :, :group_size], q_gain), position[:, None, None]
    ).astype(jnp.bfloat16)
    new_keys = rotate(rms_norm(projected[:, :, group_size], k_gain), position[:, None]).astype(
        jnp.bfloat16
    )
    new_values = projected[:, :, group_size + 1].astype(jnp.bfloat16)
    everyone = lax.all_gather(queries.reshape(rows_dev, heads_dev * HD), "wide", axis=0, tiled=True)
    global_slot = wide_index * slot_count + jnp.arange(slot_count, dtype=jnp.int32)
    owners = lookup(global_slot, slot_prompt)
    slot_length = lookup(owners, prompt_lens)
    first_row = owners * per_prompt
    chosen = jax.vmap(
        lambda row_begin: lax.dynamic_slice_in_dim(everyone, row_begin, per_prompt, 0)
    )(first_row)
    chosen = chosen.reshape(slot_count, per_prompt, groups, group_size, HD)
    held_keys = prefix_cache[0].reshape(slot_count, PLEN, groups, HD)
    held_values = prefix_cache[1].reshape(slot_count, PLEN, groups, HD)
    prefix_scores = (
        jnp.einsum("srghd,skgd->srghk", chosen, held_keys, preferred_element_type=jnp.float32)
        * scaling
    )
    alive = jnp.arange(PLEN, dtype=jnp.int32)[None, :] < slot_length[:, None]
    prefix_scores = jnp.where(alive[:, None, None, None, :], prefix_scores, negative_fill)
    prefix_max = jnp.max(prefix_scores, axis=-1)
    prefix_weights = jnp.exp(prefix_scores - prefix_max[..., None])
    prefix_total = jnp.sum(prefix_weights, axis=-1)
    prefix_num = jnp.einsum(
        "srghk,skgd->srghd",
        prefix_weights.astype(jnp.bfloat16),
        held_values,
        preferred_element_type=jnp.float32,
    )
    prefix_out = prefix_num / prefix_total[..., None]
    prefix_lse = prefix_max + jnp.log(prefix_total)
    spread_out = jnp.zeros((everyone.shape[0], heads_dev * HD), jnp.float32)
    spread_lse = jnp.zeros((everyone.shape[0], heads_dev), jnp.float32)
    for slot_number in range(slot_count):
        spread_out = lax.dynamic_update_slice_in_dim(
            spread_out,
            prefix_out[slot_number].reshape(per_prompt, heads_dev * HD),
            first_row[slot_number],
            0,
        )
        spread_lse = lax.dynamic_update_slice_in_dim(
            spread_lse,
            prefix_lse[slot_number].reshape(per_prompt, heads_dev),
            first_row[slot_number],
            0,
        )
    mine_out, mine_lse = (
        lax.psum_scatter(spread_out, "wide", scatter_dimension=0, tiled=True),
        lax.psum_scatter(spread_lse, "wide", scatter_dimension=0, tiled=True),
    )
    tail_query = queries.reshape(conts_dev, NEW, groups, group_size, HD)
    tail_keys = tail_cache[0].reshape(conts_dev, TLEN, groups, HD)
    tail_values = tail_cache[1].reshape(conts_dev, TLEN, groups, HD)
    own_keys = new_keys.reshape(conts_dev, NEW, groups, HD)
    own_values = new_values.reshape(conts_dev, NEW, groups, HD)
    cached_scores = (
        jnp.einsum("ctghd,csgd->ctghs", tail_query, tail_keys, preferred_element_type=jnp.float32)
        * scaling
    )
    cached_alive = jnp.arange(TLEN, dtype=jnp.int32)[None, :] < tail_lens[:, None]
    cached_scores = jnp.where(cached_alive[:, None, None, None, :], cached_scores, negative_fill)
    own_scores = (
        jnp.einsum("ctghd,cugd->ctghu", tail_query, own_keys, preferred_element_type=jnp.float32)
        * scaling
    )
    causal = jnp.arange(NEW)[None, :] <= jnp.arange(NEW)[:, None]
    own_scores = jnp.where(causal[None, :, None, None, :], own_scores, negative_fill)
    tail_max = jnp.maximum(jnp.max(cached_scores, axis=-1), jnp.max(own_scores, axis=-1))
    cached_weights = jnp.exp(cached_scores - tail_max[..., None])
    own_weights = jnp.exp(own_scores - tail_max[..., None])
    tail_total = jnp.sum(cached_weights, axis=-1) + jnp.sum(own_weights, axis=-1)
    tail_num = jnp.einsum(
        "ctghs,csgd->ctghd",
        cached_weights.astype(jnp.bfloat16),
        tail_values,
        preferred_element_type=jnp.float32,
    )
    tail_num = tail_num + jnp.einsum(
        "ctghu,cugd->ctghd",
        own_weights.astype(jnp.bfloat16),
        own_values,
        preferred_element_type=jnp.float32,
    )
    tail_out = (tail_num / tail_total[..., None]).reshape(rows_dev, heads_dev, HD)
    tail_lse = (tail_max + jnp.log(tail_total)).reshape(rows_dev, heads_dev)
    attention, scores = combine_parts(
        mine_out.reshape(rows_dev, heads_dev, HD), mine_lse, tail_out, tail_lse
    )
    attention = attention.reshape(rows_dev, heads_dev * HD)
    partial_out = jnp.dot(
        attention,
        lax.all_gather(w_out, "wide", axis=1, tiled=True),
        preferred_element_type=jnp.float32,
    )
    summed = lax.psum(partial_out.astype(jnp.bfloat16), "narrow").astype(jnp.float32)
    hidden_out = (residual + summed).astype(jnp.bfloat16)
    new_cache = jnp.stack(
        [new_keys.reshape(rows_dev, groups * HD), new_values.reshape(rows_dev, groups * HD)]
    )
    return (hidden_out, scores, new_cache)


def solution(mesh):
    in_specs = (
        P("wide", None),
        P(),
        P("wide", "narrow"),
        P(),
        P(),
        P("narrow", "wide"),
        P(None, "wide", None, "narrow"),
        P(None, "wide", None, "narrow"),
        P(),
        P("wide"),
        P(),
    )
    out_specs = (P("wide", None), P("wide", "narrow"), P(None, "wide", "narrow"))
    return jax.shard_map(body, mesh=mesh, in_specs=in_specs, out_specs=out_specs, check_vma=False)
```

profile of v0, /device:TPU:1, one launch (start us, length us, event | category | flops | bytes accessed | tf_op | source)
XLA Modules:
  0.0 433.9 jit_solution(1047986188421033371)
XLA Ops:
  8.5 1.3 copy_bitcast_fusion
  9.8 18.9 %all_to_all.19 = bf16[128,16,128]{2,0,1:T(8,128)(2,1)S(1)} all-to-all(bf16[128,16,128]{2,0,1:T(8,128)(2,1)S(1)} %copy_bitcast_fusion), channel_id=1, replica_groups=mesh['wide'=16,'narrow'=8] {'wide'}, dimensions={1} | all-to-all | bytes 1048576 | tf_op jit(solution)/shard_map/all_to_all | solution.py:82
  28.7 2.6 fusion.99
  32.0 74.5 %reduce-scatter.6.cloned.1.call-done = f32[128,512]{1,0:T(8,128)} async-done(((f32[2048,512]{1,0:T(8,128)}), f32[128,512]{1,0:T(8,128)}) %reduce-scatter.6.cloned.1.call-update) | async-done | bytes 262160 | tf_op jit(solution)/shard_map/reduce_scatter | solution.py:83
  118.0 33.7 %all-gather.3.cloned.1.call-done = bf16[2048,256]{1,0:T(8,128)(2,1)} async-done(((bf16[128,256]{1,0:T(8,128)(2,1)}), bf16[2048,256]{1,0:T(8,128)(2,1)}) %all-gather.3.cloned.1.call-update) | async-done | bytes 1048592 | tf_op jit(solution)/shard_map/all_gather | solution.py:105
  151.7 7.9 %while.1 = (s32[]{:T(128)}, bf16[2048,256]{1,0:T(8,128)(2,1)}, s32[4,2]{0,1:T(2,128)S(1)}, bf16[4,32,256]{2,1,0:T(8,128)(2,1)S(1)}, s32[]{:T(128)}) while((s32[]{:T(128)}, bf16[2048,256]{1,0:T(8,128)(2,1)}, s32[4,2]{0,1:T(2,128)S(1)}, bf16[4,32,256]{2,1,0:T(8,128)(2,1)S(1)}, s32[]{:T(128)}) %tuple.42), condition=%wide.while_cond, body=%wide.while_body.sunk | while | flops 2 | bytes 32865 | solution.py:111
  152.3 1.4 bitcast_dynamic-update-slice_fusion.2
  154.3 1.4 bitcast_dynamic-update-slice_fusion.2
  156.3 1.4 bitcast_dynamic-update-slice_fusion.2
  158.2 1.4 bitcast_dynamic-update-slice_fusion.2
  159.6 3.9 fusion.96
  163.5 1.9 copy-done.1
  167.1 1.4 copy.100
  169.1 4.5 %fusion.45 = f32[4,32,1,2,128]{4,1,3,0,2:T(8,128)S(1)} fusion(bf16[2,4,4096,128]{3,2,1,0:T(8,128)(2,1)} %param.17, f32[4,32,1,2,4096]{4,1,3,0,2:T(8,128)} %copy-done.1, f32[4,32,2]{1,2,0:T(2,128)S(1)} %get-tuple-element.45, f32[4,32,2]{1,2,0:T(2,128)S(1)} %fusion.15), kind=kOutput, calls=%fused_computation.35 | convolution fusion | flops 270565376 | bytes 8521728 | tf_op jit(solution)/shard_map/srghk,skgd->srghd/dot_general | solution.py:125
  175.4 1.3 copy-done.2
  177.8 1.4 fusion.98
  179.1 3.6 fusion.97
  183.9 3.0 fusion.61
  186.9 54.0 %reduce-scatter.10.cloned.1.call-done = f32[128,2]{1,0:T(8,128)} async-done(((f32[2048,2]{1,0:T(8,128)}), f32[128,2]{1,0:T(8,128)}) %reduce-scatter.10.cloned.1.call-update) | async-done | bytes 1040
  242.8 43.1 %all-gather.5.cloned.1.call-done = bf16[256,2048]{1,0:T(8,128)(2,1)} async-done(((bf16[256,128]{1,0:T(8,128)(2,1)}), bf16[256,2048]{1,0:T(8,128)(2,1)}) %all-gather.5.cloned.1.call-update) | async-done | bytes 1048592 | tf_op jit(solution)/shard_map/all_gather | solution.py:193
  285.9 76.6 %reduce-scatter.8.cloned.1.call-done = f32[128,256]{1,0:T(8,128)} async-done(((f32[2048,256]{1,0:T(8,128)}), f32[128,256]{1,0:T(8,128)}) %reduce-scatter.8.cloned.1.call-update) | async-done | bytes 131088 | tf_op jit(solution)/shard_map/reduce_scatter | solution.py:149
  363.1 2.4 convolution_convert_fusion
  366.2 58.8 %all-reduce.3.cloned.1.call-done = bf16[128,2048]{1,0:T(8,128)(2,1)} async-done(((bf16[128,2048]{1,0:T(8,128)(2,1)}), bf16[128,2048]{1,0:T(8,128)(2,1)}) %all-reduce.3.cloned.1.call-update) | async-done | bytes 524304 | tf_op jit(solution)/shard_map/psum | solution.py:196
  425.1 2.0 fusion.54
  (106 shorter events, 17.3 us)
Async XLA Ops:
  7.2 21.5 %copy-start = (bf16[128,512]{1,0:T(8,128)(2,1)S(1)}, bf16[128,512]{1,0:T(8,128)(2,1)}, u32[]{:S(2)}) copy-start(bf16[128,512]{1,0:T(8,128)(2,1)} %param.13) | copy-start | bytes 393220
  7.2 99.3 %reduce-scatter.6.cloned.1.call-start = ((), (), s32[]{:S(2)}) async-start(), calls=%async_computation.4 | async-start | bytes 4456448 | tf_op jit(solution)/shard_map/reduce_scatter | solution.py:83
  28.7 2.7 copy-start.6
  28.7 2.8 copy-start.8
  28.7 79.1 %copy-start.4 = (f32[128]{0:T(128)S(1)}, f32[128]{0:T(128)}, u32[]{:S(2)}) copy-start(f32[128]{0:T(128)} %param.14) | copy-start | bytes 1540
  31.3 77.9 %copy-start.7 = (s32[64]{0:T(128)S(1)}, s32[64]{0:T(128)}, u32[]{:S(2)}) copy-start(s32[64]{0:T(128)} %param.21) | copy-start | bytes 772
  31.3 120.4 %all-gather.3.cloned.1.call-start = ((), (), s32[]{:S(2)}) async-start(), calls=%async_computation.5 | async-start | bytes 1114112 | tf_op jit(solution)/shard_map/all_gather | solution.py:105
  109.1 131.8 %reduce-scatter.10.cloned.1.call-start = ((), (), s32[]{:S(2)}) async-start(), calls=%async_computation.9 | async-start | bytes 1114112
  163.5 1.9 copy-start.1
  168.5 117.4 %all-gather.5.cloned.1.call-start = ((), (), s32[]{:S(2)}) async-start(), calls=%async_computation.7 | async-start | bytes 1114112 | tf_op jit(solution)/shard_map/all_gather | solution.py:193
  169.1 193.4 %reduce-scatter.8.cloned.1.call-start = ((), (), s32[]{:S(2)}) async-start(), calls=%async_computation.6 | async-start | bytes 2228224 | tf_op jit(solution)/shard_map/reduce_scatter | solution.py:149
  173.6 3.7 copy-start.5
  175.4 1.4 copy-start.2
  176.7 248.3 %all-reduce.3.cloned.1.call-start = ((), (), s32[]{:S(2)}) async-start(), calls=%async_computation.8 | async-start | bytes 1048576 | tf_op jit(solution)/shard_map/psum | solution.py:196
  183.9 241.2 %copy-start.3 = (bf16[128,2048]{1,0:T(8,128)(2,1)S(1)}, bf16[128,2048]{1,0:T(8,128)(2,1)}, u32[]{:S(2)}) copy-start(bf16[128,2048]{1,0:T(8,128)(2,1)} %param.11) | copy-start | bytes 1572868
Sparse Core Ops, SparseCore 0:
  31.5 74.9 reduce-scatter.5
  109.4 42.2 all-gather.2
  168.6 72.2 reduce-scatter.9
  242.9 42.8 all-gather.4
  289.0 73.4 reduce-scatter.7
  365.6 59.3 all-reduce.2
where the time goes:
time: 436 us; the launch traced here: 434 us
  waiting for transfers between devices  341 us (78%)
  between operations  22.1 us (5%)
  matrix products  21.7 us (5%)
  local copies, waits for them, and re-layouts  19.5 us (4%)
  blocking collectives  18.9 us (4%)
  other arithmetic  9.84 us (2%)
    reduce_scatter x1, waiting for transfers between devices, body(): lax.psum_scatter(spread_out, 'wide', scatter_dimension=0, tiled=True)  76.6 us
    reduce_scatter x1, waiting for transfers between devices, body(): lax.psum_scatter(jnp.dot(regrouped, w_qkv, preferred_element_type=jnp.flo...  74.5 us
    psum x1, waiting for transfers between devices, body(): lax.psum(partial_out.astype(jnp.bfloat16), 'narrow').astype(jnp.float32)  58.8 us
    unnamed x7, waiting for transfers between devices  54.6 us
    all_gather x1, waiting for transfers between devices, body(): lax.all_gather(w_out, 'wide', axis=1, tiled=True)  43.1 us
    all_gather x1, waiting for transfers between devices, body(): lax.all_gather(queries.reshape(rows_dev, heads_dev * HD), 'wide', axis=0,...  33.7 us
    all_to_all x1, blocking collectives, body(): lax.all_to_all(normed, 'wide', split_axis=1, concat_axis=0, tiled=True)  18.9 us
  transfers between devices with their start and end apart: 6, of which 6 were waited for; matrix products, arithmetic and copies ran while one was open for 5% of the time, Pallas kernels for 0%

commit v1 on v0

v1 whole, which is shorter than its diff:
```python
import math

import jax
import jax.numpy as jnp
from jax import lax
from jax.experimental import pallas as pl
from jax.experimental.pallas import tpu as pltpu
from jax.sharding import PartitionSpec as P

HD = 128
ROWS = 128
PER = 32
PLEN = 4096
TLEN = 256
KB = 1024
MSG = 80
EPS = 1e-06
NEG = -1e30
SCALE = HD ** (-0.5)
LOG2E = 1.4426950408889634
F32 = jnp.float32
BF16 = jnp.bfloat16
AXES = ("wide", "narrow")
SMEM = pltpu.SMEM


def device(z, y, x, core):
    return ((z % 4) * 4 + y % 4) * 8 + (x % 4) * 2 + core


def ring(first, step):
    pairs = []
    for z in range(4):
        for y in range(4):
            for x in range(4):
                for core in range(2):
                    along_y = (core == 0) == first
                    target = device(z, y + step, x, core) if along_y else device(z + step, y, x, core)
                    pairs.append((device(z, y, x, core), target))
    return pairs


def shift(value, first, step):
    return lax.ppermute(value, AXES, ring(first, step))


def shift_x(value, step):
    return lax.ppermute(value, "narrow", [(n, (n + 2 * step) % 8) for n in range(8)])


def swap_core(value):
    return lax.ppermute(value, "narrow", [(n, n ^ 1) for n in range(8)])


def call(kernel, out_shape, args, smem=(), anys=(), scratch=(), cost=None):
    specs = []
    for i in range(len(args)):
        if i in smem:
            specs.append(pl.BlockSpec(memory_space=SMEM))
        elif i in anys:
            specs.append(pl.BlockSpec(memory_space=pl.ANY))
        else:
            specs.append(pl.BlockSpec(memory_space=pltpu.VMEM))
    single = not isinstance(out_shape, (tuple, list))
    outs = pl.BlockSpec(memory_space=pltpu.VMEM)
    if not single:
        outs = [pl.BlockSpec(memory_space=pltpu.VMEM)] * len(out_shape)
    flops, nbytes = cost or (1 << 20, 1 << 20)
    return pl.pallas_call(
        kernel,
        out_shape=out_shape,
        in_specs=specs,
        out_specs=outs,
        scratch_shapes=list(scratch),
        compiler_params=pltpu.CompilerParams(vmem_limit_bytes=40 << 20),
        cost_estimate=pl.CostEstimate(flops=flops, bytes_accessed=nbytes, transcendentals=0),
    )(*args)


def struct(shape, dtype):
    return jax.ShapeDtypeStruct(shape, dtype)


def norm_kernel(ids, hidden, gain, *outs):
    values = hidden[...].astype(F32)
    mean_square = jnp.mean(values * values, axis=-1, keepdims=True)
    factor = lax.rsqrt(mean_square + EPS)
    b, core = ids[1], ids[2]
    for block in range(16):
        fz, fy = block // 4, block % 4
        part = hidden[:, block * HD : (block + 1) * HD].astype(F32) * factor
        part = (part * gain[:, block * HD : (block + 1) * HD]).astype(BF16)
        fa = jnp.where(core == 0, fy, fz)
        fb = jnp.where(core == 0, fz, fy)
        target = lax.rem(fb - b + 4, 4)
        for d in range(4):

            @pl.when(target == d)
            def _():
                outs[d][fa] = part


def project_kernel(ids, *refs):
    acts, weights, outs = refs[:4], refs[4:8], refs[8:]
    a = ids[0]
    weight = jnp.concatenate([weights[e][...] for e in range(4)], axis=0)
    order = [lax.rem(a - e + 4, 4) for e in range(4)]
    for d in range(4):
        act = jnp.concatenate([acts[d][order[e]] for e in range(4)], axis=1)
        product = jnp.dot(act, weight, preferred_element_type=F32)
        outs[d][...] = product[:, : 2 * HD]
        outs[4 + d][...] = product[:, 2 * HD :]


def head_norm(values, gain, cosine, sine):
    mean_square = jnp.mean(values * values, axis=-1, keepdims=True)
    values = values * lax.rsqrt(mean_square + EPS) * gain
    return values * cosine + pltpu.roll(values, HD // 2, 1) * sine


def query_kernel(p0, p1, p2, p3, gain, cosine, sine, out):
    total = (p0[...] + p1[...]) + (p2[...] + p3[...])
    for h in range(2):
        head = head_norm(total[:, h * HD : (h + 1) * HD], gain[...], cosine[...], sine[...])
        head = head.astype(BF16)
        for j in range(4):
            out[j, h * PER : (h + 1) * PER] = head[j * PER : (j + 1) * PER]


def route_kernel(index, x0, x1, x2, x3, o0, o1, o2, o3, held):
    for d, ref in enumerate((x0, x1, x2, x3)):
        held[4 * d : 4 * d + 4] = ref[...]
    for e, ref in enumerate((o0, o1, o2, o3)):
        for k in range(4):
            ref[k] = held[index[4 * e + k]]


def column(rows, count):
    lane = lax.broadcasted_iota(jnp.int32, (count, HD), 1)
    row = lax.broadcasted_iota(jnp.int32, (count, HD), 0)
    spread = jnp.broadcast_to(rows, (count, HD))
    return jnp.sum(jnp.where(lane == row, spread, 0.0), axis=1, keepdims=True)


def tail_kernel(
    lens, p0, p1, p2, p3, queries, gain, cosine, sine, cache,
    new_cache, out, lse, keys, values, sems,
):
    groups = 8
    conts = 8

    def fetch(which, g, target):
        return pltpu.make_async_copy(
            cache.at[which, pl.ds(g * conts, conts)], target.at[g], sems.at[which, g]
        )

    for g in range(groups):
        fetch(0, g, keys).start()
        fetch(1, g, values).start()
    total = (p0[...] + p1[...]) + (p2[...] + p3[...])
    new_cache[0] = head_norm(total[:, :HD], gain[...], cosine[...], sine[...]).astype(BF16)
    new_cache[1] = total[:, HD:].astype(BF16)
    row = lax.broadcasted_iota(jnp.int32, (32, TLEN), 0)
    lane = lax.broadcasted_iota(jnp.int32, (32, TLEN), 1)
    owner = lax.rem(row, 16) // 2
    small_row = lax.broadcasted_iota(jnp.int32, (32, 16), 0)
    small_col = lax.broadcasted_iota(jnp.int32, (32, 16), 1)
    visible = (lax.rem(small_row, 16) // 2 == small_col // 2) & (
        lax.rem(small_col, 2) <= lax.rem(small_row, 2)
    )
    owner_out = lax.rem(lax.broadcasted_iota(jnp.int32, (32, HD), 0), 16) // 2
    contract = (((1,), (1,)), ((), ()))
    for g in range(groups):
        j, half = g // 2, (g % 2) * 16
        q = jnp.concatenate(
            [queries[j, half : half + 16], queries[j, PER + half : PER + half + 16]], axis=0
        )
        fetch(0, g, keys).wait()
        score = jnp.zeros((32, TLEN), F32)
        length = jnp.zeros((32, TLEN), jnp.int32)
        for i in range(conts):
            part = lax.dot_general(q, keys[g, i], contract, preferred_element_type=F32)
            score = jnp.where(owner == i, part, score)
            length = jnp.where(owner == i, lens[g * conts + i], length)
        score = jnp.where(lane < length, score, NEG)
        fresh = lax.dot_general(
            q, new_cache[0, g * 16 : g * 16 + 16], contract, preferred_element_type=F32
        )
        fresh = jnp.where(visible, fresh, NEG)
        high = jnp.maximum(
            jnp.max(score, axis=1, keepdims=True), jnp.max(fresh, axis=1, keepdims=True)
        )
        weight = jnp.exp2((score - high) * (SCALE * LOG2E))
        fresh_weight = jnp.exp2((fresh - high) * (SCALE * LOG2E))
        sums = jnp.sum(weight, axis=1, keepdims=True) + jnp.sum(
            fresh_weight, axis=1, keepdims=True
        )
        weight = weight.astype(BF16)
        fetch(1, g, values).wait()
        acc = jnp.zeros((32, HD), F32)
        for i in range(conts):
            part = jnp.dot(weight, values[g, i], preferred_element_type=F32)
            acc = jnp.where(owner_out == i, part, acc)
        acc = acc + jnp.dot(
            fresh_weight.astype(BF16),
            new_cache[1, g * 16 : g * 16 + 16],
            preferred_element_type=F32,
        )
        acc = acc / sums
        logs = jnp.broadcast_to(high * SCALE + jnp.log(sums), (32, HD))
        for h in range(2):
            out[h, g * 16 : g * 16 + 16] = acc[h * 16 : h * 16 + 16]
            lse[h, g * 16 : g * 16 + 16] = logs[h * 16 : h * 16 + 16]


def prefix_kernel(select, lens, r0, r1, r2, r3, cache, out, held, keys, values, scores, sems):
    blocks = PLEN // KB

    def fetch(which, s, i, target):
        return pltpu.make_async_copy(
            cache.at[which, s, pl.ds(i * KB, KB)], target.at[s, i], sems.at[which, s, i]
        )

    counts = [(lens[s] + (KB - 1)) // KB for s in range(4)]
    for s in range(4):
        for i in range(blocks):

            @pl.when(i < counts[s])
            def _():
                fetch(0, s, i, keys).start()
                fetch(1, s, i, values).start()

    for e, ref in enumerate((r0, r1, r2, r3)):
        held[e] = ref[...]
    lane = lax.broadcasted_iota(jnp.int32, (64, KB), 1)
    contract = (((1,), (1,)), ((), ()))
    for s in range(4):
        q = held[select[s], s]

        def first(i, high):
            fetch(0, s, i, keys).wait()
            part = lax.dot_general(q, keys[s, i], contract, preferred_element_type=F32)
            part = jnp.where(lane < lens[s] - i * KB, part, NEG)
            scores[i] = part
            for c in range(KB // HD):
                high = jnp.maximum(high, part[:, c * HD : (c + 1) * HD])
            return high

        high = lax.fori_loop(0, counts[s], first, jnp.full((64, HD), NEG, F32))
        high = jnp.max(high, axis=1, keepdims=True)

        def second(i, carry):
            sums, acc = carry
            weight = jnp.exp2((scores[i] - high) * (SCALE * LOG2E))
            for c in range(KB // HD):
                sums = sums + weight[:, c * HD : (c + 1) * HD]
            fetch(1, s, i, values).wait()
            acc = acc + jnp.dot(weight.astype(BF16), values[s, i], preferred_element_type=F32)
            return sums, acc

        zero = jnp.zeros((64, HD), F32)
        sums, acc = lax.fori_loop(0, counts[s], second, (zero, zero))
        sums = jnp.sum(sums, axis=1, keepdims=True)
        out[s, :64] = (acc / sums).astype(BF16)
        logs = jnp.broadcast_to(high * SCALE + jnp.log(sums), (64, HD))
        row = lax.broadcasted_iota(jnp.int32, (64, HD), 0)
        column_of = lax.broadcasted_iota(jnp.int32, (64, HD), 1)
        line = jnp.sum(jnp.where(row == column_of, logs, 0.0), axis=0, keepdims=True)
        top = line.astype(BF16).astype(F32)
        middle = (line - top).astype(BF16).astype(F32)
        low = line - top - middle
        which = lax.broadcasted_iota(jnp.int32, (16, HD), 0)
        lines = jnp.where(
            which == 0, top, jnp.where(which == 1, middle, jnp.where(which == 2, low, 0.0))
        )
        out[s, 64:MSG] = lines.astype(BF16)


def finish_kernel(
    ids, select, c0, c1, c2, c3, tail_out, tail_lse, w0, w1, w2, w3,
    scores, keep, send, held, attention,
):
    for e, ref in enumerate((c0, c1, c2, c3)):
        held[e] = ref[...]
    for j in range(4):
        message = held[select[j], j]
        lines = message[64:MSG].astype(F32)
        line = (lines[0:1] + lines[1:2]) + lines[2:3]
        logs = column(line, 64)
        for h in range(2):
            rows = slice(j * PER, (j + 1) * PER)
            prefix_out = message[h * PER : (h + 1) * PER].astype(F32)
            prefix_lse = logs[h * PER : (h + 1) * PER]
            own_lse = tail_lse[h, rows][:, 0:1]
            high = jnp.maximum(prefix_lse, own_lse)
            share_a = jnp.exp(prefix_lse - high)
            share_b = jnp.exp(own_lse - high)
            both = share_a + share_b
            merged = (share_a * prefix_out + share_b * tail_out[h, rows]) / both
            attention[rows, h * HD : (h + 1) * HD] = merged.astype(BF16)
            scores[rows, h : h + 1] = high + jnp.log(both)
    a, b, core, x = ids[0], ids[1], ids[2], ids[3]
    left = attention[...]
    for e, ref in enumerate((w0, w1, w2, w3)):
        for d in range(4):
            product = jnp.dot(left, ref[d], preferred_element_type=F32)
            at_a, at_b = lax.rem(a - d + 4, 4), lax.rem(b - e + 4, 4)
            block = jnp.where(core == 0, 4 * at_b + at_a, 4 * at_a + at_b)
            mine = (block // 8) == core
            pair = lax.rem(block, 8) // 2
            side = lax.rem(block, 2)

            @pl.when(mine)
            def _():
                keep[lax.rem(pair - x + 4, 4), side] = product

            @pl.when(jnp.logical_not(mine))
            def _():
                send[pair, side] = product.astype(BF16)


def first_sum_kernel(ids, keep, got, o0, o1, o2, o3):
    x = ids[3]
    for d in range(4):
        total = keep[d] + got[lax.rem(x + d, 4)].astype(F32)
        if d == 0:
            o0[...] = total
        else:
            (o1, o2, o3)[d - 1][...] = total.astype(BF16)


def second_sum_kernel(ids, o0, g1, g2, g3, hidden, out):
    core, x = ids[2], ids[3]
    for side in range(2):
        total = o0[side] + (
            g1[side].astype(F32) + g2[side].astype(F32) + g3[side].astype(F32)
        )
        at = pl.multiple_of((core * 8 + x * 2 + side) * HD, HD)
        out[side] = (hidden[:, pl.ds(at, HD)].astype(F32) + total).astype(BF16)


def gather_kernel(ids, mine, other, out):
    core, x = ids[2], ids[3]
    for d in range(4):
        for side in range(2):
            at = lax.rem(x - d + 4, 4) * 2 + side
            out[:, pl.ds(pl.multiple_of((core * 8 + at) * HD, HD), HD)] = mine[d, side]
            out[:, pl.ds(pl.multiple_of(((1 - core) * 8 + at) * HD, HD), HD)] = other[d, side]


def lookup(indices, table):
    entries = jnp.arange(table.shape[0], dtype=jnp.int32)
    return jnp.sum(jnp.where(indices[:, None] == entries[None, :], table[None, :], 0), axis=1)


def split(wide, core):
    z, y = wide // 4, wide % 4
    return jnp.where(core == 0, y, z), jnp.where(core == 0, z, y)


def routing(source, a, b, core):
    step = jnp.arange(16, dtype=jnp.int32) // 4
    at_b = (b + step) % 4
    wide = jnp.where(core == 0, 4 * at_b + a, 4 * a + at_b)
    wanted = lookup(wide * 4 + jnp.arange(16, dtype=jnp.int32) % 4, source)
    from_a, from_b = split(wanted // 4, core)
    index = ((a - from_a) % 4) * 4 + wanted % 4
    sender = (b - from_b[:4]) % 4
    return index, sender, wanted[:4]


def gather_ring(value, first):
    return [value] + [shift(value, first, step) for step in (1, 2, 3)]


def route(values, index, rows):
    held = gather_ring(values, True)
    shape = struct((4, rows, HD), BF16)
    sends = call(
        route_kernel,
        [shape] * 4,
        [index] + held,
        smem=(0,),
        scratch=[pltpu.VMEM((16, rows, HD), BF16)],
    )
    return [sends[0]] + [shift(sends[step], False, step) for step in (1, 2, 3)]


def body(
    hidden_in, attn_gain, w_qkv, q_gain, k_gain, w_out,
    prefix_cache, tail_cache, prompt_lens, tail_lens, slot_prompt,
):
    wide = lax.axis_index("wide").astype(jnp.int32)
    narrow = lax.axis_index("narrow").astype(jnp.int32)
    core, x = narrow % 2, narrow // 2
    a, b = split(wide, core)
    ids = jnp.stack([a, b, core, x]).astype(jnp.int32)

    everyone = jnp.arange(64, dtype=jnp.int32)
    inverse = jnp.sum(
        jnp.where(slot_prompt[:, None] == everyone[None, :], everyone[:, None], 0), axis=0
    )
    ask_index, ask_sender, owners = routing(slot_prompt, a, b, core)
    home_index, home_sender, _ = routing(inverse, a, b, core)
    slot_lens = lookup(owners, prompt_lens)
    row = jnp.arange(ROWS, dtype=jnp.int32)
    position = (
        lookup(wide * 4 + row // PER, prompt_lens) + lookup(row // 2, tail_lens) + row % 2
    ).astype(F32)
    channel = jnp.arange(HD // 2, dtype=F32)
    inverse_freq = jnp.exp(channel * (-2.0 / HD) * math.log(1000000.0))
    angles = position[:, None] * inverse_freq
    cosine, sine = jnp.cos(angles), jnp.sin(angles)
    cosine = jnp.concatenate([cosine, cosine], axis=1)
    sine = jnp.concatenate([-sine, sine], axis=1)
    q_gain, k_gain = q_gain.reshape(1, HD), k_gain.reshape(1, HD)

    weights = gather_ring(w_qkv, True)
    shape = struct((4, ROWS, HD), BF16)
    acts = call(norm_kernel, [shape] * 4, [ids, hidden_in, attn_gain.reshape(1, -1)], smem=(0,))
    acts = [acts[0]] + [shift(acts[step], False, step) for step in (1, 2, 3)]
    partial = struct((ROWS, 2 * HD), F32)
    parts = call(
        project_kernel,
        [partial] * 8,
        [ids] + acts + weights,
        smem=(0,),
        cost=(2 * 512 * 512 * 512, 3 << 20),
    )
    query_parts = [parts[0]] + [shift(parts[step], False, 4 - step) for step in (1, 2, 3)]
    pair_parts = [parts[4]] + [shift(parts[4 + step], False, 4 - step) for step in (1, 2, 3)]
    queries = call(
        query_kernel, struct((4, 64, HD), BF16), query_parts + [q_gain, cosine, sine]
    )

    asked = route(queries, ask_index, 64)

    new_cache, tail_out, tail_lse = call(
        tail_kernel,
        [
            struct((2, ROWS, HD), BF16),
            struct((2, ROWS, HD), F32),
            struct((2, ROWS, HD), F32),
        ],
        [tail_lens] + pair_parts + [queries, k_gain, cosine, sine, tail_cache],
        smem=(0,),
        anys=(9,),
        scratch=[
            pltpu.VMEM((8, 8, TLEN, HD), BF16),
            pltpu.VMEM((8, 8, TLEN, HD), BF16),
            pltpu.SemaphoreType.DMA((2, 8)),
        ],
        cost=(2 * 2 * 64 * 32 * TLEN * HD, 8 << 20),
    )

    results = call(
        prefix_kernel,
        struct((4, MSG, HD), BF16),
        [ask_sender, slot_lens] + asked + [prefix_cache],
        smem=(0, 1),
        anys=(6,),
        scratch=[
            pltpu.VMEM((4, 4, 64, HD), BF16),
            pltpu.VMEM((4, PLEN // KB, KB, HD), BF16),
            pltpu.VMEM((4, PLEN // KB, KB, HD), BF16),
            pltpu.VMEM((PLEN // KB, 64, KB), F32),
            pltpu.SemaphoreType.DMA((2, 4, PLEN // KB)),
        ],
        cost=(2 * 2 * 4 * 64 * PLEN * HD, 8 << 20),
    )
    homes = route(results, home_index, MSG)

    near = jnp.stack(gather_ring(w_out, True))
    far = gather_ring(near, False)

    scores, keep, send = call(
        finish_kernel,
        [
            struct((ROWS, 2), F32),
            struct((4, 2, ROWS, HD), F32),
            struct((4, 2, ROWS, HD), BF16),
        ],
        [ids, home_sender] + homes + [tail_out, tail_lse] + far,
        smem=(0, 1),
        scratch=[pltpu.VMEM((4, 4, MSG, HD), BF16), pltpu.VMEM((ROWS, 2 * HD), BF16)],
        cost=(2 * ROWS * 256 * 2048, 3 << 20),
    )
    got = swap_core(send)
    block = struct((2, ROWS, HD), BF16)
    sums = call(
        first_sum_kernel,
        [struct((2, ROWS, HD), F32), block, block, block],
        [ids, keep, got],
        smem=(0,),
    )
    moved = [shift_x(sums[step], step) for step in (1, 2, 3)]
    mine = call(second_sum_kernel, block, [ids, sums[0]] + moved + [hidden_in], smem=(0,))
    ours = jnp.stack([mine] + [shift_x(mine, step) for step in (1, 2, 3)])
    theirs = swap_core(ours)
    hidden_out = call(
        gather_kernel, struct((ROWS, 2048), BF16), [ids, ours, theirs], smem=(0,)
    )
    return (hidden_out, scores, new_cache)


def solution(mesh):
    in_specs = (
        P("wide", None),
        P(),
        P("wide", "narrow"),
        P(),
        P(),
        P("narrow", "wide"),
        P(None, "wide", None, "narrow"),
        P(None, "wide", None, "narrow"),
        P(),
        P("wide"),
        P(),
    )
    out_specs = (P("wide", None), P("wide", "narrow"), P(None, "wide", "narrow"))
    return jax.shard_map(body, mesh=mesh, in_specs=in_specs, out_specs=out_specs, check_vma=False)
```

time: 436 us -> 123 us (0.28)
  waiting for transfers between devices: 341 us -> 23.8 us
  starting transfers between devices: 0.42 us -> 62.5 us
  Pallas kernels: 0 us -> 22 us
  matrix products: 21.7 us -> 0 us
  between operations: 22.1 us -> 0.94 us
  blocking collectives: 18.9 us -> 0 us
  local copies, waits for them, and re-layouts: 19.5 us -> 7.32 us
  other arithmetic: 9.84 us -> 5.34 us
    reduce_scatter x2 -> x0, waiting for transfers between devices: 151 us -> none  [the longest x1 76.6 us: body(): lax.psum_scatter(spread_out, 'wide', scatter_dimension=0, tiled=True)]
    all_gather x2 -> x0, waiting for transfers between devices: 76.8 us -> none  [the longest x1 43.1 us: body(): lax.all_gather(w_out, 'wide', axis=1, tiled=True)]
    ppermute x0 -> x38, starting transfers between devices: none -> 62.5 us  [the longest x30 39.4 us: shift(): return lax.ppermute(value, AXES, ring(first, step))]
    psum x1 -> x0, waiting for transfers between devices: 58.8 us -> none  [body(): lax.psum(partial_out.astype(jnp.bfloat16), 'narrow').astype(jnp.float32)]
    unnamed x7 -> x0, waiting for transfers between devices: 54.6 us -> none
    ppermute x0 -> x38, waiting for transfers between devices: none -> 23.8 us  [the longest x30 16.8 us: shift(): return lax.ppermute(value, AXES, ring(first, step))]
    pallas_call x0 -> x11, Pallas kernels: none -> 22 us  [call(): pl.pallas_call(kernel, out_shape=out_shape, in_specs=specs, out_specs=out...]
    dot_general x8 -> x0, matrix products: 21.7 us -> none  [the longest x1 4.48 us: body(): jnp.einsum('srghk,skgd->srghd', prefix_weights.astype(jnp.bfloat16), held...]
  transfers between devices with their start and end apart: 6 -> 38, of which waited for: 6 -> 15; matrix products, arithmetic and copies ran while one was open for 5% -> 5% of each run, Pallas kernels for 0% -> 13%
where the time goes in v1:
time: 123 us; the launch traced here: 122 us
  starting transfers between devices  62.5 us (51%)
  waiting for transfers between devices  23.8 us (19%)
  Pallas kernels  22 us (18%)
  local copies, waits for them, and re-layouts  7.32 us (6%)
  other arithmetic  5.34 us (4%)
    ppermute x30, starting transfers between devices, shift(): return lax.ppermute(value, AXES, ring(first, step))  39.4 us
    pallas_call x11, Pallas kernels, call(): pl.pallas_call(kernel, out_shape=out_shape, in_specs=specs, out_specs=out...  22 us
    ppermute x30, waiting for transfers between devices, shift(): return lax.ppermute(value, AXES, ring(first, step))  16.8 us
    ppermute x2, starting transfers between devices, swap_core(): return lax.ppermute(value, 'narrow', [(n, n ^ 1) for n in range(8)])  14.5 us
    ppermute x6, starting transfers between devices, shift_x(): lax.ppermute(value, 'narrow', [(n, (n + 2 * step) % 8) for n in range(8)])  8.58 us
    unnamed x19, local copies, waits for them, and re-layouts  7.32 us
    ppermute x6, waiting for transfers between devices, shift_x(): lax.ppermute(value, 'narrow', [(n, (n + 2 * step) % 8) for n in range(8)])  5.29 us
    reduce_sum x3, other arithmetic, lookup(): jnp.sum(jnp.where(indices[:, None] == entries[None, :], table[None, :], 0...  2.83 us
  transfers between devices with their start and end apart: 38, of which 15 were waited for; matrix products, arithmetic and copies ran while one was open for 5% of the time, Pallas kernels for 13%

profile of v1, /device:TPU:1, one launch (start us, length us, event | category | flops | bytes accessed | tf_op | source)
XLA Modules:
  0.0 121.8 jit_solution(5830138973431341779)
XLA Ops:
  0.7 2.5 %collective-permute-start.3 = (bf16[128,512]{1,0:T(8,128)(2,1)}, bf16[128,512]{1,0:T(8,128)(2,1)S(1)}, u32[]{:S(2)}, u32[]{:S(2)}) collective-permute-start(bf16[128,512]{1,0:T(8,128)(2,1)} %refs_4_.1), channel_id=1, source_target_pairs={{0,8},{1,33},{2,10},{3,35},{4,12},{5,37},{6,14},{7,39},{8,16},{9,4... | collective-permute-start | bytes 393224 | tf_op jit(solution)/shard_map/ppermute | solution.py:44
  3.2 3.3 %collective-permute-start.4 = (bf16[128,512]{1,0:T(8,128)(2,1)}, bf16[128,512]{1,0:T(8,128)(2,1)S(1)}, u32[]{:S(2)}, u32[]{:S(2)}) collective-permute-start(bf16[128,512]{1,0:T(8,128)(2,1)} %refs_4_.1), channel_id=1, source_target_pairs={{0,16},{1,65},{2,18},{3,67},{4,20},{5,69},{6,22},{7,71},{8,24},{9,... | collective-permute-start | bytes 393224 | tf_op jit(solution)/shard_map/ppermute | solution.py:44
  11.6 2.6 %collective-permute-start.1 = (bf16[4,128,128]{2,1,0:T(8,128)(2,1)S(1)}, bf16[4,128,128]{2,1,0:T(8,128)(2,1)S(1)}, u32[]{:S(2)}, u32[]{:S(2)}) collective-permute-start(bf16[4,128,128]{2,1,0:T(8,128)(2,1)S(1)} %get-tuple-element.35), channel_id=1, source_target_pairs={{0,64},{1,17},{2,66},{3,19},{4,68},{5,21},{6,70},{7,23},{8,72},{9,... | collective-permute-start | bytes 393224 | tf_op jit(solution)/shard_map/ppermute | solution.py:44
  18.7 2.7 %collective-permute-done.2.refs_3_ = bf16[4,128,128]{2,1,0:T(8,128)(2,1)S(1)} collective-permute-done((bf16[4,128,128]{2,1,0:T(8,128)(2,1)S(1)}, bf16[4,128,128]{2,1,0:T(8,128)(2,1)S(1)}, u32[]{:S(2)}, u32[]{:S(2)}) %collective-permute-start.2) | collective-permute-done | bytes 131104 | tf_op jit(solution)/shard_map/ppermute | solution.py:44
  24.3 2.1 %collective-permute-start.6 = (f32[128,256]{1,0:T(8,128)S(1)}, f32[128,256]{1,0:T(8,128)S(1)}, u32[]{:S(2)}, u32[]{:S(2)}) collective-permute-start(f32[128,256]{1,0:T(8,128)S(1)} %get-tuple-element.38), channel_id=1, source_target_pairs={{0,96},{1,25},{2,98},{3,27},{4,100},{5,29},{6,102},{7,31},{8,104},... | collective-permute-start | bytes 393224 | tf_op jit(solution)/shard_map/ppermute | solution.py:44
  27.2 2.5 %collective-permute-done.6.p1 = f32[128,256]{1,0:T(8,128)S(1)} collective-permute-done((f32[128,256]{1,0:T(8,128)S(1)}, f32[128,256]{1,0:T(8,128)S(1)}, u32[]{:S(2)}, u32[]{:S(2)}) %collective-permute-start.6) | collective-permute-done | bytes 131104 | tf_op jit(solution)/shard_map/ppermute | solution.py:44
  34.2 2.0 %collective-permute-start.11 = (bf16[4,64,128]{2,1,0:T(8,128)(2,1)S(1)}, bf16[4,64,128]{2,1,0:T(8,128)(2,1)S(1)}, u32[]{:S(2)}, u32[]{:S(2)}) collective-permute-start(bf16[4,64,128]{2,1,0:T(8,128)(2,1)S(1)} %shard_map.132.x0.queries), channel_id=1, source_target_pairs={{0,24},{1,97},{2,26},{3,99},{4,28},{5,101},{6,30},{7,103},{8,0},{9... | collective-permute-start | bytes 196616 | tf_op jit(solution)/shard_map/ppermute | solution.py:44
  36.2 2.2 %collective-permute-done.10.x2 = bf16[4,64,128]{2,1,0:T(8,128)(2,1)S(1)} collective-permute-done((bf16[4,64,128]{2,1,0:T(8,128)(2,1)S(1)}, bf16[4,64,128]{2,1,0:T(8,128)(2,1)S(1)}, u32[]{:S(2)}, u32[]{:S(2)}) %collective-permute-start.10) | collective-permute-done | bytes 65568 | tf_op jit(solution)/shard_map/ppermute | solution.py:44
  39.5 3.2 %collective-permute-done.9.x1 = bf16[4,64,128]{2,1,0:T(8,128)(2,1)S(1)} collective-permute-done((bf16[4,64,128]{2,1,0:T(8,128)(2,1)S(1)}, bf16[4,64,128]{2,1,0:T(8,128)(2,1)S(1)}, u32[]{:S(2)}, u32[]{:S(2)}) %collective-permute-start.9) | collective-permute-done | bytes 65568 | tf_op jit(solution)/shard_map/ppermute | solution.py:44
  43.4 2.8 %collective-permute-start.13 = (bf16[4,64,128]{2,1,0:T(8,128)(2,1)S(1)}, bf16[4,64,128]{2,1,0:T(8,128)(2,1)S(1)}, u32[]{:S(2)}, u32[]{:S(2)}) collective-permute-start(bf16[4,64,128]{2,1,0:T(8,128)(2,1)S(1)} %get-tuple-element.43), channel_id=1, source_target_pairs={{0,64},{1,17},{2,66},{3,19},{4,68},{5,21},{6,70},{7,23},{8,72},{9,... | collective-permute-start | bytes 196616 | tf_op jit(solution)/shard_map/ppermute | solution.py:44
  49.9 3.4 %copy-done.1 = bf16[2,4,4096,128]{3,2,1,0:T(8,128)(2,1)S(1)} copy-done((bf16[2,4,4096,128]{3,2,1,0:T(8,128)(2,1)S(1)}, bf16[2,4,4096,128]{3,2,1,0:T(8,128)(2,1)}, u32[]{:S(2)}) %copy-start.1) | copy-done | bytes 8388632
  53.3 5.1 %shard_map.134.x0 = bf16[4,80,128]{2,1,0:T(8,128)(2,1)S(1)} custom-call(s32[4]{0:T(128)S(1)} %and_select_fusion.5.select, s32[4]{0:T(128)S(1)} %select_reduce_fusion.5.lens, bf16[4,64,128]{2,1,0:T(8,128)(2,1)S(1)} %get-tuple-element.41.r0, bf16[4,64,128]{2,1,0:T(8,128)(2,1)S(1)} %collective-permute-done.12.r1, ...), custom_call_target="tpu_custom_call" | custom-call | flops 536870912 | bytes 8388608 | tf_op jit(solution)/shard_map/pallas_call | solution.py:69
  61.1 2.2 %collective-permute-start.28 = (bf16[4,256,128]{2,1,0:T(8,128)(2,1)S(1)}, bf16[4,256,128]{2,1,0:T(8,128)(2,1)S(1)}, u32[]{:S(2)}, u32[]{:S(2)}) collective-permute-start(bf16[4,256,128]{2,1,0:T(8,128)(2,1)S(1)} %pad_maximum_fusion.w0), channel_id=1, source_target_pairs={{0,64},{1,17},{2,66},{3,19},{4,68},{5,21},{6,70},{7,23},{8,72},{9,... | collective-permute-start | bytes 786440 | tf_op jit(solution)/shard_map/ppermute | solution.py:44
  65.5 1.8 %collective-permute-start.22 = (f32[128,256]{1,0:T(8,128)S(1)}, f32[128,256]{1,0:T(8,128)S(1)}, u32[]{:S(2)}, u32[]{:S(2)}) collective-permute-start(f32[128,256]{1,0:T(8,128)S(1)} %get-tuple-element.51), channel_id=1, source_target_pairs={{0,64},{1,17},{2,66},{3,19},{4,68},{5,21},{6,70},{7,23},{8,72},{9,... | collective-permute-start | bytes 393224 | tf_op jit(solution)/shard_map/ppermute | solution.py:44
  67.9 2.9 %collective-permute-done.22.p2 = f32[128,256]{1,0:T(8,128)S(1)} collective-permute-done((f32[128,256]{1,0:T(8,128)S(1)}, f32[128,256]{1,0:T(8,128)S(1)}, u32[]{:S(2)}, u32[]{:S(2)}) %collective-permute-start.22) | collective-permute-done | bytes 131104 | tf_op jit(solution)/shard_map/ppermute | solution.py:44
  70.8 4.4 %collective-permute-start.18 = (bf16[4,80,128]{2,1,0:T(8,128)(2,1)S(1)}, bf16[4,80,128]{2,1,0:T(8,128)(2,1)S(1)}, u32[]{:S(2)}, u32[]{:S(2)}) collective-permute-start(bf16[4,80,128]{2,1,0:T(8,128)(2,1)S(1)} %get-tuple-element.46), channel_id=1, source_target_pairs={{0,32},{1,9},{2,34},{3,11},{4,36},{5,13},{6,38},{7,15},{8,40},{9,1... | collective-permute-start | bytes 245768 | tf_op jit(solution)/shard_map/ppermute | solution.py:44
  75.3 2.2 %collective-permute-start.20 = (bf16[4,80,128]{2,1,0:T(8,128)(2,1)S(1)}, bf16[4,80,128]{2,1,0:T(8,128)(2,1)S(1)}, u32[]{:S(2)}, u32[]{:S(2)}) collective-permute-start(bf16[4,80,128]{2,1,0:T(8,128)(2,1)S(1)} %get-tuple-element.48), channel_id=1, source_target_pairs={{0,96},{1,25},{2,98},{3,27},{4,100},{5,29},{6,102},{7,31},{8,104},... | collective-permute-start | bytes 245768 | tf_op jit(solution)/shard_map/ppermute | solution.py:44
  77.6 7.2 %shard_map.136 = (bf16[2,128,128]{2,1,0:T(8,128)(2,1)}, f32[2,128,128]{2,1,0:T(8,128)S(1)}, f32[2,128,128]{2,1,0:T(8,128)S(1)}) custom-call(s32[64]{0:T(128)S(1)} %copy-done.6, f32[128,256]{1,0:T(8,128)S(1)} %get-tuple-element.49.p0, f32[128,256]{1,0:T(8,128)S(1)} %collective-permute-done.21.p1, f32[128,256]{1,0:T(8,128)S(1)} %collective-permute-done.22.p2, ...), custom_call_target="tpu_custom_call" | custom-call | flops 268435456 | bytes 8388608 | tf_op jit(solution)/shard_map/pallas_call | solution.py:69
  84.9 3.5 %shard_map.137 = (f32[128,2]{1,0:T(8,128)S(1)}, f32[4,2,128,128]{3,2,1,0:T(8,128)S(1)}, bf16[4,2,128,128]{3,2,1,0:T(8,128)(2,1)S(1)}) custom-call(s32[4]{0:T(128)S(1)} %pad_add_fusion.ids, s32[4]{0:T(128)S(1)} %and_select_fusion.11.select, bf16[4,80,128]{2,1,0:T(8,128)(2,1)S(1)} %get-tuple-element.45.c0, bf16[4,80,128]{2,1,0:T(8,128)(2,1)S(1)} %collective-permute-done.18.c1, ...), custom_call_target="tpu_custom_call" | custom-call | flops 134217728 | bytes 3145728 | tf_op jit(solution)/shard_map/pallas_call | solution.py:69
  88.4 10.9 %collective-permute-start.30 = (bf16[4,2,128,128]{3,2,1,0:T(8,128)(2,1)S(1)}, bf16[4,2,128,128]{3,2,1,0:T(8,128)(2,1)S(1)}, u32[]{:S(2)}, u32[]{:S(2)}) collective-permute-start(bf16[4,2,128,128]{3,2,1,0:T(8,128)(2,1)S(1)} %get-tuple-element.56), channel_id=1, source_target_pairs={{0,1},{1,0},{2,3},{3,2},{4,5},{5,4},{6,7},{7,6},{8,9},{9,8},{10,11... | collective-permute-start | bytes 786440 | tf_op jit(solution)/shard_map/ppermute | solution.py:52
  102.4 2.4 %collective-permute-start.32 = (bf16[2,128,128]{2,1,0:T(8,128)(2,1)S(1)}, bf16[2,128,128]{2,1,0:T(8,128)(2,1)S(1)}, u32[]{:S(2)}, u32[]{:S(2)}) collective-permute-start(bf16[2,128,128]{2,1,0:T(8,128)(2,1)S(1)} %get-tuple-element.59), channel_id=1, source_target_pairs={{0,4},{1,5},{2,6},{3,7},{4,0},{5,1},{6,2},{7,3},{8,12},{9,13},{10,... | collective-permute-start | bytes 196616 | tf_op jit(solution)/shard_map/ppermute | solution.py:48
  106.0 1.8 %collective-permute-done.32.g2 = bf16[2,128,128]{2,1,0:T(8,128)(2,1)S(1)} collective-permute-done((bf16[2,128,128]{2,1,0:T(8,128)(2,1)S(1)}, bf16[2,128,128]{2,1,0:T(8,128)(2,1)S(1)}, u32[]{:S(2)}, u32[]{:S(2)}) %collective-permute-start.32) | collective-permute-done | bytes 65568 | tf_op jit(solution)/shard_map/ppermute | solution.py:48
  108.9 3.2 %collective-permute-start.35 = (bf16[2,128,128]{2,1,0:T(8,128)(2,1)S(1)}, bf16[2,128,128]{2,1,0:T(8,128)(2,1)S(1)}, u32[]{:S(2)}, u32[]{:S(2)}) collective-permute-start(bf16[2,128,128]{2,1,0:T(8,128)(2,1)S(1)} %shard_map.139), channel_id=1, source_target_pairs={{0,4},{1,5},{2,6},{3,7},{4,0},{5,1},{6,2},{7,3},{8,12},{9,13},{10,... | collective-permute-start | bytes 196616 | tf_op jit(solution)/shard_map/ppermute | solution.py:48
  115.6 3.6 %collective-permute-start.37 = (bf16[4,2,128,128]{3,2,1,0:T(8,128)(2,1)S(1)}, bf16[4,2,128,128]{3,2,1,0:T(8,128)(2,1)S(1)}, u32[]{:S(2)}, u32[]{:S(2)}) collective-permute-start(bf16[4,2,128,128]{3,2,1,0:T(8,128)(2,1)S(1)} %pad_maximum_fusion.1.mine), channel_id=1, source_target_pairs={{0,1},{1,0},{2,3},{3,2},{4,5},{5,4},{6,7},{7,6},{8,9},{9,8},{10,11... | collective-permute-start | bytes 786440 | tf_op jit(solution)/shard_map/ppermute | solution.py:52
  (103 shorter events, 40.4 us)
Async XLA Ops:
  0.7 21.8 %collective-permute-start.3 = (bf16[128,512]{1,0:T(8,128)(2,1)}, bf16[128,512]{1,0:T(8,128)(2,1)S(1)}, u32[]{:S(2)}, u32[]{:S(2)}) collective-permute-start(bf16[128,512]{1,0:T(8,128)(2,1)} %refs_4_.1), channel_id=1, source_target_pairs={{0,8},{1,33},{2,10},{3,35},{4,12},{5,37},{6,14},{7,39},{8,16},{9,4... | collective-permute-start | bytes 393224 | tf_op jit(solution)/shard_map/ppermute | solution.py:44
  3.2 19.2 %collective-permute-start.4 = (bf16[128,512]{1,0:T(8,128)(2,1)}, bf16[128,512]{1,0:T(8,128)(2,1)S(1)}, u32[]{:S(2)}, u32[]{:S(2)}) collective-permute-start(bf16[128,512]{1,0:T(8,128)(2,1)} %refs_4_.1), channel_id=1, source_target_pairs={{0,16},{1,65},{2,18},{3,67},{4,20},{5,69},{6,22},{7,71},{8,24},{9,... | collective-permute-start | bytes 393224 | tf_op jit(solution)/shard_map/ppermute | solution.py:44
  6.5 15.9 %collective-permute-start.5 = (bf16[128,512]{1,0:T(8,128)(2,1)}, bf16[128,512]{1,0:T(8,128)(2,1)S(1)}, u32[]{:S(2)}, u32[]{:S(2)}) collective-permute-start(bf16[128,512]{1,0:T(8,128)(2,1)} %refs_4_.1), channel_id=1, source_target_pairs={{0,24},{1,97},{2,26},{3,99},{4,28},{5,101},{6,30},{7,103},{8,0},{9... | collective-permute-start | bytes 393224 | tf_op jit(solution)/shard_map/ppermute | solution.py:44
  10.2 7.3 %collective-permute-start = (bf16[4,128,128]{2,1,0:T(8,128)(2,1)S(1)}, bf16[4,128,128]{2,1,0:T(8,128)(2,1)S(1)}, u32[]{:S(2)}, u32[]{:S(2)}) collective-permute-start(bf16[4,128,128]{2,1,0:T(8,128)(2,1)S(1)} %get-tuple-element.34), channel_id=1, source_target_pairs={{0,32},{1,9},{2,34},{3,11},{4,36},{5,13},{6,38},{7,15},{8,40},{9,1... | collective-permute-start | bytes 393224 | tf_op jit(solution)/shard_map/ppermute | solution.py:44
  11.6 7.1 %collective-permute-start.1 = (bf16[4,128,128]{2,1,0:T(8,128)(2,1)S(1)}, bf16[4,128,128]{2,1,0:T(8,128)(2,1)S(1)}, u32[]{:S(2)}, u32[]{:S(2)}) collective-permute-start(bf16[4,128,128]{2,1,0:T(8,128)(2,1)S(1)} %get-tuple-element.35), channel_id=1, source_target_pairs={{0,64},{1,17},{2,66},{3,19},{4,68},{5,21},{6,70},{7,23},{8,72},{9,... | collective-permute-start | bytes 393224 | tf_op jit(solution)/shard_map/ppermute | solution.py:44
  18.7 27.6 %collective-permute-start.26 = (bf16[256,128]{1,0:T(8,128)(2,1)}, bf16[256,128]{1,0:T(8,128)(2,1)S(1)}, u32[]{:S(2)}, u32[]{:S(2)}) collective-permute-start(bf16[256,128]{1,0:T(8,128)(2,1)} %param.16), channel_id=1, source_target_pairs={{0,24},{1,97},{2,26},{3,99},{4,28},{5,101},{6,30},{7,103},{8,0},{9... | collective-permute-start | bytes 196616 | tf_op jit(solution)/shard_map/ppermute | solution.py:44
  21.4 24.8 %collective-permute-start.24 = (bf16[256,128]{1,0:T(8,128)(2,1)}, bf16[256,128]{1,0:T(8,128)(2,1)S(1)}, u32[]{:S(2)}, u32[]{:S(2)}) collective-permute-start(bf16[256,128]{1,0:T(8,128)(2,1)} %param.16), channel_id=1, source_target_pairs={{0,8},{1,33},{2,10},{3,35},{4,12},{5,37},{6,14},{7,39},{8,16},{9,4... | collective-permute-start | bytes 196616 | tf_op jit(solution)/shard_map/ppermute | solution.py:44
  26.4 6.4 %collective-permute-start.8 = (f32[128,256]{1,0:T(8,128)S(1)}, f32[128,256]{1,0:T(8,128)S(1)}, u32[]{:S(2)}, u32[]{:S(2)}) collective-permute-start(f32[128,256]{1,0:T(8,128)S(1)} %get-tuple-element.40), channel_id=1, source_target_pairs={{0,32},{1,9},{2,34},{3,11},{4,36},{5,13},{6,38},{7,15},{8,40},{9,1... | collective-permute-start | bytes 393224 | tf_op jit(solution)/shard_map/ppermute | solution.py:44
  29.7 16.5 %collective-permute-start.25 = (bf16[256,128]{1,0:T(8,128)(2,1)}, bf16[256,128]{1,0:T(8,128)(2,1)S(1)}, u32[]{:S(2)}, u32[]{:S(2)}) collective-permute-start(bf16[256,128]{1,0:T(8,128)(2,1)} %param.16), channel_id=1, source_target_pairs={{0,16},{1,65},{2,18},{3,67},{4,20},{5,69},{6,22},{7,71},{8,24},{9,... | collective-permute-start | bytes 196616 | tf_op jit(solution)/shard_map/ppermute | solution.py:44
  43.3 6.6 %collective-permute-start.12 = (bf16[4,64,128]{2,1,0:T(8,128)(2,1)S(1)}, bf16[4,64,128]{2,1,0:T(8,128)(2,1)S(1)}, u32[]{:S(2)}, u32[]{:S(2)}) collective-permute-start(bf16[4,64,128]{2,1,0:T(8,128)(2,1)S(1)} %get-tuple-element.42), channel_id=1, source_target_pairs={{0,32},{1,9},{2,34},{3,11},{4,36},{5,13},{6,38},{7,15},{8,40},{9,1... | collective-permute-start | bytes 196616 | tf_op jit(solution)/shard_map/ppermute | solution.py:44
  43.4 6.5 %collective-permute-start.13 = (bf16[4,64,128]{2,1,0:T(8,128)(2,1)S(1)}, bf16[4,64,128]{2,1,0:T(8,128)(2,1)S(1)}, u32[]{:S(2)}, u32[]{:S(2)}) collective-permute-start(bf16[4,64,128]{2,1,0:T(8,128)(2,1)S(1)} %get-tuple-element.43), channel_id=1, source_target_pairs={{0,64},{1,17},{2,66},{3,19},{4,68},{5,21},{6,70},{7,23},{8,72},{9,... | collective-permute-start | bytes 196616 | tf_op jit(solution)/shard_map/ppermute | solution.py:44
  47.1 28.2 %collective-permute-start.27 = (bf16[4,256,128]{2,1,0:T(8,128)(2,1)S(1)}, bf16[4,256,128]{2,1,0:T(8,128)(2,1)S(1)}, u32[]{:S(2)}, u32[]{:S(2)}) collective-permute-start(bf16[4,256,128]{2,1,0:T(8,128)(2,1)S(1)} %pad_maximum_fusion.w0), channel_id=1, source_target_pairs={{0,32},{1,9},{2,34},{3,11},{4,36},{5,13},{6,38},{7,15},{8,40},{9,1... | collective-permute-start | bytes 786440 | tf_op jit(solution)/shard_map/ppermute | solution.py:44
  48.6 12.5 %collective-permute-start.21 = (f32[128,256]{1,0:T(8,128)S(1)}, f32[128,256]{1,0:T(8,128)S(1)}, u32[]{:S(2)}, u32[]{:S(2)}) collective-permute-start(f32[128,256]{1,0:T(8,128)S(1)} %get-tuple-element.50), channel_id=1, source_target_pairs={{0,96},{1,25},{2,98},{3,27},{4,100},{5,29},{6,102},{7,31},{8,104},... | collective-permute-start | bytes 393224 | tf_op jit(solution)/shard_map/ppermute | solution.py:44
  58.4 5.6 %collective-permute-start.15 = (bf16[4,80,128]{2,1,0:T(8,128)(2,1)S(1)}, bf16[4,80,128]{2,1,0:T(8,128)(2,1)S(1)}, u32[]{:S(2)}, u32[]{:S(2)}) collective-permute-start(bf16[4,80,128]{2,1,0:T(8,128)(2,1)S(1)} %shard_map.134.x0), channel_id=1, source_target_pairs={{0,8},{1,33},{2,10},{3,35},{4,12},{5,37},{6,14},{7,39},{8,16},{9,4... | collective-permute-start | bytes 245768 | tf_op jit(solution)/shard_map/ppermute | solution.py:44
  58.4 7.0 %collective-permute-start.16 = (bf16[4,80,128]{2,1,0:T(8,128)(2,1)S(1)}, bf16[4,80,128]{2,1,0:T(8,128)(2,1)S(1)}, u32[]{:S(2)}, u32[]{:S(2)}) collective-permute-start(bf16[4,80,128]{2,1,0:T(8,128)(2,1)S(1)} %shard_map.134.x0), channel_id=1, source_target_pairs={{0,16},{1,65},{2,18},{3,67},{4,20},{5,69},{6,22},{7,71},{8,24},{9,... | collective-permute-start | bytes 245768 | tf_op jit(solution)/shard_map/ppermute | solution.py:44
  59.9 7.4 %collective-permute-start.17 = (bf16[4,80,128]{2,1,0:T(8,128)(2,1)S(1)}, bf16[4,80,128]{2,1,0:T(8,128)(2,1)S(1)}, u32[]{:S(2)}, u32[]{:S(2)}) collective-permute-start(bf16[4,80,128]{2,1,0:T(8,128)(2,1)S(1)} %shard_map.134.x0), channel_id=1, source_target_pairs={{0,24},{1,97},{2,26},{3,99},{4,28},{5,101},{6,30},{7,103},{8,0},{9... | collective-permute-start | bytes 245768 | tf_op jit(solution)/shard_map/ppermute | solution.py:44
  61.1 23.7 %collective-permute-start.28 = (bf16[4,256,128]{2,1,0:T(8,128)(2,1)S(1)}, bf16[4,256,128]{2,1,0:T(8,128)(2,1)S(1)}, u32[]{:S(2)}, u32[]{:S(2)}) collective-permute-start(bf16[4,256,128]{2,1,0:T(8,128)(2,1)S(1)} %pad_maximum_fusion.w0), channel_id=1, source_target_pairs={{0,64},{1,17},{2,66},{3,19},{4,68},{5,21},{6,70},{7,23},{8,72},{9,... | collective-permute-start | bytes 786440 | tf_op jit(solution)/shard_map/ppermute | solution.py:44
  64.0 20.9 %collective-permute-start.29 = (bf16[4,256,128]{2,1,0:T(8,128)(2,1)S(1)}, bf16[4,256,128]{2,1,0:T(8,128)(2,1)S(1)}, u32[]{:S(2)}, u32[]{:S(2)}) collective-permute-start(bf16[4,256,128]{2,1,0:T(8,128)(2,1)S(1)} %pad_maximum_fusion.w0), channel_id=1, source_target_pairs={{0,96},{1,25},{2,98},{3,27},{4,100},{5,29},{6,102},{7,31},{8,104},... | collective-permute-start | bytes 786440 | tf_op jit(solution)/shard_map/ppermute | solution.py:44
  67.3 7.9 %collective-permute-start.23 = (f32[128,256]{1,0:T(8,128)S(1)}, f32[128,256]{1,0:T(8,128)S(1)}, u32[]{:S(2)}, u32[]{:S(2)}) collective-permute-start(f32[128,256]{1,0:T(8,128)S(1)} %get-tuple-element.52), channel_id=1, source_target_pairs={{0,32},{1,9},{2,34},{3,11},{4,36},{5,13},{6,38},{7,15},{8,40},{9,1... | collective-permute-start | bytes 393224 | tf_op jit(solution)/shard_map/ppermute | solution.py:44
  70.8 14.1 %collective-permute-start.18 = (bf16[4,80,128]{2,1,0:T(8,128)(2,1)S(1)}, bf16[4,80,128]{2,1,0:T(8,128)(2,1)S(1)}, u32[]{:S(2)}, u32[]{:S(2)}) collective-permute-start(bf16[4,80,128]{2,1,0:T(8,128)(2,1)S(1)} %get-tuple-element.46), channel_id=1, source_target_pairs={{0,32},{1,9},{2,34},{3,11},{4,36},{5,13},{6,38},{7,15},{8,40},{9,1... | collective-permute-start | bytes 245768 | tf_op jit(solution)/shard_map/ppermute | solution.py:44
  75.2 9.7 %collective-permute-start.19 = (bf16[4,80,128]{2,1,0:T(8,128)(2,1)S(1)}, bf16[4,80,128]{2,1,0:T(8,128)(2,1)S(1)}, u32[]{:S(2)}, u32[]{:S(2)}) collective-permute-start(bf16[4,80,128]{2,1,0:T(8,128)(2,1)S(1)} %get-tuple-element.47), channel_id=1, source_target_pairs={{0,64},{1,17},{2,66},{3,19},{4,68},{5,21},{6,70},{7,23},{8,72},{9,... | collective-permute-start | bytes 245768 | tf_op jit(solution)/shard_map/ppermute | solution.py:44
  75.3 9.5 %collective-permute-start.20 = (bf16[4,80,128]{2,1,0:T(8,128)(2,1)S(1)}, bf16[4,80,128]{2,1,0:T(8,128)(2,1)S(1)}, u32[]{:S(2)}, u32[]{:S(2)}) collective-permute-start(bf16[4,80,128]{2,1,0:T(8,128)(2,1)S(1)} %get-tuple-element.48), channel_id=1, source_target_pairs={{0,96},{1,25},{2,98},{3,27},{4,100},{5,29},{6,102},{7,31},{8,104},... | collective-permute-start | bytes 245768 | tf_op jit(solution)/shard_map/ppermute | solution.py:44
  88.4 12.1 %collective-permute-start.30 = (bf16[4,2,128,128]{3,2,1,0:T(8,128)(2,1)S(1)}, bf16[4,2,128,128]{3,2,1,0:T(8,128)(2,1)S(1)}, u32[]{:S(2)}, u32[]{:S(2)}) collective-permute-start(bf16[4,2,128,128]{3,2,1,0:T(8,128)(2,1)S(1)} %get-tuple-element.56), channel_id=1, source_target_pairs={{0,1},{1,0},{2,3},{3,2},{4,5},{5,4},{6,7},{7,6},{8,9},{9,8},{10,11... | collective-permute-start | bytes 786440 | tf_op jit(solution)/shard_map/ppermute | solution.py:52
  108.9 5.6 %collective-permute-start.35 = (bf16[2,128,128]{2,1,0:T(8,128)(2,1)S(1)}, bf16[2,128,128]{2,1,0:T(8,128)(2,1)S(1)}, u32[]{:S(2)}, u32[]{:S(2)}) collective-permute-start(bf16[2,128,128]{2,1,0:T(8,128)(2,1)S(1)} %shard_map.139), channel_id=1, source_target_pairs={{0,4},{1,5},{2,6},{3,7},{4,0},{5,1},{6,2},{7,3},{8,12},{9,13},{10,... | collective-permute-start | bytes 196616 | tf_op jit(solution)/shard_map/ppermute | solution.py:48
  (23 other events, 343.2 us)

commit v2 on v1

v2 whole, which is shorter than its diff:
```python
import functools
import math

import jax
import jax.numpy as jnp
from jax import lax
from jax.experimental import pallas as pl
from jax.experimental.pallas import tpu as pltpu
from jax.sharding import PartitionSpec as P

HD = 128
ROWS = 128
PER = 32
PLEN = 4096
TLEN = 256
KB = 1024
MSG = 80
EPS = 1e-06
NEG = -1e30
HINT = 1 << 34
SCALE = HD ** (-0.5)
LOG2E = 1.4426950408889634
F32 = jnp.float32
BF16 = jnp.bfloat16
AXES = ("wide", "narrow")
SMEM = pltpu.SMEM


def device(z, y, x, core):
    return ((z % 4) * 4 + y % 4) * 8 + (x % 4) * 2 + core


def ring(first, step):
    pairs = []
    for z in range(4):
        for y in range(4):
            for x in range(4):
                for core in range(2):
                    along_y = (core == 0) == first
                    target = device(z, y + step, x, core) if along_y else device(z + step, y, x, core)
                    pairs.append((device(z, y, x, core), target))
    return pairs


def shift(value, first, step):
    return lax.ppermute(value, AXES, ring(first, step))


def shift_x(value, step):
    return lax.ppermute(value, "narrow", [(n, (n + 2 * step) % 8) for n in range(8)])


def swap_core(value):
    return lax.ppermute(value, "narrow", [(n, n ^ 1) for n in range(8)])


def call(kernel, out_shape, args, smem=(), smem_out=(), scratch=(), cost=None):
    def spec(is_scalar):
        return pl.BlockSpec(memory_space=SMEM if is_scalar else pltpu.VMEM)

    specs = [spec(i in smem) for i in range(len(args))]
    if isinstance(out_shape, (tuple, list)):
        outs = [spec(i in smem_out) for i in range(len(out_shape))]
    else:
        outs = spec(False)
    flops, nbytes = cost or (1 << 20, 1 << 20)
    return pl.pallas_call(
        kernel,
        out_shape=out_shape,
        in_specs=specs,
        out_specs=outs,
        scratch_shapes=list(scratch),
        compiler_params=pltpu.CompilerParams(vmem_limit_bytes=8 << 20),
        cost_estimate=pl.CostEstimate(flops=flops, bytes_accessed=nbytes, transcendentals=0),
    )(*args)


def struct(shape, dtype):
    return jax.ShapeDtypeStruct(shape, dtype)


def tables_kernel(ids, prompts, lens, tails, freq, table, angles, inverse):
    a, b, core = ids[0], ids[1], ids[2]
    wide = jnp.where(core == 0, 4 * b + a, 4 * a + b)

    def invert(i, carry):
        inverse[prompts[i]] = i
        return carry

    lax.fori_loop(0, 64, invert, 0, unroll=True)
    for base, source in ((0, prompts), (24, inverse)):
        for e in range(4):
            at_b = lax.rem(b + e, 4)
            there = jnp.where(core == 0, 4 * at_b + a, 4 * a + at_b)
            for k in range(4):
                item = source[there * 4 + k]
                z, y = item // 16, lax.rem(item // 4, 4)
                from_a, from_b = jnp.where(core == 0, y, z), jnp.where(core == 0, z, y)
                table[base + 4 * e + k] = lax.rem(a - from_a + 4, 4) * 4 + lax.rem(item, 4)
                if e == 0:
                    table[base + 16 + k] = lax.rem(b - from_b + 4, 4)
                    table[base + 20 + k] = lens[item]
    row = lax.broadcasted_iota(jnp.int32, (ROWS, HD), 0)
    pair = row // 2
    position = jnp.zeros((ROWS, HD), jnp.int32)
    for c in range(64):
        position = jnp.where(pair == c, lens[wide * 4 + c // 16] + tails[c], position)
    position = position + lax.rem(row, 2)
    angles[...] = position.astype(F32) * freq[...]


def norm_kernel(hidden, gain, out):
    values = hidden[...].astype(F32)
    mean_square = jnp.mean(values * values, axis=-1, keepdims=True)
    factor = lax.rsqrt(mean_square + EPS)
    for block in range(16):
        part = hidden[:, block * HD : (block + 1) * HD].astype(F32) * factor
        out[block] = (part * gain[:, block * HD : (block + 1) * HD]).astype(BF16)


def pack_kernel(w0, w1, w2, w3, first, second):
    for d, ref in enumerate((w0, w1, w2, w3)):
        first[d] = ref[:, : 2 * HD]
        second[d] = ref[:, 2 * HD :]


def project(ids, normed, refs):
    a, b, core = ids[0], ids[1], ids[2]
    total = jnp.zeros((ROWS, 2 * HD), F32)
    for e in range(4):
        at_b = lax.rem(b - e + 4, 4)
        left = []
        for d in range(4):
            at_a = lax.rem(a - d + 4, 4)
            left.append(normed[jnp.where(core == 0, 4 * at_b + at_a, 4 * at_a + at_b)])
        right = jnp.concatenate([refs[e][d, :, : 2 * HD] for d in range(4)], axis=0)
        total = total + jnp.dot(
            jnp.concatenate(left, axis=1), right, preferred_element_type=F32
        )
    return total


def head_norm(values, gain, cosine, sine):
    mean_square = jnp.mean(values * values, axis=-1, keepdims=True)
    values = values * lax.rsqrt(mean_square + EPS) * gain
    return values * cosine + pltpu.roll(values, HD // 2, 1) * sine


def query_kernel(ids, normed, w0, w1, w2, w3, gain, cosine, sine, out):
    total = project(ids, normed, (w0, w1, w2, w3))
    for h in range(2):
        head = head_norm(total[:, h * HD : (h + 1) * HD], gain[...], cosine[...], sine[...])
        head = head.astype(BF16)
        for j in range(4):
            out[j, h * PER : (h + 1) * PER] = head[j * PER : (j + 1) * PER]


def pair_kernel(ids, normed, w0, w1, w2, w3, gain, cosine, sine, out):
    total = project(ids, normed, (w0, w1, w2, w3))
    out[0] = head_norm(total[:, :HD], gain[...], cosine[...], sine[...]).astype(BF16)
    out[1] = total[:, HD:].astype(BF16)


def route_kernel(base, index, x0, x1, x2, x3, o0, o1, o2, o3, held):
    for d, ref in enumerate((x0, x1, x2, x3)):
        held[4 * d : 4 * d + 4] = ref[...]
    for e, ref in enumerate((o0, o1, o2, o3)):
        for k in range(4):
            ref[k] = held[index[base + 4 * e + k]]


def column(rows, count):
    lane = lax.broadcasted_iota(jnp.int32, (count, HD), 1)
    row = lax.broadcasted_iota(jnp.int32, (count, HD), 0)
    spread = jnp.broadcast_to(rows, (count, HD))
    return jnp.sum(jnp.where(lane == row, spread, 0.0), axis=1, keepdims=True)


def tail_kernel(start, lens, queries, new_cache, cache, out, lse):
    conts = 8
    row = lax.broadcasted_iota(jnp.int32, (32, TLEN), 0)
    lane = lax.broadcasted_iota(jnp.int32, (32, TLEN), 1)
    owner = lax.rem(row, 16) // 2
    small_row = lax.broadcasted_iota(jnp.int32, (32, 16), 0)
    small_col = lax.broadcasted_iota(jnp.int32, (32, 16), 1)
    visible = (lax.rem(small_row, 16) // 2 == small_col // 2) & (
        lax.rem(small_col, 2) <= lax.rem(small_row, 2)
    )
    owner_out = lax.rem(lax.broadcasted_iota(jnp.int32, (32, HD), 0), 16) // 2
    contract = (((1,), (1,)), ((), ()))
    for g in range(start, start + 4):
        j, half = g // 2, (g % 2) * 16
        q = jnp.concatenate(
            [queries[j, half : half + 16], queries[j, PER + half : PER + half + 16]], axis=0
        )
        score = jnp.zeros((32, TLEN), F32)
        length = jnp.zeros((32, TLEN), jnp.int32)
        for i in range(conts):
            part = lax.dot_general(q, cache[0, g * conts + i], contract, preferred_element_type=F32)
            score = jnp.where(owner == i, part, score)
            length = jnp.where(owner == i, lens[g * conts + i], length)
        score = jnp.where(lane < length, score, NEG)
        fresh = lax.dot_general(
            q, new_cache[0, g * 16 : g * 16 + 16], contract, preferred_element_type=F32
        )
        fresh = jnp.where(visible, fresh, NEG)
        high = jnp.maximum(
            jnp.max(score, axis=1, keepdims=True), jnp.max(fresh, axis=1, keepdims=True)
        )
        weight = jnp.exp2((score - high) * (SCALE * LOG2E))
        fresh_weight = jnp.exp2((fresh - high) * (SCALE * LOG2E))
        sums = jnp.sum(weight, axis=1, keepdims=True) + jnp.sum(
            fresh_weight, axis=1, keepdims=True
        )
        weight = weight.astype(BF16)
        acc = jnp.zeros((32, HD), F32)
        for i in range(conts):
            part = jnp.dot(weight, cache[1, g * conts + i], preferred_element_type=F32)
            acc = jnp.where(owner_out == i, part, acc)
        acc = acc + jnp.dot(
            fresh_weight.astype(BF16),
            new_cache[1, g * 16 : g * 16 + 16],
            preferred_element_type=F32,
        )
        acc = acc / sums
        logs = jnp.broadcast_to(high * SCALE + jnp.log(sums), (32, HD))
        for h in range(2):
            at = (g - start) * 16
            out[h, at : at + 16] = acc[h * 16 : h * 16 + 16]
            lse[h, at : at + 16] = logs[h * 16 : h * 16 + 16]


def prefix_kernel(table, r0, r1, r2, r3, cache, out, held, scores):
    select = [table[16 + s] for s in range(4)]
    lens = [table[20 + s] for s in range(4)]
    counts = [(lens[s] + (KB - 1)) // KB for s in range(4)]
    for e, ref in enumerate((r0, r1, r2, r3)):
        held[e] = ref[...]
    lane = lax.broadcasted_iota(jnp.int32, (64, KB), 1)
    contract = (((1,), (1,)), ((), ()))
    for s in range(4):
        q = held[select[s], s]

        def first(i, high):
            block = cache[0, s, pl.ds(pl.multiple_of(i * KB, KB), KB)]
            part = lax.dot_general(q, block, contract, preferred_element_type=F32)
            part = jnp.where(lane < lens[s] - i * KB, part, NEG)
            scores[i] = part
            for c in range(KB // HD):
                high = jnp.maximum(high, part[:, c * HD : (c + 1) * HD])
            return high

        high = lax.fori_loop(0, counts[s], first, jnp.full((64, HD), NEG, F32))
        high = jnp.max(high, axis=1, keepdims=True)

        def second(i, carry):
            sums, acc = carry
            weight = jnp.exp2((scores[i] - high) * (SCALE * LOG2E))
            for c in range(KB // HD):
                sums = sums + weight[:, c * HD : (c + 1) * HD]
            block = cache[1, s, pl.ds(pl.multiple_of(i * KB, KB), KB)]
            acc = acc + jnp.dot(weight.astype(BF16), block, preferred_element_type=F32)
            return sums, acc

        zero = jnp.zeros((64, HD), F32)
        sums, acc = lax.fori_loop(0, counts[s], second, (zero, zero))
        sums = jnp.sum(sums, axis=1, keepdims=True)
        out[s, :64] = (acc / sums).astype(BF16)
        logs = jnp.broadcast_to(high * SCALE + jnp.log(sums), (64, HD))
        row = lax.broadcasted_iota(jnp.int32, (64, HD), 0)
        column_of = lax.broadcasted_iota(jnp.int32, (64, HD), 1)
        line = jnp.sum(jnp.where(row == column_of, logs, 0.0), axis=0, keepdims=True)
        top = line.astype(BF16).astype(F32)
        middle = (line - top).astype(BF16).astype(F32)
        low = line - top - middle
        which = lax.broadcasted_iota(jnp.int32, (16, HD), 0)
        lines = jnp.where(
            which == 0, top, jnp.where(which == 1, middle, jnp.where(which == 2, low, 0.0))
        )
        out[s, 64:MSG] = lines.astype(BF16)


def finish_kernel(
    ids, table, c0, c1, c2, c3, out_0, lse_0, out_1, lse_1, w0, w1, w2, w3,
    scores, keep, send, held, attention,
):
    for e, ref in enumerate((c0, c1, c2, c3)):
        held[e] = ref[...]
    totals = [[], []]
    for j in range(4):
        message = held[table[40 + j], j]
        lines = message[64:MSG].astype(F32)
        line = (lines[0:1] + lines[1:2]) + lines[2:3]
        logs = column(line, 64)
        for h in range(2):
            rows = slice(j * PER, (j + 1) * PER)
            near_rows = slice((j % 2) * PER, (j % 2 + 1) * PER)
            tail_out, tail_lse = ((out_0, lse_0), (out_1, lse_1))[j // 2]
            prefix_out = message[h * PER : (h + 1) * PER].astype(F32)
            prefix_lse = logs[h * PER : (h + 1) * PER]
            own_lse = tail_lse[h, near_rows][:, 0:1]
            high = jnp.maximum(prefix_lse, own_lse)
            share_a = jnp.exp(prefix_lse - high)
            share_b = jnp.exp(own_lse - high)
            both = share_a + share_b
            merged = (share_a * prefix_out + share_b * tail_out[h, near_rows]) / both
            attention[rows, h * HD : (h + 1) * HD] = merged.astype(BF16)
            totals[h].append(jnp.broadcast_to(high + jnp.log(both), (PER, HD)))
    diagonal = lax.broadcasted_iota(jnp.int32, (ROWS, HD), 0) == lax.broadcasted_iota(
        jnp.int32, (ROWS, HD), 1
    )
    for h in range(2):
        total = jnp.concatenate(totals[h], axis=0)
        scores[h : h + 1] = jnp.sum(jnp.where(diagonal, total, 0.0), axis=0, keepdims=True)
    a, b, core, x = ids[0], ids[1], ids[2], ids[3]
    left = attention[...]
    for e, ref in enumerate((w0, w1, w2, w3)):
        for d in (0, 2):
            right = jnp.concatenate(
                [
                    jnp.concatenate([ref[i, :, h * HD : (h + 1) * HD] for i in (d, d + 1)], axis=1)
                    for h in (2, 3)
                ],
                axis=0,
            )
            both = jnp.dot(left, right, preferred_element_type=F32)
            for i in range(2):
                product = both[:, i * HD : (i + 1) * HD]
                at_a, at_b = lax.rem(a - d - i + 4, 4), lax.rem(b - e + 4, 4)
                block = jnp.where(core == 0, 4 * at_b + at_a, 4 * at_a + at_b)
                mine = (block // 8) == core
                pair = lax.rem(block, 8) // 2
                side = lax.rem(block, 2)

                @pl.when(mine)
                def _():
                    keep[lax.rem(pair - x + 4, 4), side] = product

                @pl.when(jnp.logical_not(mine))
                def _():
                    send[pair, side] = product.astype(BF16)


def first_sum_kernel(ids, keep, got, o0, o1, o2, o3):
    x = ids[3]
    for d in range(4):
        total = keep[d] + got[lax.rem(x + d, 4)].astype(F32)
        if d == 0:
            o0[...] = total
        else:
            (o1, o2, o3)[d - 1][...] = total.astype(BF16)


def second_sum_kernel(ids, o0, g1, g2, g3, hidden, out):
    core, x = ids[2], ids[3]
    for side in range(2):
        total = o0[side] + (
            g1[side].astype(F32) + g2[side].astype(F32) + g3[side].astype(F32)
        )
        at = pl.multiple_of((core * 8 + x * 2 + side) * HD, HD)
        out[side] = (hidden[:, pl.ds(at, HD)].astype(F32) + total).astype(BF16)


def gather_kernel(ids, *refs):
    mine, other, out = refs[:4], refs[4:8], refs[8]
    core, x = ids[2], ids[3]
    for d in range(4):
        for side in range(2):
            at = lax.rem(x - d + 4, 4) * 2 + side
            out[:, pl.ds(pl.multiple_of((core * 8 + at) * HD, HD), HD)] = mine[d][side]
            out[:, pl.ds(pl.multiple_of(((1 - core) * 8 + at) * HD, HD), HD)] = other[d][side]


def split(wide, core):
    z, y = wide // 4, wide % 4
    return jnp.where(core == 0, y, z), jnp.where(core == 0, z, y)


def gather_ring(value, first):
    return [value] + [shift(value, first, step) for step in (1, 2, 3)]


def choose(held, table, base, rows):
    shape = struct((4, rows, HD), BF16)
    sends = call(
        functools.partial(route_kernel, base),
        [shape] * 4,
        [table] + held,
        smem=(0,),
        scratch=[pltpu.VMEM((16, rows, HD), BF16)],
    )
    return [sends[0]] + [shift(sends[step], False, step) for step in (1, 2, 3)]


def body(
    hidden_in, attn_gain, w_qkv, q_gain, k_gain, w_out,
    prefix_cache, tail_cache, prompt_lens, tail_lens, slot_prompt,
):
    wide = lax.axis_index("wide").astype(jnp.int32)
    narrow = lax.axis_index("narrow").astype(jnp.int32)
    core, x = narrow % 2, narrow // 2
    a, b = split(wide, core)
    ids = jnp.stack([a, b, core, x]).astype(jnp.int32)

    channel = jnp.arange(HD, dtype=jnp.int32)
    inverse_freq = jnp.exp((channel % 64).astype(F32) * (-2.0 / HD) * math.log(1000000.0))
    table, angles = call(
        tables_kernel,
        [struct((64,), jnp.int32), struct((ROWS, HD), F32)],
        [ids, slot_prompt, prompt_lens, tail_lens, inverse_freq.reshape(1, HD)],
        smem=(0, 1, 2, 3),
        smem_out=(0,),
        scratch=[pltpu.SMEM((64,), jnp.int32)],
    )
    cosine = jnp.cos(angles)
    sine = jnp.sin(angles) * jnp.where(channel < HD // 2, -1.0, 1.0)[None, :]
    q_gain, k_gain = q_gain.reshape(1, HD), k_gain.reshape(1, HD)

    mixed = jnp.concatenate([w_qkv, w_out[:HD], w_out[HD:]], axis=1)
    near = gather_ring(mixed, True)
    normed = call(
        norm_kernel,
        struct((16, ROWS, HD), BF16),
        [hidden_in, attn_gain.reshape(1, -1)],
        cost=(HINT, 1 << 20),
    )
    near, normed, table = lax.optimization_barrier((near, normed, table))
    near_query, near_other = call(
        pack_kernel, [struct((4, ROWS, 2 * HD), BF16), struct((4, ROWS, 4 * HD), BF16)], near
    )
    far_query = gather_ring(near_query, False)
    far_other = gather_ring(near_other, False)
    queries = call(
        query_kernel,
        struct((4, 64, HD), BF16),
        [ids, normed] + far_query + [q_gain, cosine, sine],
        smem=(0,),
        cost=(2 * ROWS * 256 * 2048, 2 << 20),
    )

    held = gather_ring(queries, True)
    asked = choose(held, table, 0, 64)
    new_cache = call(
        pair_kernel,
        struct((2, ROWS, HD), BF16),
        [ids, normed] + far_other + [k_gain, cosine, sine],
        smem=(0,),
        cost=(2 * ROWS * 256 * 2048, 2 << 20),
    )
    tails = []
    for start in (0, 4):
        tails.append(
            call(
                functools.partial(tail_kernel, start),
                [struct((2, 64, HD), F32), struct((2, 64, HD), F32)],
                [tail_lens, queries, new_cache, tail_cache],
                smem=(0,),
                cost=(2 * 64 * 32 * TLEN * HD, 4 << 20),
            )
        )
    asked, tails[0] = lax.optimization_barrier((asked, tails[0]))
    results = call(
        prefix_kernel,
        struct((4, MSG, HD), BF16),
        [table] + asked + [prefix_cache],
        smem=(0,),
        scratch=[pltpu.VMEM((4, 4, 64, HD), BF16), pltpu.VMEM((PLEN // KB, 64, KB), F32)],
        cost=(2 * 2 * 4 * 64 * PLEN * HD, 8 << 20),
    )
    held = gather_ring(results, True)
    held, tails[1] = lax.optimization_barrier((held, tails[1]))
    homes = choose(held, table, 24, MSG)

    scores, keep, send = call(
        finish_kernel,
        [
            struct((2, ROWS), F32),
            struct((4, 2, ROWS, HD), F32),
            struct((4, 2, ROWS, HD), BF16),
        ],
        [ids, table] + homes + [*tails[0], *tails[1]] + far_other,
        smem=(0, 1),
        scratch=[pltpu.VMEM((4, 4, MSG, HD), BF16), pltpu.VMEM((ROWS, 2 * HD), BF16)],
        cost=(2 * ROWS * 256 * 2048, 3 << 20),
    )
    got = swap_core(send)
    block = struct((2, ROWS, HD), BF16)
    sums = call(
        first_sum_kernel,
        [struct((2, ROWS, HD), F32), block, block, block],
        [ids, keep, got],
        smem=(0,),
    )
    moved = [shift_x(sums[step], step) for step in (1, 2, 3)]
    mine = call(second_sum_kernel, block, [ids, sums[0]] + moved + [hidden_in], smem=(0,))
    ours = [mine] + [shift_x(mine, step) for step in (1, 2, 3)]
    theirs = [swap_core(piece) for piece in ours]
    hidden_out = call(gather_kernel, struct((ROWS, 2048), BF16), [ids] + ours + theirs, smem=(0,))
    return (hidden_out, scores.T, new_cache)


def solution(mesh):
    in_specs = (
        P("wide", None),
        P(),
        P("wide", "narrow"),
        P(),
        P(),
        P("narrow", "wide"),
        P(None, "wide", None, "narrow"),
        P(None, "wide", None, "narrow"),
        P(),
        P("wide"),
        P(),
    )
    out_specs = (P("wide", None), P("wide", "narrow"), P(None, "wide", "narrow"))
    return jax.shard_map(body, mesh=mesh, in_specs=in_specs, out_specs=out_specs, check_vma=False)
```

time: 123 us -> 101 us (0.82)
  starting transfers between devices: 62.5 us -> 44.3 us
  waiting for transfers between devices: 23.8 us -> 29.3 us
  other arithmetic: 5.34 us -> 1.26 us
  local copies, waits for them, and re-layouts: 7.32 us -> 4.58 us
  Pallas kernels: 22 us -> 19.7 us
    ppermute x30 -> x21, starting transfers between devices: 39.4 us -> 25.5 us  [shift(): return lax.ppermute(value, AXES, ring(first, step))]
    ppermute x30 -> x21, waiting for transfers between devices: 16.8 us -> 24.9 us  [shift(): return lax.ppermute(value, AXES, ring(first, step))]
    reduce_sum x4 -> x0, other arithmetic: 3.73 us -> none  [the longest x3 2.83 us: lookup(): jnp.sum(jnp.where(indices[:, None] == entries[None, :], table[None, :], 0...]
    unnamed x19 -> x28, local copies, waits for them, and re-layouts: 7.32 us -> 3.8 us
    ppermute x2 -> x5, starting transfers between devices: 14.5 us -> 11.1 us  [swap_core(): return lax.ppermute(value, 'narrow', [(n, n ^ 1) for n in range(8)])]
    ppermute x6, waiting for transfers between devices: 5.29 us -> 2.27 us  [shift_x(): lax.ppermute(value, 'narrow', [(n, (n + 2 * step) % 8) for n in range(8)])]
    pallas_call x11 -> x14, Pallas kernels: 22 us -> 19.7 us  [call(): pl.pallas_call(kernel, out_shape=out_shape, in_specs=specs, out_specs=out...]
  transfers between devices with their start and end apart: 38 -> 32, of which waited for: 15 -> 15; matrix products, arithmetic and copies ran while one was open for 5% -> 0% of each run, Pallas kernels for 13% -> 10%
where the time goes in v2:
time: 101 us; the launch traced here: 100 us
  starting transfers between devices  44.3 us (44%)
  waiting for transfers between devices  29.3 us (29%)
  Pallas kernels  19.7 us (20%)
  local copies, waits for them, and re-layouts  4.58 us (5%)
  other arithmetic  1.26 us (1%)
    ppermute x21, starting transfers between devices, shift(): return lax.ppermute(value, AXES, ring(first, step))  25.5 us
    ppermute x21, waiting for transfers between devices, shift(): return lax.ppermute(value, AXES, ring(first, step))  24.9 us
    pallas_call x14, Pallas kernels, call(): pl.pallas_call(kernel, out_shape=out_shape, in_specs=specs, out_specs=out...  19.7 us
    ppermute x5, starting transfers between devices, swap_core(): return lax.ppermute(value, 'narrow', [(n, n ^ 1) for n in range(8)])  11.1 us
    ppermute x6, starting transfers between devices, shift_x(): lax.ppermute(value, 'narrow', [(n, (n + 2 * step) % 8) for n in range(8)])  7.68 us
    unnamed x28, local copies, waits for them, and re-layouts  3.8 us
    ppermute x6, waiting for transfers between devices, shift_x(): lax.ppermute(value, 'narrow', [(n, (n + 2 * step) % 8) for n in range(8)])  2.27 us
    ppermute x5, waiting for transfers between devices, swap_core(): return lax.ppermute(value, 'narrow', [(n, n ^ 1) for n in range(8)])  2.1 us
  transfers between devices with their start and end apart: 32, of which 15 were waited for; matrix products, arithmetic and copies ran while one was open for 0% of the time, Pallas kernels for 10%

profile of v2, /device:TPU:1, one launch (start us, length us, event | category | flops | bytes accessed | tf_op | source)
XLA Modules:
  0.0 100.0 jit_solution(2160627631178412273)
XLA Ops:
  2.3 4.7 %collective-permute-start.2 = (bf16[128,768]{1,0:T(8,128)(2,1)S(1)}, bf16[128,768]{1,0:T(8,128)(2,1)S(1)}, u32[]{:S(2)}, u32[]{:S(2)}) collective-permute-start(bf16[128,768]{1,0:T(8,128)(2,1)S(1)} %pad_maximum_fusion.w0), channel_id=1, source_target_pairs={{0,24},{1,97},{2,26},{3,99},{4,28},{5,101},{6,30},{7,103},{8,0},{9... | collective-permute-start | bytes 589832 | tf_op jit(solution)/shard_map/ppermute | solution.py:46
  11.0 1.7 %shard_map.131 = (s32[64]{0:T(128)S(1)}, f32[128,128]{1,0:T(8,128)S(1)}) custom-call(s32[4]{0:T(128)S(1)} %pad_add_fusion.ids, s32[64]{0:T(128)S(1)} %copy-done.8, s32[64]{0:T(128)S(1)} %copy-done.9, s32[64]{0:T(128)S(1)} %copy-done.4, f32[1,128]{1,0:T(1,128)S(1)} %fusion.2.freq), custom_call_target="tpu_custom_call" | custom-call | flops 1048576 | bytes 1048576 | tf_op jit(solution)/shard_map/pallas_call | solution.py:67
  13.4 1.8 %collective-permute-done.w1 = bf16[128,768]{1,0:T(8,128)(2,1)S(1)} collective-permute-done((bf16[128,768]{1,0:T(8,128)(2,1)S(1)}, bf16[128,768]{1,0:T(8,128)(2,1)S(1)}, u32[]{:S(2)}, u32[]{:S(2)}) %collective-permute-start) | collective-permute-done | bytes 196640 | tf_op jit(solution)/shard_map/ppermute | solution.py:46
  15.2 2.5 %collective-permute-start.5 = (bf16[4,128,256]{2,1,0:T(8,128)(2,1)S(1)}, bf16[4,128,256]{2,1,0:T(8,128)(2,1)S(1)}, u32[]{:S(2)}, u32[]{:S(2)}) collective-permute-start(bf16[4,128,256]{2,1,0:T(8,128)(2,1)S(1)} %get-tuple-element.51.w0), channel_id=1, source_target_pairs={{0,96},{1,25},{2,98},{3,27},{4,100},{5,29},{6,102},{7,31},{8,104},... | collective-permute-start | bytes 786440 | tf_op jit(solution)/shard_map/ppermute | solution.py:46
  19.2 3.6 %collective-permute-start.13 = (bf16[4,128,512]{2,1,0:T(8,128)(2,1)S(1)}, bf16[4,128,512]{2,1,0:T(8,128)(2,1)S(1)}, u32[]{:S(2)}, u32[]{:S(2)}) collective-permute-start(bf16[4,128,512]{2,1,0:T(8,128)(2,1)S(1)} %get-tuple-element.57.w0), channel_id=1, source_target_pairs={{0,64},{1,17},{2,66},{3,19},{4,68},{5,21},{6,70},{7,23},{8,72},{9,... | collective-permute-start | bytes 1572872 | tf_op jit(solution)/shard_map/ppermute | solution.py:46
  23.0 2.0 %collective-permute-done.4.w2 = bf16[4,128,256]{2,1,0:T(8,128)(2,1)S(1)} collective-permute-done((bf16[4,128,256]{2,1,0:T(8,128)(2,1)S(1)}, bf16[4,128,256]{2,1,0:T(8,128)(2,1)S(1)}, u32[]{:S(2)}, u32[]{:S(2)}) %collective-permute-start.4) | collective-permute-done | bytes 262176 | tf_op jit(solution)/shard_map/ppermute | solution.py:46
  25.0 3.0 %collective-permute-done.3.w1 = bf16[4,128,256]{2,1,0:T(8,128)(2,1)S(1)} collective-permute-done((bf16[4,128,256]{2,1,0:T(8,128)(2,1)S(1)}, bf16[4,128,256]{2,1,0:T(8,128)(2,1)S(1)}, u32[]{:S(2)}, u32[]{:S(2)}) %collective-permute-start.3) | collective-permute-done | bytes 262176 | tf_op jit(solution)/shard_map/ppermute | solution.py:46
  30.4 8.3 %collective-permute-done.8.x3 = bf16[4,64,128]{2,1,0:T(8,128)(2,1)S(1)} collective-permute-done((bf16[4,64,128]{2,1,0:T(8,128)(2,1)S(1)}, bf16[4,64,128]{2,1,0:T(8,128)(2,1)S(1)}, u32[]{:S(2)}, u32[]{:S(2)}) %collective-permute-start.8) | collective-permute-done | bytes 65568 | tf_op jit(solution)/shard_map/ppermute | solution.py:46
  38.7 5.2 %collective-permute-done.6.x1 = bf16[4,64,128]{2,1,0:T(8,128)(2,1)S(1)} collective-permute-done((bf16[4,64,128]{2,1,0:T(8,128)(2,1)S(1)}, bf16[4,64,128]{2,1,0:T(8,128)(2,1)S(1)}, u32[]{:S(2)}, u32[]{:S(2)}) %collective-permute-start.6) | collective-permute-done | bytes 65568 | tf_op jit(solution)/shard_map/ppermute | solution.py:46
  47.2 1.7 %shard_map.135.new_cache = bf16[2,128,128]{2,1,0:T(8,128)(2,1)} custom-call(s32[4]{0:T(128)S(1)} %pad_add_fusion.ids, bf16[16,128,128]{2,1,0:T(8,128)(2,1)S(1)} %shard_map.130.normed, bf16[4,128,512]{2,1,0:T(8,128)(2,1)S(1)} %get-tuple-element.57.w0, bf16[4,128,512]{2,1,0:T(8,128)(2,1)S(1)} %collective-permute-done.12.w1, ...), custom_call_target="tpu_custom_call" | custom-call | flops 134217728 | bytes 2097152 | tf_op jit(solution)/shard_map/pallas_call | solution.py:67
  49.7 2.4 %shard_map.136 = (f32[2,64,128]{2,1,0:T(8,128)S(1)}, f32[2,64,128]{2,1,0:T(8,128)S(1)}) custom-call(s32[64]{0:T(128)S(1)} %copy-done.4, bf16[4,64,128]{2,1,0:T(8,128)(2,1)S(1)} %shard_map.133.x0.queries, bf16[2,128,128]{2,1,0:T(8,128)(2,1)S(1)} %copy-done, bf16[2,64,256,128]{3,2,1,0:T(8,128)(2,1)S(1)} %bitcast.9), custom_call_target="tpu_custom_call" | custom-call | flops 134217728 | bytes 4194304 | tf_op jit(solution)/shard_map/pallas_call | solution.py:67
  52.2 3.4 %shard_map.137.x0 = bf16[4,80,128]{2,1,0:T(8,128)(2,1)S(1)} custom-call(s32[64]{0:T(128)S(1)} %get-tuple-element.45.index.table, bf16[4,64,128]{2,1,0:T(8,128)(2,1)S(1)} %get-tuple-element.60.r0, bf16[4,64,128]{2,1,0:T(8,128)(2,1)S(1)} %collective-permute-done.9.r1, bf16[4,64,128]{2,1,0:T(8,128)(2,1)S(1)} %collective-permute-done.10.r2, ...), custom_call_target="tpu_custom_call" | custom-call | flops 536870912 | bytes 8388608 | tf_op jit(solution)/shard_map/pallas_call | solution.py:67
  55.6 2.4 %collective-permute-start.17 = (bf16[4,80,128]{2,1,0:T(8,128)(2,1)S(1)}, bf16[4,80,128]{2,1,0:T(8,128)(2,1)S(1)}, u32[]{:S(2)}, u32[]{:S(2)}) collective-permute-start(bf16[4,80,128]{2,1,0:T(8,128)(2,1)S(1)} %shard_map.137.x0), channel_id=1, source_target_pairs={{0,24},{1,97},{2,26},{3,99},{4,28},{5,101},{6,30},{7,103},{8,0},{9... | collective-permute-start | bytes 245768 | tf_op jit(solution)/shard_map/ppermute | solution.py:46
  58.6 2.4 %shard_map.138 = (f32[2,64,128]{2,1,0:T(8,128)S(1)}, f32[2,64,128]{2,1,0:T(8,128)S(1)}) custom-call(s32[64]{0:T(128)S(1)} %copy-done.4, bf16[4,64,128]{2,1,0:T(8,128)(2,1)S(1)} %shard_map.133.x0.queries, bf16[2,128,128]{2,1,0:T(8,128)(2,1)S(1)} %copy-done.1, bf16[2,64,256,128]{3,2,1,0:T(8,128)(2,1)S(1)} %bitcast.9), custom_call_target="tpu_custom_call" | custom-call | flops 134217728 | bytes 4194304 | tf_op jit(solution)/shard_map/pallas_call | solution.py:67
  61.1 2.0 %collective-permute-done.16.x2 = bf16[4,80,128]{2,1,0:T(8,128)(2,1)S(1)} collective-permute-done((bf16[4,80,128]{2,1,0:T(8,128)(2,1)S(1)}, bf16[4,80,128]{2,1,0:T(8,128)(2,1)S(1)}, u32[]{:S(2)}, u32[]{:S(2)}) %collective-permute-start.16) | collective-permute-done | bytes 81952 | tf_op jit(solution)/shard_map/ppermute | solution.py:46
  64.6 3.1 %collective-permute-start.19 = (bf16[4,80,128]{2,1,0:T(8,128)(2,1)S(1)}, bf16[4,80,128]{2,1,0:T(8,128)(2,1)S(1)}, u32[]{:S(2)}, u32[]{:S(2)}) collective-permute-start(bf16[4,80,128]{2,1,0:T(8,128)(2,1)S(1)} %get-tuple-element.72), channel_id=1, source_target_pairs={{0,64},{1,17},{2,66},{3,19},{4,68},{5,21},{6,70},{7,23},{8,72},{9,... | collective-permute-start | bytes 245768 | tf_op jit(solution)/shard_map/ppermute | solution.py:46
  67.7 2.0 %collective-permute-start.20 = (bf16[4,80,128]{2,1,0:T(8,128)(2,1)S(1)}, bf16[4,80,128]{2,1,0:T(8,128)(2,1)S(1)}, u32[]{:S(2)}, u32[]{:S(2)}) collective-permute-start(bf16[4,80,128]{2,1,0:T(8,128)(2,1)S(1)} %get-tuple-element.73), channel_id=1, source_target_pairs={{0,96},{1,25},{2,98},{3,27},{4,100},{5,29},{6,102},{7,31},{8,104},... | collective-permute-start | bytes 245768 | tf_op jit(solution)/shard_map/ppermute | solution.py:46
  71.2 3.0 %shard_map.140 = (f32[2,128]{1,0:T(2,128)}, f32[4,2,128,128]{3,2,1,0:T(8,128)S(1)}, bf16[4,2,128,128]{3,2,1,0:T(8,128)(2,1)S(1)}) custom-call(s32[4]{0:T(128)S(1)} %pad_add_fusion.ids, s32[64]{0:T(128)S(1)} %get-tuple-element.45.index.table, bf16[4,80,128]{2,1,0:T(8,128)(2,1)S(1)} %get-tuple-element.70.c0, ...), custom_call_target="tpu_custom_call" | custom-call | flops 134217728 | bytes 3145728 | tf_op jit(solution)/shard_map/pallas_call | solution.py:67
  74.1 3.2 %collective-permute-start.21 = (bf16[4,2,128,128]{3,2,1,0:T(8,128)(2,1)S(1)}, bf16[4,2,128,128]{3,2,1,0:T(8,128)(2,1)S(1)}, u32[]{:S(2)}, u32[]{:S(2)}) collective-permute-start(bf16[4,2,128,128]{3,2,1,0:T(8,128)(2,1)S(1)} %get-tuple-element.79), channel_id=1, source_target_pairs={{0,1},{1,0},{2,3},{3,2},{4,5},{5,4},{6,7},{7,6},{8,9},{9,8},{10,11... | collective-permute-start | bytes 786440 | tf_op jit(solution)/shard_map/ppermute | solution.py:54
  80.4 2.4 %collective-permute-start.23 = (bf16[2,128,128]{2,1,0:T(8,128)(2,1)S(1)}, bf16[2,128,128]{2,1,0:T(8,128)(2,1)S(1)}, u32[]{:S(2)}, u32[]{:S(2)}) collective-permute-start(bf16[2,128,128]{2,1,0:T(8,128)(2,1)S(1)} %get-tuple-element.82), channel_id=1, source_target_pairs={{0,4},{1,5},{2,6},{3,7},{4,0},{5,1},{6,2},{7,3},{8,12},{9,13},{10,... | collective-permute-start | bytes 196616 | tf_op jit(solution)/shard_map/ppermute | solution.py:50
  84.0 1.8 %collective-permute-done.23.g2 = bf16[2,128,128]{2,1,0:T(8,128)(2,1)S(1)} collective-permute-done((bf16[2,128,128]{2,1,0:T(8,128)(2,1)S(1)}, bf16[2,128,128]{2,1,0:T(8,128)(2,1)S(1)}, u32[]{:S(2)}, u32[]{:S(2)}) %collective-permute-start.23) | collective-permute-done | bytes 65568 | tf_op jit(solution)/shard_map/ppermute | solution.py:50
  86.9 2.1 %collective-permute-start.27 = (bf16[2,128,128]{2,1,0:T(8,128)(2,1)S(1)}, bf16[2,128,128]{2,1,0:T(8,128)(2,1)S(1)}, u32[]{:S(2)}, u32[]{:S(2)}) collective-permute-start(bf16[2,128,128]{2,1,0:T(8,128)(2,1)S(1)} %shard_map.142.refs_0_), channel_id=1, source_target_pairs={{0,6},{1,7},{2,0},{3,1},{4,2},{5,3},{6,4},{7,5},{8,14},{9,15},{10,... | collective-permute-start | bytes 196616 | tf_op jit(solution)/shard_map/ppermute | solution.py:50
  89.7 2.6 %collective-permute-start.28 = (bf16[2,128,128]{2,1,0:T(8,128)(2,1)S(1)}, bf16[2,128,128]{2,1,0:T(8,128)(2,1)S(1)}, u32[]{:S(2)}, u32[]{:S(2)}) collective-permute-start(bf16[2,128,128]{2,1,0:T(8,128)(2,1)S(1)} %shard_map.142.refs_0_), channel_id=1, source_target_pairs={{0,1},{1,0},{2,3},{3,2},{4,5},{5,4},{6,7},{7,6},{8,9},{9,8},{10,11... | collective-permute-start | bytes 196616 | tf_op jit(solution)/shard_map/ppermute | solution.py:54
  93.9 3.4 %collective-permute-start.30 = (bf16[2,128,128]{2,1,0:T(8,128)(2,1)S(1)}, bf16[2,128,128]{2,1,0:T(8,128)(2,1)S(1)}, u32[]{:S(2)}, u32[]{:S(2)}) collective-permute-start(bf16[2,128,128]{2,1,0:T(8,128)(2,1)S(1)} %collective-permute-done.26.refs_2_), channel_id=1, source_target_pairs={{0,1},{1,0},{2,3},{3,2},{4,5},{5,4},{6,7},{7,6},{8,9},{9,8},{10,11... | collective-permute-start | bytes 196616 | tf_op jit(solution)/shard_map/ppermute | solution.py:54
  (90 shorter events, 28.6 us)
Async XLA Ops:
  2.3 10.4 %collective-permute-start.2 = (bf16[128,768]{1,0:T(8,128)(2,1)S(1)}, bf16[128,768]{1,0:T(8,128)(2,1)S(1)}, u32[]{:S(2)}, u32[]{:S(2)}) collective-permute-start(bf16[128,768]{1,0:T(8,128)(2,1)S(1)} %pad_maximum_fusion.w0), channel_id=1, source_target_pairs={{0,24},{1,97},{2,26},{3,99},{4,28},{5,101},{6,30},{7,103},{8,0},{9... | collective-permute-start | bytes 589832 | tf_op jit(solution)/shard_map/ppermute | solution.py:46
  7.0 6.4 %collective-permute-start.1 = (bf16[128,768]{1,0:T(8,128)(2,1)S(1)}, bf16[128,768]{1,0:T(8,128)(2,1)S(1)}, u32[]{:S(2)}, u32[]{:S(2)}) collective-permute-start(bf16[128,768]{1,0:T(8,128)(2,1)S(1)} %pad_maximum_fusion.w0), channel_id=1, source_target_pairs={{0,16},{1,65},{2,18},{3,67},{4,20},{5,69},{6,22},{7,71},{8,24},{9,... | collective-permute-start | bytes 589832 | tf_op jit(solution)/shard_map/ppermute | solution.py:46
  7.0 8.1 %collective-permute-start = (bf16[128,768]{1,0:T(8,128)(2,1)S(1)}, bf16[128,768]{1,0:T(8,128)(2,1)S(1)}, u32[]{:S(2)}, u32[]{:S(2)}) collective-permute-start(bf16[128,768]{1,0:T(8,128)(2,1)S(1)} %pad_maximum_fusion.w0), channel_id=1, source_target_pairs={{0,8},{1,33},{2,10},{3,35},{4,12},{5,37},{6,14},{7,39},{8,16},{9,4... | collective-permute-start | bytes 589832 | tf_op jit(solution)/shard_map/ppermute | solution.py:46
  15.2 7.6 %collective-permute-start.5 = (bf16[4,128,256]{2,1,0:T(8,128)(2,1)S(1)}, bf16[4,128,256]{2,1,0:T(8,128)(2,1)S(1)}, u32[]{:S(2)}, u32[]{:S(2)}) collective-permute-start(bf16[4,128,256]{2,1,0:T(8,128)(2,1)S(1)} %get-tuple-element.51.w0), channel_id=1, source_target_pairs={{0,96},{1,25},{2,98},{3,27},{4,100},{5,29},{6,102},{7,31},{8,104},... | collective-permute-start | bytes 786440 | tf_op jit(solution)/shard_map/ppermute | solution.py:46
  17.7 28.4 %collective-permute-start.14 = (bf16[4,128,512]{2,1,0:T(8,128)(2,1)S(1)}, bf16[4,128,512]{2,1,0:T(8,128)(2,1)S(1)}, u32[]{:S(2)}, u32[]{:S(2)}) collective-permute-start(bf16[4,128,512]{2,1,0:T(8,128)(2,1)S(1)} %get-tuple-element.57.w0), channel_id=1, source_target_pairs={{0,96},{1,25},{2,98},{3,27},{4,100},{5,29},{6,102},{7,31},{8,104},... | collective-permute-start | bytes 1572872 | tf_op jit(solution)/shard_map/ppermute | solution.py:46
  18.2 6.8 %collective-permute-start.4 = (bf16[4,128,256]{2,1,0:T(8,128)(2,1)S(1)}, bf16[4,128,256]{2,1,0:T(8,128)(2,1)S(1)}, u32[]{:S(2)}, u32[]{:S(2)}) collective-permute-start(bf16[4,128,256]{2,1,0:T(8,128)(2,1)S(1)} %get-tuple-element.51.w0), channel_id=1, source_target_pairs={{0,64},{1,17},{2,66},{3,19},{4,68},{5,21},{6,70},{7,23},{8,72},{9,... | collective-permute-start | bytes 786440 | tf_op jit(solution)/shard_map/ppermute | solution.py:46
  18.5 9.5 %collective-permute-start.3 = (bf16[4,128,256]{2,1,0:T(8,128)(2,1)S(1)}, bf16[4,128,256]{2,1,0:T(8,128)(2,1)S(1)}, u32[]{:S(2)}, u32[]{:S(2)}) collective-permute-start(bf16[4,128,256]{2,1,0:T(8,128)(2,1)S(1)} %get-tuple-element.51.w0), channel_id=1, source_target_pairs={{0,32},{1,9},{2,34},{3,11},{4,36},{5,13},{6,38},{7,15},{8,40},{9,1... | collective-permute-start | bytes 786440 | tf_op jit(solution)/shard_map/ppermute | solution.py:46
  19.2 28.1 %collective-permute-start.13 = (bf16[4,128,512]{2,1,0:T(8,128)(2,1)S(1)}, bf16[4,128,512]{2,1,0:T(8,128)(2,1)S(1)}, u32[]{:S(2)}, u32[]{:S(2)}) collective-permute-start(bf16[4,128,512]{2,1,0:T(8,128)(2,1)S(1)} %get-tuple-element.57.w0), channel_id=1, source_target_pairs={{0,64},{1,17},{2,66},{3,19},{4,68},{5,21},{6,70},{7,23},{8,72},{9,... | collective-permute-start | bytes 1572872 | tf_op jit(solution)/shard_map/ppermute | solution.py:46
  22.7 24.5 %collective-permute-start.12 = (bf16[4,128,512]{2,1,0:T(8,128)(2,1)S(1)}, bf16[4,128,512]{2,1,0:T(8,128)(2,1)S(1)}, u32[]{:S(2)}, u32[]{:S(2)}) collective-permute-start(bf16[4,128,512]{2,1,0:T(8,128)(2,1)S(1)} %get-tuple-element.57.w0), channel_id=1, source_target_pairs={{0,32},{1,9},{2,34},{3,11},{4,36},{5,13},{6,38},{7,15},{8,40},{9,1... | collective-permute-start | bytes 1572872 | tf_op jit(solution)/shard_map/ppermute | solution.py:46
  29.0 9.7 %collective-permute-start.8 = (bf16[4,64,128]{2,1,0:T(8,128)(2,1)S(1)}, bf16[4,64,128]{2,1,0:T(8,128)(2,1)S(1)}, u32[]{:S(2)}, u32[]{:S(2)}) collective-permute-start(bf16[4,64,128]{2,1,0:T(8,128)(2,1)S(1)} %shard_map.133.x0.queries), channel_id=1, source_target_pairs={{0,24},{1,97},{2,26},{3,99},{4,28},{5,101},{6,30},{7,103},{8,0},{9... | collective-permute-start | bytes 196616 | tf_op jit(solution)/shard_map/ppermute | solution.py:46
  30.0 8.7 %collective-permute-start.7 = (bf16[4,64,128]{2,1,0:T(8,128)(2,1)S(1)}, bf16[4,64,128]{2,1,0:T(8,128)(2,1)S(1)}, u32[]{:S(2)}, u32[]{:S(2)}) collective-permute-start(bf16[4,64,128]{2,1,0:T(8,128)(2,1)S(1)} %shard_map.133.x0.queries), channel_id=1, source_target_pairs={{0,16},{1,65},{2,18},{3,67},{4,20},{5,69},{6,22},{7,71},{8,24},{9,... | collective-permute-start | bytes 196616 | tf_op jit(solution)/shard_map/ppermute | solution.py:46
  38.7 5.2 %collective-permute-start.6 = (bf16[4,64,128]{2,1,0:T(8,128)(2,1)S(1)}, bf16[4,64,128]{2,1,0:T(8,128)(2,1)S(1)}, u32[]{:S(2)}, u32[]{:S(2)}) collective-permute-start(bf16[4,64,128]{2,1,0:T(8,128)(2,1)S(1)} %shard_map.133.x0.queries), channel_id=1, source_target_pairs={{0,8},{1,33},{2,10},{3,35},{4,12},{5,37},{6,14},{7,39},{8,16},{9,4... | collective-permute-start | bytes 196616 | tf_op jit(solution)/shard_map/ppermute | solution.py:46
  44.5 7.7 %collective-permute-start.9 = (bf16[4,64,128]{2,1,0:T(8,128)(2,1)S(1)}, bf16[4,64,128]{2,1,0:T(8,128)(2,1)S(1)}, u32[]{:S(2)}, u32[]{:S(2)}) collective-permute-start(bf16[4,64,128]{2,1,0:T(8,128)(2,1)S(1)} %get-tuple-element.54), channel_id=1, source_target_pairs={{0,32},{1,9},{2,34},{3,11},{4,36},{5,13},{6,38},{7,15},{8,40},{9,1... | collective-permute-start | bytes 196616 | tf_op jit(solution)/shard_map/ppermute | solution.py:46
  44.6 7.6 %collective-permute-start.10 = (bf16[4,64,128]{2,1,0:T(8,128)(2,1)S(1)}, bf16[4,64,128]{2,1,0:T(8,128)(2,1)S(1)}, u32[]{:S(2)}, u32[]{:S(2)}) collective-permute-start(bf16[4,64,128]{2,1,0:T(8,128)(2,1)S(1)} %get-tuple-element.55), channel_id=1, source_target_pairs={{0,64},{1,17},{2,66},{3,19},{4,68},{5,21},{6,70},{7,23},{8,72},{9,... | collective-permute-start | bytes 196616 | tf_op jit(solution)/shard_map/ppermute | solution.py:46
  46.0 6.2 %collective-permute-start.11 = (bf16[4,64,128]{2,1,0:T(8,128)(2,1)S(1)}, bf16[4,64,128]{2,1,0:T(8,128)(2,1)S(1)}, u32[]{:S(2)}, u32[]{:S(2)}) collective-permute-start(bf16[4,64,128]{2,1,0:T(8,128)(2,1)S(1)} %get-tuple-element.56), channel_id=1, source_target_pairs={{0,96},{1,25},{2,98},{3,27},{4,100},{5,29},{6,102},{7,31},{8,104},... | collective-permute-start | bytes 196616 | tf_op jit(solution)/shard_map/ppermute | solution.py:46
  55.6 5.5 %collective-permute-start.17 = (bf16[4,80,128]{2,1,0:T(8,128)(2,1)S(1)}, bf16[4,80,128]{2,1,0:T(8,128)(2,1)S(1)}, u32[]{:S(2)}, u32[]{:S(2)}) collective-permute-start(bf16[4,80,128]{2,1,0:T(8,128)(2,1)S(1)} %shard_map.137.x0), channel_id=1, source_target_pairs={{0,24},{1,97},{2,26},{3,99},{4,28},{5,101},{6,30},{7,103},{8,0},{9... | collective-permute-start | bytes 245768 | tf_op jit(solution)/shard_map/ppermute | solution.py:46
  58.0 5.7 %collective-permute-start.15 = (bf16[4,80,128]{2,1,0:T(8,128)(2,1)S(1)}, bf16[4,80,128]{2,1,0:T(8,128)(2,1)S(1)}, u32[]{:S(2)}, u32[]{:S(2)}) collective-permute-start(bf16[4,80,128]{2,1,0:T(8,128)(2,1)S(1)} %shard_map.137.x0), channel_id=1, source_target_pairs={{0,8},{1,33},{2,10},{3,35},{4,12},{5,37},{6,14},{7,39},{8,16},{9,4... | collective-permute-start | bytes 245768 | tf_op jit(solution)/shard_map/ppermute | solution.py:46
  64.2 5.4 %collective-permute-start.18 = (bf16[4,80,128]{2,1,0:T(8,128)(2,1)S(1)}, bf16[4,80,128]{2,1,0:T(8,128)(2,1)S(1)}, u32[]{:S(2)}, u32[]{:S(2)}) collective-permute-start(bf16[4,80,128]{2,1,0:T(8,128)(2,1)S(1)} %get-tuple-element.71), channel_id=1, source_target_pairs={{0,32},{1,9},{2,34},{3,11},{4,36},{5,13},{6,38},{7,15},{8,40},{9,1... | collective-permute-start | bytes 245768 | tf_op jit(solution)/shard_map/ppermute | solution.py:46
  64.6 5.7 %collective-permute-start.19 = (bf16[4,80,128]{2,1,0:T(8,128)(2,1)S(1)}, bf16[4,80,128]{2,1,0:T(8,128)(2,1)S(1)}, u32[]{:S(2)}, u32[]{:S(2)}) collective-permute-start(bf16[4,80,128]{2,1,0:T(8,128)(2,1)S(1)} %get-tuple-element.72), channel_id=1, source_target_pairs={{0,64},{1,17},{2,66},{3,19},{4,68},{5,21},{6,70},{7,23},{8,72},{9,... | collective-permute-start | bytes 245768 | tf_op jit(solution)/shard_map/ppermute | solution.py:46
  80.4 5.4 %collective-permute-start.23 = (bf16[2,128,128]{2,1,0:T(8,128)(2,1)S(1)}, bf16[2,128,128]{2,1,0:T(8,128)(2,1)S(1)}, u32[]{:S(2)}, u32[]{:S(2)}) collective-permute-start(bf16[2,128,128]{2,1,0:T(8,128)(2,1)S(1)} %get-tuple-element.82), channel_id=1, source_target_pairs={{0,4},{1,5},{2,6},{3,7},{4,0},{5,1},{6,2},{7,3},{8,12},{9,13},{10,... | collective-permute-start | bytes 196616 | tf_op jit(solution)/shard_map/ppermute | solution.py:50
  86.9 5.5 %collective-permute-start.27 = (bf16[2,128,128]{2,1,0:T(8,128)(2,1)S(1)}, bf16[2,128,128]{2,1,0:T(8,128)(2,1)S(1)}, u32[]{:S(2)}, u32[]{:S(2)}) collective-permute-start(bf16[2,128,128]{2,1,0:T(8,128)(2,1)S(1)} %shard_map.142.refs_0_), channel_id=1, source_target_pairs={{0,6},{1,7},{2,0},{3,1},{4,2},{5,3},{6,4},{7,5},{8,14},{9,15},{10,... | collective-permute-start | bytes 196616 | tf_op jit(solution)/shard_map/ppermute | solution.py:50
  89.0 8.2 %collective-permute-start.25 = (bf16[2,128,128]{2,1,0:T(8,128)(2,1)S(1)}, bf16[2,128,128]{2,1,0:T(8,128)(2,1)S(1)}, u32[]{:S(2)}, u32[]{:S(2)}) collective-permute-start(bf16[2,128,128]{2,1,0:T(8,128)(2,1)S(1)} %shard_map.142.refs_0_), channel_id=1, source_target_pairs={{0,2},{1,3},{2,4},{3,5},{4,6},{5,7},{6,0},{7,1},{8,10},{9,11},{10,... | collective-permute-start | bytes 196616 | tf_op jit(solution)/shard_map/ppermute | solution.py:50
  89.7 7.9 %collective-permute-start.28 = (bf16[2,128,128]{2,1,0:T(8,128)(2,1)S(1)}, bf16[2,128,128]{2,1,0:T(8,128)(2,1)S(1)}, u32[]{:S(2)}, u32[]{:S(2)}) collective-permute-start(bf16[2,128,128]{2,1,0:T(8,128)(2,1)S(1)} %shard_map.142.refs_0_), channel_id=1, source_target_pairs={{0,1},{1,0},{2,3},{3,2},{4,5},{5,4},{6,7},{7,6},{8,9},{9,8},{10,11... | collective-permute-start | bytes 196616 | tf_op jit(solution)/shard_map/ppermute | solution.py:54
  92.3 5.2 %collective-permute-start.31 = (bf16[2,128,128]{2,1,0:T(8,128)(2,1)S(1)}, bf16[2,128,128]{2,1,0:T(8,128)(2,1)S(1)}, u32[]{:S(2)}, u32[]{:S(2)}) collective-permute-start(bf16[2,128,128]{2,1,0:T(8,128)(2,1)S(1)} %collective-permute-done.27.refs_3_), channel_id=1, source_target_pairs={{0,1},{1,0},{2,3},{3,2},{4,5},{5,4},{6,7},{7,6},{8,9},{9,8},{10,11... | collective-permute-start | bytes 196616 | tf_op jit(solution)/shard_map/ppermute | solution.py:54
  (22 other events, 301.8 us)

commit v3 on v2

--- a/solution.py
+++ b/solution.py
@@ -17,6 +17,7 @@
 MSG = 80
 EPS = 1e-06
 NEG = -1e30
+CONTRACT = (((1,), (1,)), ((), ()))
 HINT = 1 << 34
 SCALE = HD ** (-0.5)
 LOG2E = 1.4426950408889634
@@ -46,6 +47,19 @@
     return lax.ppermute(value, AXES, ring(first, step))
 
 
+def shift_pair(value, across):
+    pairs = []
+    for z in range(4):
+        for y in range(4):
+            for x in range(4):
+                for core in range(2):
+                    b = y if core else z
+                    to = 3 - b if across else b ^ 1
+                    target = device(z, to, x, core) if core else device(to, y, x, core)
+                    pairs.append((device(z, y, x, core), target))
+    return lax.ppermute(value, AXES, pairs)
+
+
 def shift_x(value, step):
     return lax.ppermute(value, "narrow", [(n, (n + 2 * step) % 8) for n in range(8)])
 
@@ -54,15 +68,16 @@
     return lax.ppermute(value, "narrow", [(n, n ^ 1) for n in range(8)])
 
 
-def call(kernel, out_shape, args, smem=(), smem_out=(), scratch=(), cost=None):
-    def spec(is_scalar):
-        return pl.BlockSpec(memory_space=SMEM if is_scalar else pltpu.VMEM)
-
-    specs = [spec(i in smem) for i in range(len(args))]
+def call(kernel, out_shape, args, smem=(), smem_out=(), hbm=(), hbm_out=False, scratch=(), cost=None):
+    def spec(is_scalar, is_far):
+        space = SMEM if is_scalar else pltpu.HBM if is_far else pltpu.VMEM
+        return pl.BlockSpec(memory_space=space)
+
+    specs = [spec(i in smem, i in hbm) for i in range(len(args))]
     if isinstance(out_shape, (tuple, list)):
-        outs = [spec(i in smem_out) for i in range(len(out_shape))]
+        outs = [spec(i in smem_out, False) for i in range(len(out_shape))]
     else:
-        outs = spec(False)
+        outs = spec(False, hbm_out)
     flops, nbytes = cost or (1 << 20, 1 << 20)
     return pl.pallas_call(
         kernel,
@@ -118,17 +133,34 @@
         out[block] = (part * gain[:, block * HD : (block + 1) * HD]).astype(BF16)
 
 
+def mix_kernel(w_qkv, w_out, out, sems):
+    copies = [
+        pltpu.make_async_copy(w_qkv, out.at[:, : 4 * HD], sems.at[0]),
+        pltpu.make_async_copy(w_out.at[:HD], out.at[:, 4 * HD : 5 * HD], sems.at[1]),
+        pltpu.make_async_copy(w_out.at[HD:], out.at[:, 5 * HD :], sems.at[2]),
+    ]
+    for copy in copies:
+        copy.start()
+    for copy in copies:
+        copy.wait()
+
+
 def pack_kernel(w0, w1, w2, w3, first, second):
     for d, ref in enumerate((w0, w1, w2, w3)):
         first[d] = ref[:, : 2 * HD]
         second[d] = ref[:, 2 * HD :]
 
 
-def project(ids, normed, refs):
+def around(b, pairs):
+    if pairs:
+        return [b, b + 1 - 2 * lax.rem(b, 2), 3 - b, 2 - b + 2 * lax.rem(b, 2)]
+    return [lax.rem(b - e + 4, 4) for e in range(4)]
+
+
+def project(ids, normed, refs, pairs):
     a, b, core = ids[0], ids[1], ids[2]
     total = jnp.zeros((ROWS, 2 * HD), F32)
-    for e in range(4):
-        at_b = lax.rem(b - e + 4, 4)
+    for e, at_b in enumerate(around(b, pairs)):
         left = []
         for d in range(4):
             at_a = lax.rem(a - d + 4, 4)
@@ -147,7 +179,7 @@
 
 
 def query_kernel(ids, normed, w0, w1, w2, w3, gain, cosine, sine, out):
-    total = project(ids, normed, (w0, w1, w2, w3))
+    total = project(ids, normed, (w0, w1, w2, w3), False)
     for h in range(2):
         head = head_norm(total[:, h * HD : (h + 1) * HD], gain[...], cosine[...], sine[...])
         head = head.astype(BF16)
@@ -155,10 +187,33 @@
             out[j, h * PER : (h + 1) * PER] = head[j * PER : (j + 1) * PER]
 
 
-def pair_kernel(ids, normed, w0, w1, w2, w3, gain, cosine, sine, out):
-    total = project(ids, normed, (w0, w1, w2, w3))
-    out[0] = head_norm(total[:, :HD], gain[...], cosine[...], sine[...]).astype(BF16)
-    out[1] = total[:, HD:].astype(BF16)
+def own_kernel(
+    ids, normed, w0, w1, w2, w3, gain, cosine, sine, queries, acc_0, high_0, acc_1, high_1,
+    new_cache, out, lse,
+):
+    total = project(ids, normed, (w0, w1, w2, w3), True)
+    keys = head_norm(total[:, :HD], gain[...], cosine[...], sine[...]).astype(BF16)
+    values = total[:, HD:].astype(BF16)
+    new_cache[0] = keys
+    new_cache[1] = values
+    i = lax.broadcasted_iota(jnp.int32, (2 * HD, ROWS), 0)
+    key = lax.broadcasted_iota(jnp.int32, (2 * HD, ROWS), 1)
+    row = i // 64 * PER + lax.rem(i, PER)
+    visible = (row // 2 == key // 2) & (key <= row)
+    score = lax.dot_general(
+        queries[...].reshape(2 * HD, HD), keys, CONTRACT, preferred_element_type=F32
+    )
+    score = jnp.where(visible, score, NEG)
+    acc = jnp.concatenate([acc_0[...], acc_1[...]], axis=0)
+    stats = jnp.concatenate([high_0[...], high_1[...]], axis=0)
+    before, sums = stats[:, 0:1], stats[:, 64:65]
+    high = jnp.maximum(before, jnp.max(score, axis=1, keepdims=True))
+    scale = jnp.exp2((before - high) * (SCALE * LOG2E))
+    weight = jnp.exp2((score - high) * (SCALE * LOG2E))
+    sums = sums * scale + jnp.sum(weight, axis=1, keepdims=True)
+    acc = acc * scale + jnp.dot(weight.astype(BF16), values, preferred_element_type=F32)
+    out[...] = acc / sums
+    lse[...] = jnp.broadcast_to(high * SCALE + jnp.log(sums), (2 * HD, HD))
 
 
 def route_kernel(base, index, x0, x1, x2, x3, o0, o1, o2, o3, held):
@@ -176,18 +231,12 @@
     return jnp.sum(jnp.where(lane == row, spread, 0.0), axis=1, keepdims=True)
 
 
-def tail_kernel(start, lens, queries, new_cache, cache, out, lse):
+def tail_kernel(start, lens, queries, cache, out, stats):
     conts = 8
     row = lax.broadcasted_iota(jnp.int32, (32, TLEN), 0)
     lane = lax.broadcasted_iota(jnp.int32, (32, TLEN), 1)
     owner = lax.rem(row, 16) // 2
-    small_row = lax.broadcasted_iota(jnp.int32, (32, 16), 0)
-    small_col = lax.broadcasted_iota(jnp.int32, (32, 16), 1)
-    visible = (lax.rem(small_row, 16) // 2 == small_col // 2) & (
-        lax.rem(small_col, 2) <= lax.rem(small_row, 2)
-    )
-    owner_out = lax.rem(lax.broadcasted_iota(jnp.int32, (32, HD), 0), 16) // 2
-    contract = (((1,), (1,)), ((), ()))
+    owner_out = owner[:, :HD]
     for g in range(start, start + 4):
         j, half = g // 2, (g % 2) * 16
         q = jnp.concatenate(
@@ -196,38 +245,25 @@
         score = jnp.zeros((32, TLEN), F32)
         length = jnp.zeros((32, TLEN), jnp.int32)
         for i in range(conts):
-            part = lax.dot_general(q, cache[0, g * conts + i], contract, preferred_element_type=F32)
+            part = lax.dot_general(
+                q, cache[0, g * conts + i], CONTRACT, preferred_element_type=F32
+            )
             score = jnp.where(owner == i, part, score)
             length = jnp.where(owner == i, lens[g * conts + i], length)
         score = jnp.where(lane < length, score, NEG)
-        fresh = lax.dot_general(
-            q, new_cache[0, g * 16 : g * 16 + 16], contract, preferred_element_type=F32
-        )
-        fresh = jnp.where(visible, fresh, NEG)
-        high = jnp.maximum(
-            jnp.max(score, axis=1, keepdims=True), jnp.max(fresh, axis=1, keepdims=True)
-        )
+        high = jnp.max(score, axis=1, keepdims=True)
         weight = jnp.exp2((score - high) * (SCALE * LOG2E))
-        fresh_weight = jnp.exp2((fresh - high) * (SCALE * LOG2E))
-        sums = jnp.sum(weight, axis=1, keepdims=True) + jnp.sum(
-            fresh_weight, axis=1, keepdims=True
-        )
+        sums = jnp.sum(weight, axis=1, keepdims=True)
         weight = weight.astype(BF16)
         acc = jnp.zeros((32, HD), F32)
         for i in range(conts):
             part = jnp.dot(weight, cache[1, g * conts + i], preferred_element_type=F32)
             acc = jnp.where(owner_out == i, part, acc)
-        acc = acc + jnp.dot(
-            fresh_weight.astype(BF16),
-            new_cache[1, g * 16 : g * 16 + 16],
-            preferred_element_type=F32,
-        )
-        acc = acc / sums
-        logs = jnp.broadcast_to(high * SCALE + jnp.log(sums), (32, HD))
+        both = jnp.where(lane[:, :HD] < 64, high, sums)
         for h in range(2):
-            at = (g - start) * 16
-            out[h, at : at + 16] = acc[h * 16 : h * 16 + 16]
-            lse[h, at : at + 16] = logs[h * 16 : h * 16 + 16]
+            at = (g - start) // 2 * 64 + h * PER + half
+            out[at : at + 16] = acc[h * 16 : h * 16 + 16]
+            stats[at : at + 16] = both[h * 16 : h * 16 + 16]
 
 
 def prefix_kernel(table, r0, r1, r2, r3, cache, out, held, scores):
@@ -237,13 +273,12 @@
     for e, ref in enumerate((r0, r1, r2, r3)):
         held[e] = ref[...]
     lane = lax.broadcasted_iota(jnp.int32, (64, KB), 1)
-    contract = (((1,), (1,)), ((), ()))
     for s in range(4):
         q = held[select[s], s]
 
         def first(i, high):
             block = cache[0, s, pl.ds(pl.multiple_of(i * KB, KB), KB)]
-            part = lax.dot_general(q, block, contract, preferred_element_type=F32)
+            part = lax.dot_general(q, block, CONTRACT, preferred_element_type=F32)
             part = jnp.where(lane < lens[s] - i * KB, part, NEG)
             scores[i] = part
             for c in range(KB // HD):
@@ -281,8 +316,8 @@
 
 
 def finish_kernel(
-    ids, table, c0, c1, c2, c3, out_0, lse_0, out_1, lse_1, w0, w1, w2, w3,
-    scores, keep, send, held, attention,
+    ids, table, c0, c1, c2, c3, tail_out, tail_lse, w0, w1, w2, w3,
+    scores, keep, send, held, attention, products,
 ):
     for e, ref in enumerate((c0, c1, c2, c3)):
         held[e] = ref[...]
@@ -294,16 +329,15 @@
         logs = column(line, 64)
         for h in range(2):
             rows = slice(j * PER, (j + 1) * PER)
-            near_rows = slice((j % 2) * PER, (j % 2 + 1) * PER)
-            tail_out, tail_lse = ((out_0, lse_0), (out_1, lse_1))[j // 2]
+            own = slice(j * 64 + h * PER, j * 64 + (h + 1) * PER)
             prefix_out = message[h * PER : (h + 1) * PER].astype(F32)
             prefix_lse = logs[h * PER : (h + 1) * PER]
-            own_lse = tail_lse[h, near_rows][:, 0:1]
+            own_lse = tail_lse[own][:, 0:1]
             high = jnp.maximum(prefix_lse, own_lse)
             share_a = jnp.exp(prefix_lse - high)
             share_b = jnp.exp(own_lse - high)
             both = share_a + share_b
-            merged = (share_a * prefix_out + share_b * tail_out[h, near_rows]) / both
+            merged = (share_a * prefix_out + share_b * tail_out[own]) / both
             attention[rows, h * HD : (h + 1) * HD] = merged.astype(BF16)
             totals[h].append(jnp.broadcast_to(high + jnp.log(both), (PER, HD)))
     diagonal = lax.broadcasted_iota(jnp.int32, (ROWS, HD), 0) == lax.broadcasted_iota(
@@ -314,7 +348,7 @@
         scores[h : h + 1] = jnp.sum(jnp.where(diagonal, total, 0.0), axis=0, keepdims=True)
     a, b, core, x = ids[0], ids[1], ids[2], ids[3]
     left = attention[...]
-    for e, ref in enumerate((w0, w1, w2, w3)):
+    for ref, at_b in zip((w0, w1, w2, w3), around(b, True)):
         for d in (0, 2):
             right = jnp.concatenate(
                 [
@@ -325,20 +359,13 @@
             )
             both = jnp.dot(left, right, preferred_element_type=F32)
             for i in range(2):
-                product = both[:, i * HD : (i + 1) * HD]
-                at_a, at_b = lax.rem(a - d - i + 4, 4), lax.rem(b - e + 4, 4)
+                at_a = lax.rem(a - d - i + 4, 4)
                 block = jnp.where(core == 0, 4 * at_b + at_a, 4 * at_a + at_b)
-                mine = (block // 8) == core
-                pair = lax.rem(block, 8) // 2
-                side = lax.rem(block, 2)
-
-                @pl.when(mine)
-                def _():
-                    keep[lax.rem(pair - x + 4, 4), side] = product
-
-                @pl.when(jnp.logical_not(mine))
-                def _():
-                    send[pair, side] = product.astype(BF16)
+                products[block] = both[:, i * HD : (i + 1) * HD]
+    for pair in range(4):
+        for side in range(2):
+            keep[lax.rem(pair - x + 4, 4), side] = products[core * 8 + pair * 2 + side]
+            send[pair, side] = products[(1 - core) * 8 + pair * 2 + side].astype(BF16)
 
 
 def first_sum_kernel(ids, keep, got, o0, o1, o2, o3):
@@ -362,13 +389,22 @@
 
 
 def gather_kernel(ids, *refs):
-    mine, other, out = refs[:4], refs[4:8], refs[8]
+    mine, other, out, sems = refs[:4], refs[4:8], refs[8], refs[9]
     core, x = ids[2], ids[3]
+    copies = []
     for d in range(4):
         for side in range(2):
             at = lax.rem(x - d + 4, 4) * 2 + side
-            out[:, pl.ds(pl.multiple_of((core * 8 + at) * HD, HD), HD)] = mine[d][side]
-            out[:, pl.ds(pl.multiple_of(((1 - core) * 8 + at) * HD, HD), HD)] = other[d][side]
+            for pieces, half in ((mine, core), (other, 1 - core)):
+                columns = pl.ds(pl.multiple_of((half * 8 + at) * HD, HD), HD)
+                copies.append(
+                    pltpu.make_async_copy(
+                        pieces[d].at[side], out.at[:, columns], sems.at[len(copies)]
+                    )
+                )
+                copies[-1].start()
+    for copy in copies:
+        copy.wait()
 
 
 def split(wide, core):
@@ -416,7 +452,13 @@
     sine = jnp.sin(angles) * jnp.where(channel < HD // 2, -1.0, 1.0)[None, :]
     q_gain, k_gain = q_gain.reshape(1, HD), k_gain.reshape(1, HD)
 
-    mixed = jnp.concatenate([w_qkv, w_out[:HD], w_out[HD:]], axis=1)
+    mixed = call(
+        mix_kernel,
+        struct((ROWS, 6 * HD), BF16),
+        [w_qkv, w_out],
+        hbm=(0, 1),
+        scratch=[pltpu.SemaphoreType.DMA((3,))],
+    )
     near = gather_ring(mixed, True)
     normed = call(
         norm_kernel,
@@ -429,7 +471,8 @@
         pack_kernel, [struct((4, ROWS, 2 * HD), BF16), struct((4, ROWS, 4 * HD), BF16)], near
     )
     far_query = gather_ring(near_query, False)
-    far_other = gather_ring(near_other, False)
+    beside = shift_pair(near_other, False)
+    far_other = [near_other, beside, shift_pair(near_other, True), shift_pair(beside, True)]
     queries = call(
         query_kernel,
         struct((4, 64, HD), BF16),
@@ -439,26 +482,20 @@
     )
 
     held = gather_ring(queries, True)
-    asked = choose(held, table, 0, 64)
-    new_cache = call(
-        pair_kernel,
-        struct((2, ROWS, HD), BF16),
-        [ids, normed] + far_other + [k_gain, cosine, sine],
-        smem=(0,),
-        cost=(2 * ROWS * 256 * 2048, 2 << 20),
-    )
     tails = []
     for start in (0, 4):
         tails.append(
             call(
                 functools.partial(tail_kernel, start),
-                [struct((2, 64, HD), F32), struct((2, 64, HD), F32)],
-                [tail_lens, queries, new_cache, tail_cache],
+                [struct((HD, HD), F32)] * 2,
+                [tail_lens, queries, tail_cache],
                 smem=(0,),
                 cost=(2 * 64 * 32 * TLEN * HD, 4 << 20),
             )
         )
-    asked, tails[0] = lax.optimization_barrier((asked, tails[0]))
+    held, tails[0] = lax.optimization_barrier((held, tails[0]))
+    asked = choose(held, table, 0, 64)
+    asked, tails[1] = lax.optimization_barrier((asked, tails[1]))
     results = call(
         prefix_kernel,
         struct((4, MSG, HD), BF16),
@@ -468,7 +505,14 @@
         cost=(2 * 2 * 4 * 64 * PLEN * HD, 8 << 20),
     )
     held = gather_ring(results, True)
-    held, tails[1] = lax.optimization_barrier((held, tails[1]))
+    new_cache, tail_out, tail_lse = call(
+        own_kernel,
+        [struct((2, ROWS, HD), BF16)] + [struct((2 * HD, HD), F32)] * 2,
+        [ids, normed] + far_other + [k_gain, cosine, sine, queries, *tails[0], *tails[1]],
+        smem=(0,),
+        cost=(2 * ROWS * 256 * 2048, 3 << 20),
+    )
+    held, tail_out = lax.optimization_barrier((held, tail_out))
     homes = choose(held, table, 24, MSG)
 
     scores, keep, send = call(
@@ -478,9 +522,11 @@
             struct((4, 2, ROWS, HD), F32),
             struct((4, 2, ROWS, HD), BF16),
         ],
-        [ids, table] + homes + [*tails[0], *tails[1]] + far_other,
+        [ids, table] + homes + [tail_out, tail_lse] + far_other,
         smem=(0, 1),
-        scratch=[pltpu.VMEM((4, 4, MSG, HD), BF16), pltpu.VMEM((ROWS, 2 * HD), BF16)],
+        scratch=[pltpu.VMEM((4, 4, MSG, HD), BF16), pltpu.VMEM((ROWS, 2 * HD), BF16),
+            pltpu.VMEM((16, ROWS, HD), F32),
+        ],
         cost=(2 * ROWS * 256 * 2048, 3 << 20),
     )
     got = swap_core(send)
@@ -495,7 +541,9 @@
     mine = call(second_sum_kernel, block, [ids, sums[0]] + moved + [hidden_in], smem=(0,))
     ours = [mine] + [shift_x(mine, step) for step in (1, 2, 3)]
     theirs = [swap_core(piece) for piece in ours]
-    hidden_out = call(gather_kernel, struct((ROWS, 2048), BF16), [ids] + ours + theirs, smem=(0,))
+    hidden_out = call(gather_kernel, struct((ROWS, 2048), BF16), [ids] + ours + theirs, smem=(0,), hbm_out=True,
+        scratch=[pltpu.SemaphoreType.DMA((16,))],
+    )
     return (hidden_out, scores.T, new_cache)
 
 

time: 101 us -> 96.2 us (0.952)
  waiting for transfers between devices: 29.3 us -> 16.6 us
  starting transfers between devices: 44.3 us -> 55.5 us
  Pallas kernels: 19.7 us -> 18 us
    ppermute x21 -> x18, waiting for transfers between devices: 24.9 us -> 9.8 us  [shift(): return lax.ppermute(value, AXES, ring(first, step))]
    ppermute x5, starting transfers between devices: 11.1 us -> 15.8 us  [swap_core(): return lax.ppermute(value, 'narrow', [(n, n ^ 1) for n in range(8)])]
    ppermute x0 -> x3, starting transfers between devices: none -> 3.77 us  [shift_pair(): return lax.ppermute(value, AXES, pairs)]
    ppermute x0 -> x3, waiting for transfers between devices: none -> 2.5 us  [shift_pair(): return lax.ppermute(value, AXES, pairs)]
    ppermute x21 -> x18, starting transfers between devices: 25.5 us -> 27.3 us  [shift(): return lax.ppermute(value, AXES, ring(first, step))]
    pallas_call x14 -> x15, Pallas kernels: 19.7 us -> 18 us  [call(): pl.pallas_call(kernel, out_shape=out_shape, in_specs=specs, out_specs=out...]
  transfers between devices with their start and end apart: 32 -> 32, of which waited for: 15 -> 12; matrix products, arithmetic and copies ran while one was open for 0% -> 0% of each run, Pallas kernels for 10% -> 14%
where the time goes in v3:
time: 96.2 us; the launch traced here: 95.6 us
  starting transfers between devices  55.5 us (58%)
  Pallas kernels  18 us (19%)
  waiting for transfers between devices  16.6 us (17%)
  local copies, waits for them, and re-layouts  4.21 us (4%)
  between operations  1.01 us (1%)
    ppermute x18, starting transfers between devices, shift(): return lax.ppermute(value, AXES, ring(first, step))  27.3 us
    pallas_call x15, Pallas kernels, call(): pl.pallas_call(kernel, out_shape=out_shape, in_specs=specs, out_specs=out...  18 us
    ppermute x5, starting transfers between devices, swap_core(): return lax.ppermute(value, 'narrow', [(n, n ^ 1) for n in range(8)])  15.8 us
    ppermute x18, waiting for transfers between devices, shift(): return lax.ppermute(value, AXES, ring(first, step))  9.8 us
    ppermute x6, starting transfers between devices, shift_x(): lax.ppermute(value, 'narrow', [(n, (n + 2 * step) % 8) for n in range(8)])  8.59 us
    unnamed x28, local copies, waits for them, and re-layouts  4.21 us
    ppermute x3, starting transfers between devices, shift_pair(): return lax.ppermute(value, AXES, pairs)  3.77 us
    ppermute x3, waiting for transfers between devices, shift_pair(): return lax.ppermute(value, AXES, pairs)  2.5 us
  transfers between devices with their start and end apart: 32, of which 12 were waited for; matrix products, arithmetic and copies ran while one was open for 0% of the time, Pallas kernels for 14%

profile of v3, /device:TPU:1, one launch (start us, length us, event | category | flops | bytes accessed | tf_op | source)
XLA Modules:
  0.0 95.6 jit_solution(11702389549919074549)
XLA Ops:
  2.4 2.5 %collective-permute-start = (bf16[128,768]{1,0:T(8,128)(2,1)S(1)}, bf16[128,768]{1,0:T(8,128)(2,1)S(1)}, u32[]{:S(2)}, u32[]{:S(2)}) collective-permute-start(bf16[128,768]{1,0:T(8,128)(2,1)S(1)} %shard_map.130.w0), channel_id=1, source_target_pairs={{0,8},{1,33},{2,10},{3,35},{4,12},{5,37},{6,14},{7,39},{8,16},{9,4... | collective-permute-start | bytes 589832 | tf_op jit(solution)/shard_map/ppermute | solution.py:47
  5.0 3.3 %collective-permute-start.1 = (bf16[128,768]{1,0:T(8,128)(2,1)S(1)}, bf16[128,768]{1,0:T(8,128)(2,1)S(1)}, u32[]{:S(2)}, u32[]{:S(2)}) collective-permute-start(bf16[128,768]{1,0:T(8,128)(2,1)S(1)} %shard_map.130.w0), channel_id=1, source_target_pairs={{0,16},{1,65},{2,18},{3,67},{4,20},{5,69},{6,22},{7,71},{8,24},{9,... | collective-permute-start | bytes 589832 | tf_op jit(solution)/shard_map/ppermute | solution.py:47
  11.8 1.7 %shard_map.132 = (s32[64]{0:T(128)S(1)}, f32[128,128]{1,0:T(8,128)S(1)}) custom-call(s32[4]{0:T(128)S(1)} %pad_add_fusion.ids, s32[64]{0:T(128)S(1)} %copy-done.8, s32[64]{0:T(128)S(1)} %copy-done.9, s32[64]{0:T(128)S(1)} %copy-done.4, f32[1,128]{1,0:T(1,128)S(1)} %fusion.2.freq), custom_call_target="tpu_custom_call" | custom-call | flops 1048576 | bytes 1048576 | tf_op jit(solution)/shard_map/pallas_call | solution.py:82
  15.3 2.7 %collective-permute-start.4 = (bf16[4,128,256]{2,1,0:T(8,128)(2,1)S(1)}, bf16[4,128,256]{2,1,0:T(8,128)(2,1)S(1)}, u32[]{:S(2)}, u32[]{:S(2)}) collective-permute-start(bf16[4,128,256]{2,1,0:T(8,128)(2,1)S(1)} %get-tuple-element.59.w0), channel_id=1, source_target_pairs={{0,64},{1,17},{2,66},{3,19},{4,68},{5,21},{6,70},{7,23},{8,72},{9,... | collective-permute-start | bytes 786440 | tf_op jit(solution)/shard_map/ppermute | solution.py:47
  18.1 1.6 %collective-permute-start.5 = (bf16[4,128,256]{2,1,0:T(8,128)(2,1)S(1)}, bf16[4,128,256]{2,1,0:T(8,128)(2,1)S(1)}, u32[]{:S(2)}, u32[]{:S(2)}) collective-permute-start(bf16[4,128,256]{2,1,0:T(8,128)(2,1)S(1)} %get-tuple-element.59.w0), channel_id=1, source_target_pairs={{0,96},{1,25},{2,98},{3,27},{4,100},{5,29},{6,102},{7,31},{8,104},... | collective-permute-start | bytes 786440 | tf_op jit(solution)/shard_map/ppermute | solution.py:47
  19.7 2.5 %collective-permute-done.15.w1 = bf16[4,128,512]{2,1,0:T(8,128)(2,1)S(1)} collective-permute-done((bf16[4,128,512]{2,1,0:T(8,128)(2,1)S(1)}, bf16[4,128,512]{2,1,0:T(8,128)(2,1)S(1)}, u32[]{:S(2)}, u32[]{:S(2)}) %collective-permute-start.15) | collective-permute-done | bytes 524320 | tf_op jit(solution)/shard_map/ppermute | solution.py:60
  22.2 2.5 %collective-permute-start.17 = (bf16[4,128,512]{2,1,0:T(8,128)(2,1)S(1)}, bf16[4,128,512]{2,1,0:T(8,128)(2,1)S(1)}, u32[]{:S(2)}, u32[]{:S(2)}) collective-permute-start(bf16[4,128,512]{2,1,0:T(8,128)(2,1)S(1)} %collective-permute-done.15.w1), channel_id=1, source_target_pairs={{0,96},{1,25},{2,98},{3,27},{4,100},{5,29},{6,102},{7,31},{8,104},... | collective-permute-start | bytes 1572872 | tf_op jit(solution)/shard_map/ppermute | solution.py:60
  25.0 5.1 %collective-permute-done.4.w2 = bf16[4,128,256]{2,1,0:T(8,128)(2,1)S(1)} collective-permute-done((bf16[4,128,256]{2,1,0:T(8,128)(2,1)S(1)}, bf16[4,128,256]{2,1,0:T(8,128)(2,1)S(1)}, u32[]{:S(2)}, u32[]{:S(2)}) %collective-permute-start.4) | collective-permute-done | bytes 262176 | tf_op jit(solution)/shard_map/ppermute | solution.py:47
  32.1 2.1 %collective-permute-start.7 = (bf16[4,64,128]{2,1,0:T(8,128)(2,1)S(1)}, bf16[4,64,128]{2,1,0:T(8,128)(2,1)S(1)}, u32[]{:S(2)}, u32[]{:S(2)}) collective-permute-start(bf16[4,64,128]{2,1,0:T(8,128)(2,1)S(1)} %shard_map.134.queries.x0), channel_id=1, source_target_pairs={{0,16},{1,65},{2,18},{3,67},{4,20},{5,69},{6,22},{7,71},{8,24},{9,... | collective-permute-start | bytes 196616 | tf_op jit(solution)/shard_map/ppermute | solution.py:47
  35.2 2.4 %shard_map.135 = (f32[128,128]{1,0:T(8,128)S(1)}, f32[128,128]{1,0:T(8,128)S(1)}) custom-call(s32[64]{0:T(128)S(1)} %copy-done.4, bf16[4,64,128]{2,1,0:T(8,128)(2,1)S(1)} %shard_map.134.queries.x0, bf16[2,64,256,128]{3,2,1,0:T(8,128)(2,1)S(1)} %bitcast.9), custom_call_target="tpu_custom_call" | custom-call | flops 134217728 | bytes 4194304 | tf_op jit(solution)/shard_map/pallas_call | solution.py:82
  40.5 2.4 %shard_map.137 = (f32[128,128]{1,0:T(8,128)S(1)}, f32[128,128]{1,0:T(8,128)S(1)}) custom-call(s32[64]{0:T(128)S(1)} %copy-done.4, bf16[4,64,128]{2,1,0:T(8,128)(2,1)S(1)} %shard_map.134.queries.x0, bf16[2,64,256,128]{3,2,1,0:T(8,128)(2,1)S(1)} %bitcast.9), custom_call_target="tpu_custom_call" | custom-call | flops 134217728 | bytes 4194304 | tf_op jit(solution)/shard_map/pallas_call | solution.py:82
  43.7 2.9 %shard_map.138.x0 = bf16[4,80,128]{2,1,0:T(8,128)(2,1)S(1)} custom-call(s32[64]{0:T(128)S(1)} %get-tuple-element.53.index.table, bf16[4,64,128]{2,1,0:T(8,128)(2,1)S(1)} %get-tuple-element.73.r0, bf16[4,64,128]{2,1,0:T(8,128)(2,1)S(1)} %collective-permute-done.9.r1, bf16[4,64,128]{2,1,0:T(8,128)(2,1)S(1)} %collective-permute-done.10.r2, ...), custom_call_target="tpu_custom_call" | custom-call | flops 536870912 | bytes 8388608 | tf_op jit(solution)/shard_map/pallas_call | solution.py:82
  46.6 1.7 %collective-permute-start.12 = (bf16[4,80,128]{2,1,0:T(8,128)(2,1)S(1)}, bf16[4,80,128]{2,1,0:T(8,128)(2,1)S(1)}, u32[]{:S(2)}, u32[]{:S(2)}) collective-permute-start(bf16[4,80,128]{2,1,0:T(8,128)(2,1)S(1)} %shard_map.138.x0), channel_id=1, source_target_pairs={{0,8},{1,33},{2,10},{3,35},{4,12},{5,37},{6,14},{7,39},{8,16},{9,4... | collective-permute-start | bytes 245768 | tf_op jit(solution)/shard_map/ppermute | solution.py:47
  48.3 3.2 %collective-permute-start.13 = (bf16[4,80,128]{2,1,0:T(8,128)(2,1)S(1)}, bf16[4,80,128]{2,1,0:T(8,128)(2,1)S(1)}, u32[]{:S(2)}, u32[]{:S(2)}) collective-permute-start(bf16[4,80,128]{2,1,0:T(8,128)(2,1)S(1)} %shard_map.138.x0), channel_id=1, source_target_pairs={{0,16},{1,65},{2,18},{3,67},{4,20},{5,69},{6,22},{7,71},{8,24},{9,... | collective-permute-start | bytes 245768 | tf_op jit(solution)/shard_map/ppermute | solution.py:47
  52.7 1.7 %shard_map.139 = (bf16[2,128,128]{2,1,0:T(8,128)(2,1)}, f32[256,128]{1,0:T(8,128)S(1)}, f32[256,128]{1,0:T(8,128)S(1)}) custom-call(s32[4]{0:T(128)S(1)} %pad_add_fusion.ids, bf16[16,128,128]{2,1,0:T(8,128)(2,1)S(1)} %shard_map.131.normed, bf16[4,128,512]{2,1,0:T(8,128)(2,1)S(1)} %get-tuple-element.77.w0, ...), custom_call_target="tpu_custom_call" | custom-call | flops 134217728 | bytes 3145728 | tf_op jit(solution)/shard_map/pallas_call | solution.py:82
  55.8 3.0 %collective-permute-start.19 = (bf16[4,80,128]{2,1,0:T(8,128)(2,1)S(1)}, bf16[4,80,128]{2,1,0:T(8,128)(2,1)S(1)}, u32[]{:S(2)}, u32[]{:S(2)}) collective-permute-start(bf16[4,80,128]{2,1,0:T(8,128)(2,1)S(1)} %get-tuple-element.89), channel_id=1, source_target_pairs={{0,64},{1,17},{2,66},{3,19},{4,68},{5,21},{6,70},{7,23},{8,72},{9,... | collective-permute-start | bytes 245768 | tf_op jit(solution)/shard_map/ppermute | solution.py:47
  60.3 2.2 %collective-permute-done.19.c2 = bf16[4,80,128]{2,1,0:T(8,128)(2,1)S(1)} collective-permute-done((bf16[4,80,128]{2,1,0:T(8,128)(2,1)S(1)}, bf16[4,80,128]{2,1,0:T(8,128)(2,1)S(1)}, u32[]{:S(2)}, u32[]{:S(2)}) %collective-permute-start.19) | collective-permute-done | bytes 81952 | tf_op jit(solution)/shard_map/ppermute | solution.py:47
  62.4 1.6 %shard_map.141 = (f32[2,128]{1,0:T(2,128)}, f32[4,2,128,128]{3,2,1,0:T(8,128)S(1)}, bf16[4,2,128,128]{3,2,1,0:T(8,128)(2,1)S(1)}) custom-call(s32[4]{0:T(128)S(1)} %pad_add_fusion.ids, s32[64]{0:T(128)S(1)} %get-tuple-element.53.index.table, bf16[4,80,128]{2,1,0:T(8,128)(2,1)S(1)} %get-tuple-element.87.c0, ...), custom_call_target="tpu_custom_call" | custom-call | flops 134217728 | bytes 3145728 | tf_op jit(solution)/shard_map/pallas_call | solution.py:82
  64.0 9.3 %collective-permute-start.21 = (bf16[4,2,128,128]{3,2,1,0:T(8,128)(2,1)S(1)}, bf16[4,2,128,128]{3,2,1,0:T(8,128)(2,1)S(1)}, u32[]{:S(2)}, u32[]{:S(2)}) collective-permute-start(bf16[4,2,128,128]{3,2,1,0:T(8,128)(2,1)S(1)} %get-tuple-element.94), channel_id=1, source_target_pairs={{0,1},{1,0},{2,3},{3,2},{4,5},{5,4},{6,7},{7,6},{8,9},{9,8},{10,11... | collective-permute-start | bytes 786440 | tf_op jit(solution)/shard_map/ppermute | solution.py:68
  76.4 2.4 %collective-permute-start.23 = (bf16[2,128,128]{2,1,0:T(8,128)(2,1)S(1)}, bf16[2,128,128]{2,1,0:T(8,128)(2,1)S(1)}, u32[]{:S(2)}, u32[]{:S(2)}) collective-permute-start(bf16[2,128,128]{2,1,0:T(8,128)(2,1)S(1)} %get-tuple-element.97), channel_id=1, source_target_pairs={{0,4},{1,5},{2,6},{3,7},{4,0},{5,1},{6,2},{7,3},{8,12},{9,13},{10,... | collective-permute-start | bytes 196616 | tf_op jit(solution)/shard_map/ppermute | solution.py:64
  80.0 1.8 %collective-permute-done.23.g2 = bf16[2,128,128]{2,1,0:T(8,128)(2,1)S(1)} collective-permute-done((bf16[2,128,128]{2,1,0:T(8,128)(2,1)S(1)}, bf16[2,128,128]{2,1,0:T(8,128)(2,1)S(1)}, u32[]{:S(2)}, u32[]{:S(2)}) %collective-permute-start.23) | collective-permute-done | bytes 65568 | tf_op jit(solution)/shard_map/ppermute | solution.py:64
  83.0 3.2 %collective-permute-start.26 = (bf16[2,128,128]{2,1,0:T(8,128)(2,1)S(1)}, bf16[2,128,128]{2,1,0:T(8,128)(2,1)S(1)}, u32[]{:S(2)}, u32[]{:S(2)}) collective-permute-start(bf16[2,128,128]{2,1,0:T(8,128)(2,1)S(1)} %shard_map.143.refs_0_), channel_id=1, source_target_pairs={{0,4},{1,5},{2,6},{3,7},{4,0},{5,1},{6,2},{7,3},{8,12},{9,13},{10,... | collective-permute-start | bytes 196616 | tf_op jit(solution)/shard_map/ppermute | solution.py:64
  86.6 2.7 %collective-permute-start.28 = (bf16[2,128,128]{2,1,0:T(8,128)(2,1)S(1)}, bf16[2,128,128]{2,1,0:T(8,128)(2,1)S(1)}, u32[]{:S(2)}, u32[]{:S(2)}) collective-permute-start(bf16[2,128,128]{2,1,0:T(8,128)(2,1)S(1)} %shard_map.143.refs_0_), channel_id=1, source_target_pairs={{0,1},{1,0},{2,3},{3,2},{4,5},{5,4},{6,7},{7,6},{8,9},{9,8},{10,11... | collective-permute-start | bytes 196616 | tf_op jit(solution)/shard_map/ppermute | solution.py:68
  90.2 1.6 %collective-permute-start.30 = (bf16[2,128,128]{2,1,0:T(8,128)(2,1)S(1)}, bf16[2,128,128]{2,1,0:T(8,128)(2,1)S(1)}, u32[]{:S(2)}, u32[]{:S(2)}) collective-permute-start(bf16[2,128,128]{2,1,0:T(8,128)(2,1)S(1)} %collective-permute-done.26.refs_2_), channel_id=1, source_target_pairs={{0,1},{1,0},{2,3},{3,2},{4,5},{5,4},{6,7},{7,6},{8,9},{9,8},{10,11... | collective-permute-start | bytes 196616 | tf_op jit(solution)/shard_map/ppermute | solution.py:68
  (89 shorter events, 28.3 us)
Async XLA Ops:
  2.4 11.1 %collective-permute-start = (bf16[128,768]{1,0:T(8,128)(2,1)S(1)}, bf16[128,768]{1,0:T(8,128)(2,1)S(1)}, u32[]{:S(2)}, u32[]{:S(2)}) collective-permute-start(bf16[128,768]{1,0:T(8,128)(2,1)S(1)} %shard_map.130.w0), channel_id=1, source_target_pairs={{0,8},{1,33},{2,10},{3,35},{4,12},{5,37},{6,14},{7,39},{8,16},{9,4... | collective-permute-start | bytes 589832 | tf_op jit(solution)/shard_map/ppermute | solution.py:47
  5.0 8.8 %collective-permute-start.1 = (bf16[128,768]{1,0:T(8,128)(2,1)S(1)}, bf16[128,768]{1,0:T(8,128)(2,1)S(1)}, u32[]{:S(2)}, u32[]{:S(2)}) collective-permute-start(bf16[128,768]{1,0:T(8,128)(2,1)S(1)} %shard_map.130.w0), channel_id=1, source_target_pairs={{0,16},{1,65},{2,18},{3,67},{4,20},{5,69},{6,22},{7,71},{8,24},{9,... | collective-permute-start | bytes 589832 | tf_op jit(solution)/shard_map/ppermute | solution.py:47
  8.3 5.5 %collective-permute-start.2 = (bf16[128,768]{1,0:T(8,128)(2,1)S(1)}, bf16[128,768]{1,0:T(8,128)(2,1)S(1)}, u32[]{:S(2)}, u32[]{:S(2)}) collective-permute-start(bf16[128,768]{1,0:T(8,128)(2,1)S(1)} %shard_map.130.w0), channel_id=1, source_target_pairs={{0,24},{1,97},{2,26},{3,99},{4,28},{5,101},{6,30},{7,103},{8,0},{9... | collective-permute-start | bytes 589832 | tf_op jit(solution)/shard_map/ppermute | solution.py:47
  13.8 8.4 %collective-permute-start.15 = (bf16[4,128,512]{2,1,0:T(8,128)(2,1)S(1)}, bf16[4,128,512]{2,1,0:T(8,128)(2,1)S(1)}, u32[]{:S(2)}, u32[]{:S(2)}) collective-permute-start(bf16[4,128,512]{2,1,0:T(8,128)(2,1)S(1)} %get-tuple-element.77.w0), channel_id=1, source_target_pairs={{0,32},{1,9},{2,34},{3,11},{4,36},{5,13},{6,38},{7,15},{8,40},{9,1... | collective-permute-start | bytes 1572872 | tf_op jit(solution)/shard_map/ppermute | solution.py:60
  15.0 10.0 %collective-permute-start.3 = (bf16[4,128,256]{2,1,0:T(8,128)(2,1)S(1)}, bf16[4,128,256]{2,1,0:T(8,128)(2,1)S(1)}, u32[]{:S(2)}, u32[]{:S(2)}) collective-permute-start(bf16[4,128,256]{2,1,0:T(8,128)(2,1)S(1)} %get-tuple-element.59.w0), channel_id=1, source_target_pairs={{0,32},{1,9},{2,34},{3,11},{4,36},{5,13},{6,38},{7,15},{8,40},{9,1... | collective-permute-start | bytes 786440 | tf_op jit(solution)/shard_map/ppermute | solution.py:47
  15.3 14.8 %collective-permute-start.4 = (bf16[4,128,256]{2,1,0:T(8,128)(2,1)S(1)}, bf16[4,128,256]{2,1,0:T(8,128)(2,1)S(1)}, u32[]{:S(2)}, u32[]{:S(2)}) collective-permute-start(bf16[4,128,256]{2,1,0:T(8,128)(2,1)S(1)} %get-tuple-element.59.w0), channel_id=1, source_target_pairs={{0,64},{1,17},{2,66},{3,19},{4,68},{5,21},{6,70},{7,23},{8,72},{9,... | collective-permute-start | bytes 786440 | tf_op jit(solution)/shard_map/ppermute | solution.py:47
  18.1 12.1 %collective-permute-start.5 = (bf16[4,128,256]{2,1,0:T(8,128)(2,1)S(1)}, bf16[4,128,256]{2,1,0:T(8,128)(2,1)S(1)}, u32[]{:S(2)}, u32[]{:S(2)}) collective-permute-start(bf16[4,128,256]{2,1,0:T(8,128)(2,1)S(1)} %get-tuple-element.59.w0), channel_id=1, source_target_pairs={{0,96},{1,25},{2,98},{3,27},{4,100},{5,29},{6,102},{7,31},{8,104},... | collective-permute-start | bytes 786440 | tf_op jit(solution)/shard_map/ppermute | solution.py:47
  19.7 33.0 %collective-permute-start.16 = (bf16[4,128,512]{2,1,0:T(8,128)(2,1)S(1)}, bf16[4,128,512]{2,1,0:T(8,128)(2,1)S(1)}, u32[]{:S(2)}, u32[]{:S(2)}) collective-permute-start(bf16[4,128,512]{2,1,0:T(8,128)(2,1)S(1)} %get-tuple-element.77.w0), channel_id=1, source_target_pairs={{0,96},{1,25},{2,98},{3,27},{4,100},{5,29},{6,102},{7,31},{8,104},... | collective-permute-start | bytes 1572872 | tf_op jit(solution)/shard_map/ppermute | solution.py:60
  22.2 30.5 %collective-permute-start.17 = (bf16[4,128,512]{2,1,0:T(8,128)(2,1)S(1)}, bf16[4,128,512]{2,1,0:T(8,128)(2,1)S(1)}, u32[]{:S(2)}, u32[]{:S(2)}) collective-permute-start(bf16[4,128,512]{2,1,0:T(8,128)(2,1)S(1)} %collective-permute-done.15.w1), channel_id=1, source_target_pairs={{0,96},{1,25},{2,98},{3,27},{4,100},{5,29},{6,102},{7,31},{8,104},... | collective-permute-start | bytes 1572872 | tf_op jit(solution)/shard_map/ppermute | solution.py:60
  31.2 6.5 %collective-permute-start.6 = (bf16[4,64,128]{2,1,0:T(8,128)(2,1)S(1)}, bf16[4,64,128]{2,1,0:T(8,128)(2,1)S(1)}, u32[]{:S(2)}, u32[]{:S(2)}) collective-permute-start(bf16[4,64,128]{2,1,0:T(8,128)(2,1)S(1)} %shard_map.134.queries.x0), channel_id=1, source_target_pairs={{0,8},{1,33},{2,10},{3,35},{4,12},{5,37},{6,14},{7,39},{8,16},{9,4... | collective-permute-start | bytes 196616 | tf_op jit(solution)/shard_map/ppermute | solution.py:47
  32.1 5.5 %collective-permute-start.7 = (bf16[4,64,128]{2,1,0:T(8,128)(2,1)S(1)}, bf16[4,64,128]{2,1,0:T(8,128)(2,1)S(1)}, u32[]{:S(2)}, u32[]{:S(2)}) collective-permute-start(bf16[4,64,128]{2,1,0:T(8,128)(2,1)S(1)} %shard_map.134.queries.x0), channel_id=1, source_target_pairs={{0,16},{1,65},{2,18},{3,67},{4,20},{5,69},{6,22},{7,71},{8,24},{9,... | collective-permute-start | bytes 196616 | tf_op jit(solution)/shard_map/ppermute | solution.py:47
  38.3 4.7 %collective-permute-start.10 = (bf16[4,64,128]{2,1,0:T(8,128)(2,1)S(1)}, bf16[4,64,128]{2,1,0:T(8,128)(2,1)S(1)}, u32[]{:S(2)}, u32[]{:S(2)}) collective-permute-start(bf16[4,64,128]{2,1,0:T(8,128)(2,1)S(1)} %get-tuple-element.69), channel_id=1, source_target_pairs={{0,64},{1,17},{2,66},{3,19},{4,68},{5,21},{6,70},{7,23},{8,72},{9,... | collective-permute-start | bytes 196616 | tf_op jit(solution)/shard_map/ppermute | solution.py:47
  39.1 4.6 %collective-permute-start.9 = (bf16[4,64,128]{2,1,0:T(8,128)(2,1)S(1)}, bf16[4,64,128]{2,1,0:T(8,128)(2,1)S(1)}, u32[]{:S(2)}, u32[]{:S(2)}) collective-permute-start(bf16[4,64,128]{2,1,0:T(8,128)(2,1)S(1)} %get-tuple-element.68), channel_id=1, source_target_pairs={{0,32},{1,9},{2,34},{3,11},{4,36},{5,13},{6,38},{7,15},{8,40},{9,1... | collective-permute-start | bytes 196616 | tf_op jit(solution)/shard_map/ppermute | solution.py:47
  46.6 7.8 %collective-permute-start.12 = (bf16[4,80,128]{2,1,0:T(8,128)(2,1)S(1)}, bf16[4,80,128]{2,1,0:T(8,128)(2,1)S(1)}, u32[]{:S(2)}, u32[]{:S(2)}) collective-permute-start(bf16[4,80,128]{2,1,0:T(8,128)(2,1)S(1)} %shard_map.138.x0), channel_id=1, source_target_pairs={{0,8},{1,33},{2,10},{3,35},{4,12},{5,37},{6,14},{7,39},{8,16},{9,4... | collective-permute-start | bytes 245768 | tf_op jit(solution)/shard_map/ppermute | solution.py:47
  48.3 6.1 %collective-permute-start.13 = (bf16[4,80,128]{2,1,0:T(8,128)(2,1)S(1)}, bf16[4,80,128]{2,1,0:T(8,128)(2,1)S(1)}, u32[]{:S(2)}, u32[]{:S(2)}) collective-permute-start(bf16[4,80,128]{2,1,0:T(8,128)(2,1)S(1)} %shard_map.138.x0), channel_id=1, source_target_pairs={{0,16},{1,65},{2,18},{3,67},{4,20},{5,69},{6,22},{7,71},{8,24},{9,... | collective-permute-start | bytes 245768 | tf_op jit(solution)/shard_map/ppermute | solution.py:47
  55.4 4.9 %collective-permute-start.18 = (bf16[4,80,128]{2,1,0:T(8,128)(2,1)S(1)}, bf16[4,80,128]{2,1,0:T(8,128)(2,1)S(1)}, u32[]{:S(2)}, u32[]{:S(2)}) collective-permute-start(bf16[4,80,128]{2,1,0:T(8,128)(2,1)S(1)} %get-tuple-element.88), channel_id=1, source_target_pairs={{0,32},{1,9},{2,34},{3,11},{4,36},{5,13},{6,38},{7,15},{8,40},{9,1... | collective-permute-start | bytes 245768 | tf_op jit(solution)/shard_map/ppermute | solution.py:47
  55.8 6.6 %collective-permute-start.19 = (bf16[4,80,128]{2,1,0:T(8,128)(2,1)S(1)}, bf16[4,80,128]{2,1,0:T(8,128)(2,1)S(1)}, u32[]{:S(2)}, u32[]{:S(2)}) collective-permute-start(bf16[4,80,128]{2,1,0:T(8,128)(2,1)S(1)} %get-tuple-element.89), channel_id=1, source_target_pairs={{0,64},{1,17},{2,66},{3,19},{4,68},{5,21},{6,70},{7,23},{8,72},{9,... | collective-permute-start | bytes 245768 | tf_op jit(solution)/shard_map/ppermute | solution.py:47
  64.0 10.5 %collective-permute-start.21 = (bf16[4,2,128,128]{3,2,1,0:T(8,128)(2,1)S(1)}, bf16[4,2,128,128]{3,2,1,0:T(8,128)(2,1)S(1)}, u32[]{:S(2)}, u32[]{:S(2)}) collective-permute-start(bf16[4,2,128,128]{3,2,1,0:T(8,128)(2,1)S(1)} %get-tuple-element.94), channel_id=1, source_target_pairs={{0,1},{1,0},{2,3},{3,2},{4,5},{5,4},{6,7},{7,6},{8,9},{9,8},{10,11... | collective-permute-start | bytes 786440 | tf_op jit(solution)/shard_map/ppermute | solution.py:68
  75.1 4.9 %collective-permute-start.22 = (bf16[2,128,128]{2,1,0:T(8,128)(2,1)S(1)}, bf16[2,128,128]{2,1,0:T(8,128)(2,1)S(1)}, u32[]{:S(2)}, u32[]{:S(2)}) collective-permute-start(bf16[2,128,128]{2,1,0:T(8,128)(2,1)S(1)} %get-tuple-element.96), channel_id=1, source_target_pairs={{0,2},{1,3},{2,4},{3,5},{4,6},{5,7},{6,0},{7,1},{8,10},{9,11},{10,... | collective-permute-start | bytes 196616 | tf_op jit(solution)/shard_map/ppermute | solution.py:64
  76.4 5.4 %collective-permute-start.23 = (bf16[2,128,128]{2,1,0:T(8,128)(2,1)S(1)}, bf16[2,128,128]{2,1,0:T(8,128)(2,1)S(1)}, u32[]{:S(2)}, u32[]{:S(2)}) collective-permute-start(bf16[2,128,128]{2,1,0:T(8,128)(2,1)S(1)} %get-tuple-element.97), channel_id=1, source_target_pairs={{0,4},{1,5},{2,6},{3,7},{4,0},{5,1},{6,2},{7,3},{8,12},{9,13},{10,... | collective-permute-start | bytes 196616 | tf_op jit(solution)/shard_map/ppermute | solution.py:64
  82.9 6.4 %collective-permute-start.25 = (bf16[2,128,128]{2,1,0:T(8,128)(2,1)S(1)}, bf16[2,128,128]{2,1,0:T(8,128)(2,1)S(1)}, u32[]{:S(2)}, u32[]{:S(2)}) collective-permute-start(bf16[2,128,128]{2,1,0:T(8,128)(2,1)S(1)} %shard_map.143.refs_0_), channel_id=1, source_target_pairs={{0,2},{1,3},{2,4},{3,5},{4,6},{5,7},{6,0},{7,1},{8,10},{9,11},{10,... | collective-permute-start | bytes 196616 | tf_op jit(solution)/shard_map/ppermute | solution.py:64
  83.0 7.3 %collective-permute-start.26 = (bf16[2,128,128]{2,1,0:T(8,128)(2,1)S(1)}, bf16[2,128,128]{2,1,0:T(8,128)(2,1)S(1)}, u32[]{:S(2)}, u32[]{:S(2)}) collective-permute-start(bf16[2,128,128]{2,1,0:T(8,128)(2,1)S(1)} %shard_map.143.refs_0_), channel_id=1, source_target_pairs={{0,4},{1,5},{2,6},{3,7},{4,0},{5,1},{6,2},{7,3},{8,12},{9,13},{10,... | collective-permute-start | bytes 196616 | tf_op jit(solution)/shard_map/ppermute | solution.py:64
  86.2 5.6 %collective-permute-start.27 = (bf16[2,128,128]{2,1,0:T(8,128)(2,1)S(1)}, bf16[2,128,128]{2,1,0:T(8,128)(2,1)S(1)}, u32[]{:S(2)}, u32[]{:S(2)}) collective-permute-start(bf16[2,128,128]{2,1,0:T(8,128)(2,1)S(1)} %shard_map.143.refs_0_), channel_id=1, source_target_pairs={{0,6},{1,7},{2,0},{3,1},{4,2},{5,3},{6,4},{7,5},{8,14},{9,15},{10,... | collective-permute-start | bytes 196616 | tf_op jit(solution)/shard_map/ppermute | solution.py:64
  86.6 6.5 %collective-permute-start.28 = (bf16[2,128,128]{2,1,0:T(8,128)(2,1)S(1)}, bf16[2,128,128]{2,1,0:T(8,128)(2,1)S(1)}, u32[]{:S(2)}, u32[]{:S(2)}) collective-permute-start(bf16[2,128,128]{2,1,0:T(8,128)(2,1)S(1)} %shard_map.143.refs_0_), channel_id=1, source_target_pairs={{0,1},{1,0},{2,3},{3,2},{4,5},{5,4},{6,7},{7,6},{8,9},{9,8},{10,11... | collective-permute-start | bytes 196616 | tf_op jit(solution)/shard_map/ppermute | solution.py:68
  (22 other events, 173.4 us)

commit v4 on v3

--- a/solution.py
+++ b/solution.py
@@ -13,7 +13,8 @@
 PER = 32
 PLEN = 4096
 TLEN = 256
-KB = 1024
+FIRST = 2048
+LATER = ((2048, 2048),)
 MSG = 80
 EPS = 1e-06
 NEG = -1e30
@@ -68,7 +69,10 @@
     return lax.ppermute(value, "narrow", [(n, n ^ 1) for n in range(8)])
 
 
-def call(kernel, out_shape, args, smem=(), smem_out=(), hbm=(), hbm_out=False, scratch=(), cost=None):
+def call(
+    kernel, out_shape, args, smem=(), smem_out=(), hbm=(), hbm_out=False, scratch=(), cost=None,
+    grant=8 << 20,
+):
     def spec(is_scalar, is_far):
         space = SMEM if is_scalar else pltpu.HBM if is_far else pltpu.VMEM
         return pl.BlockSpec(memory_space=space)
@@ -85,7 +89,7 @@
         in_specs=specs,
         out_specs=outs,
         scratch_shapes=list(scratch),
-        compiler_params=pltpu.CompilerParams(vmem_limit_bytes=8 << 20),
+        compiler_params=pltpu.CompilerParams(vmem_limit_bytes=grant),
         cost_estimate=pl.CostEstimate(flops=flops, bytes_accessed=nbytes, transcendentals=0),
     )(*args)
 
@@ -266,53 +270,79 @@
             stats[at : at + 16] = both[h * 16 : h * 16 + 16]
 
 
-def prefix_kernel(table, r0, r1, r2, r3, cache, out, held, scores):
-    select = [table[16 + s] for s in range(4)]
+def prefix_kernel(table, r0, r1, r2, r3, cache, out, held, scores, highs, totals, accs):
     lens = [table[20 + s] for s in range(4)]
-    counts = [(lens[s] + (KB - 1)) // KB for s in range(4)]
     for e, ref in enumerate((r0, r1, r2, r3)):
         held[e] = ref[...]
-    lane = lax.broadcasted_iota(jnp.int32, (64, KB), 1)
+    queries = [held[table[16 + s], s] for s in range(4)]
+
+    def first(s, start, size, high):
+        block = cache[0, s, pl.ds(start, size)]
+        part = lax.dot_general(queries[s], block, CONTRACT, preferred_element_type=F32)
+        lane = lax.broadcasted_iota(jnp.int32, (64, size), 1)
+        part = jnp.where(lane < lens[s] - start, part, NEG)
+        for c in range(size // HD):
+            piece = part[:, c * HD : (c + 1) * HD]
+            scores[s, start // HD + c] = piece
+            high = piece if high is None else jnp.maximum(high, piece)
+        return high
+
+    def second(s, start, size, high, sums, acc):
+        weights = []
+        for c in range(size // HD):
+            weight = jnp.exp2((scores[s, start // HD + c] - high) * (SCALE * LOG2E))
+            sums = weight if sums is None else sums + weight
+            weights.append(weight.astype(BF16))
+        block = cache[1, s, pl.ds(start, size)]
+        more = jnp.dot(jnp.concatenate(weights, axis=1), block, preferred_element_type=F32)
+        return sums, more if acc is None else acc + more
+
     for s in range(4):
-        q = held[select[s], s]
-
-        def first(i, high):
-            block = cache[0, s, pl.ds(pl.multiple_of(i * KB, KB), KB)]
-            part = lax.dot_general(q, block, CONTRACT, preferred_element_type=F32)
-            part = jnp.where(lane < lens[s] - i * KB, part, NEG)
-            scores[i] = part
-            for c in range(KB // HD):
-                high = jnp.maximum(high, part[:, c * HD : (c + 1) * HD])
-            return high
-
-        high = lax.fori_loop(0, counts[s], first, jnp.full((64, HD), NEG, F32))
-        high = jnp.max(high, axis=1, keepdims=True)
-
-        def second(i, carry):
-            sums, acc = carry
-            weight = jnp.exp2((scores[i] - high) * (SCALE * LOG2E))
-            for c in range(KB // HD):
-                sums = sums + weight[:, c * HD : (c + 1) * HD]
-            block = cache[1, s, pl.ds(pl.multiple_of(i * KB, KB), KB)]
-            acc = acc + jnp.dot(weight.astype(BF16), block, preferred_element_type=F32)
-            return sums, acc
-
-        zero = jnp.zeros((64, HD), F32)
-        sums, acc = lax.fori_loop(0, counts[s], second, (zero, zero))
-        sums = jnp.sum(sums, axis=1, keepdims=True)
-        out[s, :64] = (acc / sums).astype(BF16)
-        logs = jnp.broadcast_to(high * SCALE + jnp.log(sums), (64, HD))
-        row = lax.broadcasted_iota(jnp.int32, (64, HD), 0)
-        column_of = lax.broadcasted_iota(jnp.int32, (64, HD), 1)
+        highs[s] = first(s, 0, FIRST, None)
+    for start, size in LATER:
+        for s in range(4):
+
+            @pl.when(lens[s] > start)
+            def _():
+                highs[s] = first(s, start, size, highs[s])
+
+    for s in range(4):
+        highs[s] = jnp.broadcast_to(jnp.max(highs[s], axis=1, keepdims=True), (64, HD))
+    for s in range(4):
+        totals[s], accs[s] = second(s, 0, FIRST, highs[s], None, None)
+    for start, size in LATER:
+        for s in range(4):
+
+            @pl.when(lens[s] > start)
+            def _():
+                totals[s], accs[s] = second(s, start, size, highs[s], totals[s], accs[s])
+
+    row = lax.broadcasted_iota(jnp.int32, (64, HD), 0)
+    column_of = lax.broadcasted_iota(jnp.int32, (64, HD), 1)
+    which = lax.broadcasted_iota(jnp.int32, (16, HD), 0)
+    for s in range(4):
+        sums = jnp.broadcast_to(jnp.sum(totals[s], axis=1, keepdims=True), (64, HD))
+        out[s, :64] = (accs[s] / sums).astype(BF16)
+        logs = highs[s] * SCALE + jnp.log(sums)
         line = jnp.sum(jnp.where(row == column_of, logs, 0.0), axis=0, keepdims=True)
         top = line.astype(BF16).astype(F32)
         middle = (line - top).astype(BF16).astype(F32)
         low = line - top - middle
-        which = lax.broadcasted_iota(jnp.int32, (16, HD), 0)
         lines = jnp.where(
             which == 0, top, jnp.where(which == 1, middle, jnp.where(which == 2, low, 0.0))
         )
         out[s, 64:MSG] = lines.astype(BF16)
+
+
+def prefix_scratch():
+    part = pltpu.VMEM((4, 64, HD), F32)
+    return [
+        pltpu.VMEM((4, 4, 64, HD), BF16),
+        pltpu.VMEM((4, PLEN // HD, 64, HD), F32),
+        part,
+        part,
+        part,
+    ]
 
 
 def finish_kernel(
@@ -458,6 +488,7 @@
         [w_qkv, w_out],
         hbm=(0, 1),
         scratch=[pltpu.SemaphoreType.DMA((3,))],
+        grant=60 << 20,
     )
     near = gather_ring(mixed, True)
     normed = call(
@@ -501,7 +532,7 @@
         struct((4, MSG, HD), BF16),
         [table] + asked + [prefix_cache],
         smem=(0,),
-        scratch=[pltpu.VMEM((4, 4, 64, HD), BF16), pltpu.VMEM((PLEN // KB, 64, KB), F32)],
+        scratch=prefix_scratch(),
         cost=(2 * 2 * 4 * 64 * PLEN * HD, 8 << 20),
     )
     held = gather_ring(results, True)

time: 96.2 us -> 94.6 us (0.983)
  starting transfers between devices: 55.5 us -> 52.7 us
  waiting for transfers between devices: 16.6 us -> 18.5 us
  local copies, waits for them, and re-layouts: 4.21 us -> 2.46 us
  Pallas kernels: 18 us -> 19.2 us
    unnamed x28 -> x26, local copies, waits for them, and re-layouts: 4.21 us -> 2.46 us
    ppermute x18, starting transfers between devices: 27.3 us -> 25.6 us  [shift(): return lax.ppermute(value, AXES, ring(first, step))]
    ppermute x18, waiting for transfers between devices: 9.8 us -> 11.5 us  [shift(): return lax.ppermute(value, AXES, ring(first, step))]
    pallas_call x15, Pallas kernels: 18 us -> 19.2 us  [call(): pl.pallas_call(kernel, out_shape=out_shape, in_specs=specs, out_specs=out...]
  transfers between devices with their start and end apart: 32 -> 32, of which waited for: 12 -> 14; matrix products, arithmetic and copies ran while one was open for 0% -> 0% of each run, Pallas kernels for 14% -> 14%
where the time goes in v4:
time: 94.6 us; the launch traced here: 94.2 us
  starting transfers between devices  52.7 us (56%)
  Pallas kernels  19.2 us (20%)
  waiting for transfers between devices  18.5 us (20%)
  local copies, waits for them, and re-layouts  2.46 us (3%)
  between operations  1.03 us (1%)
    ppermute x18, starting transfers between devices, shift(): return lax.ppermute(value, AXES, ring(first, step))  25.6 us
    pallas_call x15, Pallas kernels, call(): pl.pallas_call(kernel, out_shape=out_shape, in_specs=specs, out_specs=out...  19.2 us
    ppermute x5, starting transfers between devices, swap_core(): return lax.ppermute(value, 'narrow', [(n, n ^ 1) for n in range(8)])  15 us
    ppermute x18, waiting for transfers between devices, shift(): return lax.ppermute(value, AXES, ring(first, step))  11.5 us
    ppermute x6, starting transfers between devices, shift_x(): lax.ppermute(value, 'narrow', [(n, (n + 2 * step) % 8) for n in range(8)])  8.59 us
    ppermute x3, starting transfers between devices, shift_pair(): return lax.ppermute(value, AXES, pairs)  3.55 us
    ppermute x3, waiting for transfers between devices, shift_pair(): return lax.ppermute(value, AXES, pairs)  2.6 us
    unnamed x26, local copies, waits for them, and re-layouts  2.46 us
  transfers between devices with their start and end apart: 32, of which 14 were waited for; matrix products, arithmetic and copies ran while one was open for 0% of the time, Pallas kernels for 14%

profile of v4, /device:TPU:1, one launch (start us, length us, event | category | flops | bytes accessed | tf_op | source)
XLA Modules:
  0.0 94.2 jit_solution(15851554629980766942)
XLA Ops:
  0.6 1.6 %shard_map.130.w0 = bf16[128,768]{1,0:T(8,128)(2,1)} custom-call(bf16[128,512]{1,0:T(8,128)(2,1)} %w_qkv.1, bf16[256,128]{1,0:T(8,128)(2,1)} %w_out.1), custom_call_target="tpu_custom_call" | custom-call | flops 1048576 | bytes 1048576 | tf_op jit(solution)/shard_map/pallas_call | solution.py:86
  2.2 2.5 %collective-permute-start = (bf16[128,768]{1,0:T(8,128)(2,1)}, bf16[128,768]{1,0:T(8,128)(2,1)S(1)}, u32[]{:S(2)}, u32[]{:S(2)}) collective-permute-start(bf16[128,768]{1,0:T(8,128)(2,1)} %shard_map.130.w0), channel_id=1, source_target_pairs={{0,8},{1,33},{2,10},{3,35},{4,12},{5,37},{6,14},{7,39},{8,16},{9,4... | collective-permute-start | bytes 589832 | tf_op jit(solution)/shard_map/ppermute | solution.py:48
  4.8 3.3 %collective-permute-start.1 = (bf16[128,768]{1,0:T(8,128)(2,1)}, bf16[128,768]{1,0:T(8,128)(2,1)S(1)}, u32[]{:S(2)}, u32[]{:S(2)}) collective-permute-start(bf16[128,768]{1,0:T(8,128)(2,1)} %shard_map.130.w0), channel_id=1, source_target_pairs={{0,16},{1,65},{2,18},{3,67},{4,20},{5,69},{6,22},{7,71},{8,24},{9,... | collective-permute-start | bytes 589832 | tf_op jit(solution)/shard_map/ppermute | solution.py:48
  11.6 1.7 %shard_map.132 = (s32[64]{0:T(128)S(1)}, f32[128,128]{1,0:T(8,128)S(1)}) custom-call(s32[4]{0:T(128)S(1)} %pad_add_fusion.ids, s32[64]{0:T(128)S(1)} %copy-done.7, s32[64]{0:T(128)S(1)} %copy-done.8, s32[64]{0:T(128)S(1)} %copy-done.3, f32[1,128]{1,0:T(1,128)S(1)} %fusion.2.freq), custom_call_target="tpu_custom_call" | custom-call | flops 1048576 | bytes 1048576 | tf_op jit(solution)/shard_map/pallas_call | solution.py:86
  15.4 2.6 %collective-permute-start.4 = (bf16[4,128,256]{2,1,0:T(8,128)(2,1)S(1)}, bf16[4,128,256]{2,1,0:T(8,128)(2,1)S(1)}, u32[]{:S(2)}, u32[]{:S(2)}) collective-permute-start(bf16[4,128,256]{2,1,0:T(8,128)(2,1)S(1)} %get-tuple-element.59.w0), channel_id=1, source_target_pairs={{0,64},{1,17},{2,66},{3,19},{4,68},{5,21},{6,70},{7,23},{8,72},{9,... | collective-permute-start | bytes 786440 | tf_op jit(solution)/shard_map/ppermute | solution.py:48
  18.0 1.6 %collective-permute-start.5 = (bf16[4,128,256]{2,1,0:T(8,128)(2,1)S(1)}, bf16[4,128,256]{2,1,0:T(8,128)(2,1)S(1)}, u32[]{:S(2)}, u32[]{:S(2)}) collective-permute-start(bf16[4,128,256]{2,1,0:T(8,128)(2,1)S(1)} %get-tuple-element.59.w0), channel_id=1, source_target_pairs={{0,96},{1,25},{2,98},{3,27},{4,100},{5,29},{6,102},{7,31},{8,104},... | collective-permute-start | bytes 786440 | tf_op jit(solution)/shard_map/ppermute | solution.py:48
  19.6 2.6 %collective-permute-done.15.w1 = bf16[4,128,512]{2,1,0:T(8,128)(2,1)S(1)} collective-permute-done((bf16[4,128,512]{2,1,0:T(8,128)(2,1)S(1)}, bf16[4,128,512]{2,1,0:T(8,128)(2,1)S(1)}, u32[]{:S(2)}, u32[]{:S(2)}) %collective-permute-start.15) | collective-permute-done | bytes 524320 | tf_op jit(solution)/shard_map/ppermute | solution.py:61
  22.2 2.4 %collective-permute-start.17 = (bf16[4,128,512]{2,1,0:T(8,128)(2,1)S(1)}, bf16[4,128,512]{2,1,0:T(8,128)(2,1)S(1)}, u32[]{:S(2)}, u32[]{:S(2)}) collective-permute-start(bf16[4,128,512]{2,1,0:T(8,128)(2,1)S(1)} %collective-permute-done.15.w1), channel_id=1, source_target_pairs={{0,96},{1,25},{2,98},{3,27},{4,100},{5,29},{6,102},{7,31},{8,104},... | collective-permute-start | bytes 1572872 | tf_op jit(solution)/shard_map/ppermute | solution.py:61
  24.9 5.1 %collective-permute-done.4.w2 = bf16[4,128,256]{2,1,0:T(8,128)(2,1)S(1)} collective-permute-done((bf16[4,128,256]{2,1,0:T(8,128)(2,1)S(1)}, bf16[4,128,256]{2,1,0:T(8,128)(2,1)S(1)}, u32[]{:S(2)}, u32[]{:S(2)}) %collective-permute-start.4) | collective-permute-done | bytes 262176 | tf_op jit(solution)/shard_map/ppermute | solution.py:48
  32.2 2.1 %collective-permute-start.7 = (bf16[4,64,128]{2,1,0:T(8,128)(2,1)S(1)}, bf16[4,64,128]{2,1,0:T(8,128)(2,1)S(1)}, u32[]{:S(2)}, u32[]{:S(2)}) collective-permute-start(bf16[4,64,128]{2,1,0:T(8,128)(2,1)S(1)} %shard_map.134.queries.x0), channel_id=1, source_target_pairs={{0,16},{1,65},{2,18},{3,67},{4,20},{5,69},{6,22},{7,71},{8,24},{9,... | collective-permute-start | bytes 196616 | tf_op jit(solution)/shard_map/ppermute | solution.py:48
  35.2 2.4 %shard_map.135 = (f32[128,128]{1,0:T(8,128)S(1)}, f32[128,128]{1,0:T(8,128)S(1)}) custom-call(s32[64]{0:T(128)S(1)} %copy-done.3, bf16[4,64,128]{2,1,0:T(8,128)(2,1)S(1)} %shard_map.134.queries.x0, bf16[2,64,256,128]{3,2,1,0:T(8,128)(2,1)S(1)} %bitcast.9), custom_call_target="tpu_custom_call" | custom-call | flops 134217728 | bytes 4194304 | tf_op jit(solution)/shard_map/pallas_call | solution.py:86
  40.5 2.4 %shard_map.137 = (f32[128,128]{1,0:T(8,128)S(1)}, f32[128,128]{1,0:T(8,128)S(1)}) custom-call(s32[64]{0:T(128)S(1)} %copy-done.3, bf16[4,64,128]{2,1,0:T(8,128)(2,1)S(1)} %shard_map.134.queries.x0, bf16[2,64,256,128]{3,2,1,0:T(8,128)(2,1)S(1)} %bitcast.9), custom_call_target="tpu_custom_call" | custom-call | flops 134217728 | bytes 4194304 | tf_op jit(solution)/shard_map/pallas_call | solution.py:86
  43.7 2.7 %shard_map.138.x0 = bf16[4,80,128]{2,1,0:T(8,128)(2,1)S(1)} custom-call(s32[64]{0:T(128)S(1)} %get-tuple-element.53.index.table, bf16[4,64,128]{2,1,0:T(8,128)(2,1)S(1)} %get-tuple-element.73.r0, bf16[4,64,128]{2,1,0:T(8,128)(2,1)S(1)} %collective-permute-done.9.r1, bf16[4,64,128]{2,1,0:T(8,128)(2,1)S(1)} %collective-permute-done.10.r2, ...), custom_call_target="tpu_custom_call" | custom-call | flops 536870912 | bytes 8388608 | tf_op jit(solution)/shard_map/pallas_call | solution.py:86
  47.5 3.4 %collective-permute-start.13 = (bf16[4,80,128]{2,1,0:T(8,128)(2,1)S(1)}, bf16[4,80,128]{2,1,0:T(8,128)(2,1)S(1)}, u32[]{:S(2)}, u32[]{:S(2)}) collective-permute-start(bf16[4,80,128]{2,1,0:T(8,128)(2,1)S(1)} %shard_map.138.x0), channel_id=1, source_target_pairs={{0,16},{1,65},{2,18},{3,67},{4,20},{5,69},{6,22},{7,71},{8,24},{9,... | collective-permute-start | bytes 245768 | tf_op jit(solution)/shard_map/ppermute | solution.py:48
  50.9 1.7 %shard_map.139 = (bf16[2,128,128]{2,1,0:T(8,128)(2,1)}, f32[256,128]{1,0:T(8,128)S(1)}, f32[256,128]{1,0:T(8,128)S(1)}) custom-call(s32[4]{0:T(128)S(1)} %pad_add_fusion.ids, bf16[16,128,128]{2,1,0:T(8,128)(2,1)S(1)} %shard_map.131.normed, bf16[4,128,512]{2,1,0:T(8,128)(2,1)S(1)} %get-tuple-element.77.w0, ...), custom_call_target="tpu_custom_call" | custom-call | flops 134217728 | bytes 3145728 | tf_op jit(solution)/shard_map/pallas_call | solution.py:86
  54.8 1.9 %collective-permute-start.19 = (bf16[4,80,128]{2,1,0:T(8,128)(2,1)S(1)}, bf16[4,80,128]{2,1,0:T(8,128)(2,1)S(1)}, u32[]{:S(2)}, u32[]{:S(2)}) collective-permute-start(bf16[4,80,128]{2,1,0:T(8,128)(2,1)S(1)} %get-tuple-element.89), channel_id=1, source_target_pairs={{0,64},{1,17},{2,66},{3,19},{4,68},{5,21},{6,70},{7,23},{8,72},{9,... | collective-permute-start | bytes 245768 | tf_op jit(solution)/shard_map/ppermute | solution.py:48
  59.3 2.0 %collective-permute-done.19.c2 = bf16[4,80,128]{2,1,0:T(8,128)(2,1)S(1)} collective-permute-done((bf16[4,80,128]{2,1,0:T(8,128)(2,1)S(1)}, bf16[4,80,128]{2,1,0:T(8,128)(2,1)S(1)}, u32[]{:S(2)}, u32[]{:S(2)}) %collective-permute-start.19) | collective-permute-done | bytes 81952 | tf_op jit(solution)/shard_map/ppermute | solution.py:48
  61.9 1.6 %shard_map.141 = (f32[2,128]{1,0:T(2,128)}, f32[4,2,128,128]{3,2,1,0:T(8,128)S(1)}, bf16[4,2,128,128]{3,2,1,0:T(8,128)(2,1)S(1)}) custom-call(s32[4]{0:T(128)S(1)} %pad_add_fusion.ids, s32[64]{0:T(128)S(1)} %get-tuple-element.53.index.table, bf16[4,80,128]{2,1,0:T(8,128)(2,1)S(1)} %get-tuple-element.87.c0, ...), custom_call_target="tpu_custom_call" | custom-call | flops 134217728 | bytes 3145728 | tf_op jit(solution)/shard_map/pallas_call | solution.py:86
  63.5 8.4 %collective-permute-start.21 = (bf16[4,2,128,128]{3,2,1,0:T(8,128)(2,1)S(1)}, bf16[4,2,128,128]{3,2,1,0:T(8,128)(2,1)S(1)}, u32[]{:S(2)}, u32[]{:S(2)}) collective-permute-start(bf16[4,2,128,128]{3,2,1,0:T(8,128)(2,1)S(1)} %get-tuple-element.94), channel_id=1, source_target_pairs={{0,1},{1,0},{2,3},{3,2},{4,5},{5,4},{6,7},{7,6},{8,9},{9,8},{10,11... | collective-permute-start | bytes 786440 | tf_op jit(solution)/shard_map/ppermute | solution.py:69
  75.0 2.4 %collective-permute-start.23 = (bf16[2,128,128]{2,1,0:T(8,128)(2,1)S(1)}, bf16[2,128,128]{2,1,0:T(8,128)(2,1)S(1)}, u32[]{:S(2)}, u32[]{:S(2)}) collective-permute-start(bf16[2,128,128]{2,1,0:T(8,128)(2,1)S(1)} %get-tuple-element.97), channel_id=1, source_target_pairs={{0,4},{1,5},{2,6},{3,7},{4,0},{5,1},{6,2},{7,3},{8,12},{9,13},{10,... | collective-permute-start | bytes 196616 | tf_op jit(solution)/shard_map/ppermute | solution.py:65
  78.6 1.8 %collective-permute-done.23.g2 = bf16[2,128,128]{2,1,0:T(8,128)(2,1)S(1)} collective-permute-done((bf16[2,128,128]{2,1,0:T(8,128)(2,1)S(1)}, bf16[2,128,128]{2,1,0:T(8,128)(2,1)S(1)}, u32[]{:S(2)}, u32[]{:S(2)}) %collective-permute-start.23) | collective-permute-done | bytes 65568 | tf_op jit(solution)/shard_map/ppermute | solution.py:65
  81.5 3.2 %collective-permute-start.26 = (bf16[2,128,128]{2,1,0:T(8,128)(2,1)S(1)}, bf16[2,128,128]{2,1,0:T(8,128)(2,1)S(1)}, u32[]{:S(2)}, u32[]{:S(2)}) collective-permute-start(bf16[2,128,128]{2,1,0:T(8,128)(2,1)S(1)} %shard_map.143.refs_0_), channel_id=1, source_target_pairs={{0,4},{1,5},{2,6},{3,7},{4,0},{5,1},{6,2},{7,3},{8,12},{9,13},{10,... | collective-permute-start | bytes 196616 | tf_op jit(solution)/shard_map/ppermute | solution.py:65
  85.1 2.7 %collective-permute-start.28 = (bf16[2,128,128]{2,1,0:T(8,128)(2,1)S(1)}, bf16[2,128,128]{2,1,0:T(8,128)(2,1)S(1)}, u32[]{:S(2)}, u32[]{:S(2)}) collective-permute-start(bf16[2,128,128]{2,1,0:T(8,128)(2,1)S(1)} %shard_map.143.refs_0_), channel_id=1, source_target_pairs={{0,1},{1,0},{2,3},{3,2},{4,5},{5,4},{6,7},{7,6},{8,9},{9,8},{10,11... | collective-permute-start | bytes 196616 | tf_op jit(solution)/shard_map/ppermute | solution.py:69
  88.8 1.6 %collective-permute-start.30 = (bf16[2,128,128]{2,1,0:T(8,128)(2,1)S(1)}, bf16[2,128,128]{2,1,0:T(8,128)(2,1)S(1)}, u32[]{:S(2)}, u32[]{:S(2)}) collective-permute-start(bf16[2,128,128]{2,1,0:T(8,128)(2,1)S(1)} %collective-permute-done.26.refs_2_), channel_id=1, source_target_pairs={{0,1},{1,0},{2,3},{3,2},{4,5},{5,4},{6,7},{7,6},{8,9},{9,8},{10,11... | collective-permute-start | bytes 196616 | tf_op jit(solution)/shard_map/ppermute | solution.py:69
  (87 shorter events, 29.2 us)
Async XLA Ops:
  2.2 11.1 %collective-permute-start = (bf16[128,768]{1,0:T(8,128)(2,1)}, bf16[128,768]{1,0:T(8,128)(2,1)S(1)}, u32[]{:S(2)}, u32[]{:S(2)}) collective-permute-start(bf16[128,768]{1,0:T(8,128)(2,1)} %shard_map.130.w0), channel_id=1, source_target_pairs={{0,8},{1,33},{2,10},{3,35},{4,12},{5,37},{6,14},{7,39},{8,16},{9,4... | collective-permute-start | bytes 589832 | tf_op jit(solution)/shard_map/ppermute | solution.py:48
  4.8 9.0 %collective-permute-start.1 = (bf16[128,768]{1,0:T(8,128)(2,1)}, bf16[128,768]{1,0:T(8,128)(2,1)S(1)}, u32[]{:S(2)}, u32[]{:S(2)}) collective-permute-start(bf16[128,768]{1,0:T(8,128)(2,1)} %shard_map.130.w0), channel_id=1, source_target_pairs={{0,16},{1,65},{2,18},{3,67},{4,20},{5,69},{6,22},{7,71},{8,24},{9,... | collective-permute-start | bytes 589832 | tf_op jit(solution)/shard_map/ppermute | solution.py:48
  8.1 5.7 %collective-permute-start.2 = (bf16[128,768]{1,0:T(8,128)(2,1)}, bf16[128,768]{1,0:T(8,128)(2,1)S(1)}, u32[]{:S(2)}, u32[]{:S(2)}) collective-permute-start(bf16[128,768]{1,0:T(8,128)(2,1)} %shard_map.130.w0), channel_id=1, source_target_pairs={{0,24},{1,97},{2,26},{3,99},{4,28},{5,101},{6,30},{7,103},{8,0},{9... | collective-permute-start | bytes 589832 | tf_op jit(solution)/shard_map/ppermute | solution.py:48
  13.8 8.4 %collective-permute-start.15 = (bf16[4,128,512]{2,1,0:T(8,128)(2,1)S(1)}, bf16[4,128,512]{2,1,0:T(8,128)(2,1)S(1)}, u32[]{:S(2)}, u32[]{:S(2)}) collective-permute-start(bf16[4,128,512]{2,1,0:T(8,128)(2,1)S(1)} %get-tuple-element.77.w0), channel_id=1, source_target_pairs={{0,32},{1,9},{2,34},{3,11},{4,36},{5,13},{6,38},{7,15},{8,40},{9,1... | collective-permute-start | bytes 1572872 | tf_op jit(solution)/shard_map/ppermute | solution.py:61
  14.9 10.0 %collective-permute-start.3 = (bf16[4,128,256]{2,1,0:T(8,128)(2,1)S(1)}, bf16[4,128,256]{2,1,0:T(8,128)(2,1)S(1)}, u32[]{:S(2)}, u32[]{:S(2)}) collective-permute-start(bf16[4,128,256]{2,1,0:T(8,128)(2,1)S(1)} %get-tuple-element.59.w0), channel_id=1, source_target_pairs={{0,32},{1,9},{2,34},{3,11},{4,36},{5,13},{6,38},{7,15},{8,40},{9,1... | collective-permute-start | bytes 786440 | tf_op jit(solution)/shard_map/ppermute | solution.py:48
  15.4 14.7 %collective-permute-start.4 = (bf16[4,128,256]{2,1,0:T(8,128)(2,1)S(1)}, bf16[4,128,256]{2,1,0:T(8,128)(2,1)S(1)}, u32[]{:S(2)}, u32[]{:S(2)}) collective-permute-start(bf16[4,128,256]{2,1,0:T(8,128)(2,1)S(1)} %get-tuple-element.59.w0), channel_id=1, source_target_pairs={{0,64},{1,17},{2,66},{3,19},{4,68},{5,21},{6,70},{7,23},{8,72},{9,... | collective-permute-start | bytes 786440 | tf_op jit(solution)/shard_map/ppermute | solution.py:48
  18.0 12.1 %collective-permute-start.5 = (bf16[4,128,256]{2,1,0:T(8,128)(2,1)S(1)}, bf16[4,128,256]{2,1,0:T(8,128)(2,1)S(1)}, u32[]{:S(2)}, u32[]{:S(2)}) collective-permute-start(bf16[4,128,256]{2,1,0:T(8,128)(2,1)S(1)} %get-tuple-element.59.w0), channel_id=1, source_target_pairs={{0,96},{1,25},{2,98},{3,27},{4,100},{5,29},{6,102},{7,31},{8,104},... | collective-permute-start | bytes 786440 | tf_op jit(solution)/shard_map/ppermute | solution.py:48
  19.6 31.3 %collective-permute-start.16 = (bf16[4,128,512]{2,1,0:T(8,128)(2,1)S(1)}, bf16[4,128,512]{2,1,0:T(8,128)(2,1)S(1)}, u32[]{:S(2)}, u32[]{:S(2)}) collective-permute-start(bf16[4,128,512]{2,1,0:T(8,128)(2,1)S(1)} %get-tuple-element.77.w0), channel_id=1, source_target_pairs={{0,96},{1,25},{2,98},{3,27},{4,100},{5,29},{6,102},{7,31},{8,104},... | collective-permute-start | bytes 1572872 | tf_op jit(solution)/shard_map/ppermute | solution.py:61
  22.2 28.7 %collective-permute-start.17 = (bf16[4,128,512]{2,1,0:T(8,128)(2,1)S(1)}, bf16[4,128,512]{2,1,0:T(8,128)(2,1)S(1)}, u32[]{:S(2)}, u32[]{:S(2)}) collective-permute-start(bf16[4,128,512]{2,1,0:T(8,128)(2,1)S(1)} %collective-permute-done.15.w1), channel_id=1, source_target_pairs={{0,96},{1,25},{2,98},{3,27},{4,100},{5,29},{6,102},{7,31},{8,104},... | collective-permute-start | bytes 1572872 | tf_op jit(solution)/shard_map/ppermute | solution.py:61
  31.1 6.6 %collective-permute-start.6 = (bf16[4,64,128]{2,1,0:T(8,128)(2,1)S(1)}, bf16[4,64,128]{2,1,0:T(8,128)(2,1)S(1)}, u32[]{:S(2)}, u32[]{:S(2)}) collective-permute-start(bf16[4,64,128]{2,1,0:T(8,128)(2,1)S(1)} %shard_map.134.queries.x0), channel_id=1, source_target_pairs={{0,8},{1,33},{2,10},{3,35},{4,12},{5,37},{6,14},{7,39},{8,16},{9,4... | collective-permute-start | bytes 196616 | tf_op jit(solution)/shard_map/ppermute | solution.py:48
  32.2 5.5 %collective-permute-start.7 = (bf16[4,64,128]{2,1,0:T(8,128)(2,1)S(1)}, bf16[4,64,128]{2,1,0:T(8,128)(2,1)S(1)}, u32[]{:S(2)}, u32[]{:S(2)}) collective-permute-start(bf16[4,64,128]{2,1,0:T(8,128)(2,1)S(1)} %shard_map.134.queries.x0), channel_id=1, source_target_pairs={{0,16},{1,65},{2,18},{3,67},{4,20},{5,69},{6,22},{7,71},{8,24},{9,... | collective-permute-start | bytes 196616 | tf_op jit(solution)/shard_map/ppermute | solution.py:48
  38.3 4.7 %collective-permute-start.10 = (bf16[4,64,128]{2,1,0:T(8,128)(2,1)S(1)}, bf16[4,64,128]{2,1,0:T(8,128)(2,1)S(1)}, u32[]{:S(2)}, u32[]{:S(2)}) collective-permute-start(bf16[4,64,128]{2,1,0:T(8,128)(2,1)S(1)} %get-tuple-element.69), channel_id=1, source_target_pairs={{0,64},{1,17},{2,66},{3,19},{4,68},{5,21},{6,70},{7,23},{8,72},{9,... | collective-permute-start | bytes 196616 | tf_op jit(solution)/shard_map/ppermute | solution.py:48
  39.1 4.6 %collective-permute-start.9 = (bf16[4,64,128]{2,1,0:T(8,128)(2,1)S(1)}, bf16[4,64,128]{2,1,0:T(8,128)(2,1)S(1)}, u32[]{:S(2)}, u32[]{:S(2)}) collective-permute-start(bf16[4,64,128]{2,1,0:T(8,128)(2,1)S(1)} %get-tuple-element.68), channel_id=1, source_target_pairs={{0,32},{1,9},{2,34},{3,11},{4,36},{5,13},{6,38},{7,15},{8,40},{9,1... | collective-permute-start | bytes 196616 | tf_op jit(solution)/shard_map/ppermute | solution.py:48
  46.4 6.2 %collective-permute-start.12 = (bf16[4,80,128]{2,1,0:T(8,128)(2,1)S(1)}, bf16[4,80,128]{2,1,0:T(8,128)(2,1)S(1)}, u32[]{:S(2)}, u32[]{:S(2)}) collective-permute-start(bf16[4,80,128]{2,1,0:T(8,128)(2,1)S(1)} %shard_map.138.x0), channel_id=1, source_target_pairs={{0,8},{1,33},{2,10},{3,35},{4,12},{5,37},{6,14},{7,39},{8,16},{9,4... | collective-permute-start | bytes 245768 | tf_op jit(solution)/shard_map/ppermute | solution.py:48
  47.5 6.1 %collective-permute-start.13 = (bf16[4,80,128]{2,1,0:T(8,128)(2,1)S(1)}, bf16[4,80,128]{2,1,0:T(8,128)(2,1)S(1)}, u32[]{:S(2)}, u32[]{:S(2)}) collective-permute-start(bf16[4,80,128]{2,1,0:T(8,128)(2,1)S(1)} %shard_map.138.x0), channel_id=1, source_target_pairs={{0,16},{1,65},{2,18},{3,67},{4,20},{5,69},{6,22},{7,71},{8,24},{9,... | collective-permute-start | bytes 245768 | tf_op jit(solution)/shard_map/ppermute | solution.py:48
  54.8 6.5 %collective-permute-start.19 = (bf16[4,80,128]{2,1,0:T(8,128)(2,1)S(1)}, bf16[4,80,128]{2,1,0:T(8,128)(2,1)S(1)}, u32[]{:S(2)}, u32[]{:S(2)}) collective-permute-start(bf16[4,80,128]{2,1,0:T(8,128)(2,1)S(1)} %get-tuple-element.89), channel_id=1, source_target_pairs={{0,64},{1,17},{2,66},{3,19},{4,68},{5,21},{6,70},{7,23},{8,72},{9,... | collective-permute-start | bytes 245768 | tf_op jit(solution)/shard_map/ppermute | solution.py:48
  56.8 5.1 %collective-permute-start.20 = (bf16[4,80,128]{2,1,0:T(8,128)(2,1)S(1)}, bf16[4,80,128]{2,1,0:T(8,128)(2,1)S(1)}, u32[]{:S(2)}, u32[]{:S(2)}) collective-permute-start(bf16[4,80,128]{2,1,0:T(8,128)(2,1)S(1)} %get-tuple-element.90), channel_id=1, source_target_pairs={{0,96},{1,25},{2,98},{3,27},{4,100},{5,29},{6,102},{7,31},{8,104},... | collective-permute-start | bytes 245768 | tf_op jit(solution)/shard_map/ppermute | solution.py:48
  63.5 9.6 %collective-permute-start.21 = (bf16[4,2,128,128]{3,2,1,0:T(8,128)(2,1)S(1)}, bf16[4,2,128,128]{3,2,1,0:T(8,128)(2,1)S(1)}, u32[]{:S(2)}, u32[]{:S(2)}) collective-permute-start(bf16[4,2,128,128]{3,2,1,0:T(8,128)(2,1)S(1)} %get-tuple-element.94), channel_id=1, source_target_pairs={{0,1},{1,0},{2,3},{3,2},{4,5},{5,4},{6,7},{7,6},{8,9},{9,8},{10,11... | collective-permute-start | bytes 786440 | tf_op jit(solution)/shard_map/ppermute | solution.py:69
  73.7 4.9 %collective-permute-start.22 = (bf16[2,128,128]{2,1,0:T(8,128)(2,1)S(1)}, bf16[2,128,128]{2,1,0:T(8,128)(2,1)S(1)}, u32[]{:S(2)}, u32[]{:S(2)}) collective-permute-start(bf16[2,128,128]{2,1,0:T(8,128)(2,1)S(1)} %get-tuple-element.96), channel_id=1, source_target_pairs={{0,2},{1,3},{2,4},{3,5},{4,6},{5,7},{6,0},{7,1},{8,10},{9,11},{10,... | collective-permute-start | bytes 196616 | tf_op jit(solution)/shard_map/ppermute | solution.py:65
  75.0 5.4 %collective-permute-start.23 = (bf16[2,128,128]{2,1,0:T(8,128)(2,1)S(1)}, bf16[2,128,128]{2,1,0:T(8,128)(2,1)S(1)}, u32[]{:S(2)}, u32[]{:S(2)}) collective-permute-start(bf16[2,128,128]{2,1,0:T(8,128)(2,1)S(1)} %get-tuple-element.97), channel_id=1, source_target_pairs={{0,4},{1,5},{2,6},{3,7},{4,0},{5,1},{6,2},{7,3},{8,12},{9,13},{10,... | collective-permute-start | bytes 196616 | tf_op jit(solution)/shard_map/ppermute | solution.py:65
  81.4 6.4 %collective-permute-start.25 = (bf16[2,128,128]{2,1,0:T(8,128)(2,1)S(1)}, bf16[2,128,128]{2,1,0:T(8,128)(2,1)S(1)}, u32[]{:S(2)}, u32[]{:S(2)}) collective-permute-start(bf16[2,128,128]{2,1,0:T(8,128)(2,1)S(1)} %shard_map.143.refs_0_), channel_id=1, source_target_pairs={{0,2},{1,3},{2,4},{3,5},{4,6},{5,7},{6,0},{7,1},{8,10},{9,11},{10,... | collective-permute-start | bytes 196616 | tf_op jit(solution)/shard_map/ppermute | solution.py:65
  81.5 7.3 %collective-permute-start.26 = (bf16[2,128,128]{2,1,0:T(8,128)(2,1)S(1)}, bf16[2,128,128]{2,1,0:T(8,128)(2,1)S(1)}, u32[]{:S(2)}, u32[]{:S(2)}) collective-permute-start(bf16[2,128,128]{2,1,0:T(8,128)(2,1)S(1)} %shard_map.143.refs_0_), channel_id=1, source_target_pairs={{0,4},{1,5},{2,6},{3,7},{4,0},{5,1},{6,2},{7,3},{8,12},{9,13},{10,... | collective-permute-start | bytes 196616 | tf_op jit(solution)/shard_map/ppermute | solution.py:65
  84.8 5.6 %collective-permute-start.27 = (bf16[2,128,128]{2,1,0:T(8,128)(2,1)S(1)}, bf16[2,128,128]{2,1,0:T(8,128)(2,1)S(1)}, u32[]{:S(2)}, u32[]{:S(2)}) collective-permute-start(bf16[2,128,128]{2,1,0:T(8,128)(2,1)S(1)} %shard_map.143.refs_0_), channel_id=1, source_target_pairs={{0,6},{1,7},{2,0},{3,1},{4,2},{5,3},{6,4},{7,5},{8,14},{9,15},{10,... | collective-permute-start | bytes 196616 | tf_op jit(solution)/shard_map/ppermute | solution.py:65
  85.1 6.5 %collective-permute-start.28 = (bf16[2,128,128]{2,1,0:T(8,128)(2,1)S(1)}, bf16[2,128,128]{2,1,0:T(8,128)(2,1)S(1)}, u32[]{:S(2)}, u32[]{:S(2)}) collective-permute-start(bf16[2,128,128]{2,1,0:T(8,128)(2,1)S(1)} %shard_map.143.refs_0_), channel_id=1, source_target_pairs={{0,1},{1,0},{2,3},{3,2},{4,5},{5,4},{6,7},{7,6},{8,9},{9,8},{10,11... | collective-permute-start | bytes 196616 | tf_op jit(solution)/shard_map/ppermute | solution.py:69
  (21 other events, 172.8 us)

commit v5 on v4

--- a/solution.py
+++ b/solution.py
@@ -14,7 +14,7 @@
 PLEN = 4096
 TLEN = 256
 FIRST = 2048
-LATER = ((2048, 2048),)
+LATER = ((2048, 1024), (3072, 1024))
 MSG = 80
 EPS = 1e-06
 NEG = -1e30

time: 94.6 us -> 94.3 us (level)
  transfers between devices with their start and end apart: 32 -> 32, of which waited for: 14 -> 13; matrix products, arithmetic and copies ran while one was open for 0% -> 0% of each run, Pallas kernels for 14% -> 14%
where the time goes in v5:
time: 94.3 us; the launch traced here: 94.4 us
  starting transfers between devices  53 us (56%)
  Pallas kernels  19.5 us (21%)
  waiting for transfers between devices  18 us (19%)
  local copies, waits for them, and re-layouts  2.46 us (3%)
  between operations  1.03 us (1%)
    ppermute x18, starting transfers between devices, shift(): return lax.ppermute(value, AXES, ring(first, step))  25.7 us
    pallas_call x15, Pallas kernels, call(): pl.pallas_call(kernel, out_shape=out_shape, in_specs=specs, out_specs=out...  19.5 us
    ppermute x5, starting transfers between devices, swap_core(): return lax.ppermute(value, 'narrow', [(n, n ^ 1) for n in range(8)])  15.2 us
    ppermute x18, waiting for transfers between devices, shift(): return lax.ppermute(value, AXES, ring(first, step))  11.1 us
    ppermute x6, starting transfers between devices, shift_x(): lax.ppermute(value, 'narrow', [(n, (n + 2 * step) % 8) for n in range(8)])  8.58 us
    ppermute x3, starting transfers between devices, shift_pair(): return lax.ppermute(value, AXES, pairs)  3.55 us
    ppermute x3, waiting for transfers between devices, shift_pair(): return lax.ppermute(value, AXES, pairs)  2.6 us
    unnamed x26, local copies, waits for them, and re-layouts  2.46 us
  transfers between devices with their start and end apart: 32, of which 13 were waited for; matrix products, arithmetic and copies ran while one was open for 0% of the time, Pallas kernels for 14%

profile of v5, /device:TPU:1, one launch (start us, length us, event | category | flops | bytes accessed | tf_op | source)
XLA Modules:
  0.0 94.4 jit_solution(5164519019822685046)
XLA Ops:
  0.6 1.6 %shard_map.130.w0 = bf16[128,768]{1,0:T(8,128)(2,1)} custom-call(bf16[128,512]{1,0:T(8,128)(2,1)} %w_qkv.1, bf16[256,128]{1,0:T(8,128)(2,1)} %w_out.1), custom_call_target="tpu_custom_call" | custom-call | flops 1048576 | bytes 1048576 | tf_op jit(solution)/shard_map/pallas_call | solution.py:86
  2.2 2.5 %collective-permute-start = (bf16[128,768]{1,0:T(8,128)(2,1)}, bf16[128,768]{1,0:T(8,128)(2,1)S(1)}, u32[]{:S(2)}, u32[]{:S(2)}) collective-permute-start(bf16[128,768]{1,0:T(8,128)(2,1)} %shard_map.130.w0), channel_id=1, source_target_pairs={{0,8},{1,33},{2,10},{3,35},{4,12},{5,37},{6,14},{7,39},{8,16},{9,4... | collective-permute-start | bytes 589832 | tf_op jit(solution)/shard_map/ppermute | solution.py:48
  4.8 3.3 %collective-permute-start.1 = (bf16[128,768]{1,0:T(8,128)(2,1)}, bf16[128,768]{1,0:T(8,128)(2,1)S(1)}, u32[]{:S(2)}, u32[]{:S(2)}) collective-permute-start(bf16[128,768]{1,0:T(8,128)(2,1)} %shard_map.130.w0), channel_id=1, source_target_pairs={{0,16},{1,65},{2,18},{3,67},{4,20},{5,69},{6,22},{7,71},{8,24},{9,... | collective-permute-start | bytes 589832 | tf_op jit(solution)/shard_map/ppermute | solution.py:48
  11.6 1.7 %shard_map.132 = (s32[64]{0:T(128)S(1)}, f32[128,128]{1,0:T(8,128)S(1)}) custom-call(s32[4]{0:T(128)S(1)} %pad_add_fusion.ids, s32[64]{0:T(128)S(1)} %copy-done.7, s32[64]{0:T(128)S(1)} %copy-done.8, s32[64]{0:T(128)S(1)} %copy-done.3, f32[1,128]{1,0:T(1,128)S(1)} %fusion.2.freq), custom_call_target="tpu_custom_call" | custom-call | flops 1048576 | bytes 1048576 | tf_op jit(solution)/shard_map/pallas_call | solution.py:86
  15.4 2.6 %collective-permute-start.4 = (bf16[4,128,256]{2,1,0:T(8,128)(2,1)S(1)}, bf16[4,128,256]{2,1,0:T(8,128)(2,1)S(1)}, u32[]{:S(2)}, u32[]{:S(2)}) collective-permute-start(bf16[4,128,256]{2,1,0:T(8,128)(2,1)S(1)} %get-tuple-element.59.w0), channel_id=1, source_target_pairs={{0,64},{1,17},{2,66},{3,19},{4,68},{5,21},{6,70},{7,23},{8,72},{9,... | collective-permute-start | bytes 786440 | tf_op jit(solution)/shard_map/ppermute | solution.py:48
  18.0 1.6 %collective-permute-start.5 = (bf16[4,128,256]{2,1,0:T(8,128)(2,1)S(1)}, bf16[4,128,256]{2,1,0:T(8,128)(2,1)S(1)}, u32[]{:S(2)}, u32[]{:S(2)}) collective-permute-start(bf16[4,128,256]{2,1,0:T(8,128)(2,1)S(1)} %get-tuple-element.59.w0), channel_id=1, source_target_pairs={{0,96},{1,25},{2,98},{3,27},{4,100},{5,29},{6,102},{7,31},{8,104},... | collective-permute-start | bytes 786440 | tf_op jit(solution)/shard_map/ppermute | solution.py:48
  19.6 2.6 %collective-permute-done.15.w1 = bf16[4,128,512]{2,1,0:T(8,128)(2,1)S(1)} collective-permute-done((bf16[4,128,512]{2,1,0:T(8,128)(2,1)S(1)}, bf16[4,128,512]{2,1,0:T(8,128)(2,1)S(1)}, u32[]{:S(2)}, u32[]{:S(2)}) %collective-permute-start.15) | collective-permute-done | bytes 524320 | tf_op jit(solution)/shard_map/ppermute | solution.py:61
  22.2 2.4 %collective-permute-start.17 = (bf16[4,128,512]{2,1,0:T(8,128)(2,1)S(1)}, bf16[4,128,512]{2,1,0:T(8,128)(2,1)S(1)}, u32[]{:S(2)}, u32[]{:S(2)}) collective-permute-start(bf16[4,128,512]{2,1,0:T(8,128)(2,1)S(1)} %collective-permute-done.15.w1), channel_id=1, source_target_pairs={{0,96},{1,25},{2,98},{3,27},{4,100},{5,29},{6,102},{7,31},{8,104},... | collective-permute-start | bytes 1572872 | tf_op jit(solution)/shard_map/ppermute | solution.py:61
  24.9 5.1 %collective-permute-done.4.w2 = bf16[4,128,256]{2,1,0:T(8,128)(2,1)S(1)} collective-permute-done((bf16[4,128,256]{2,1,0:T(8,128)(2,1)S(1)}, bf16[4,128,256]{2,1,0:T(8,128)(2,1)S(1)}, u32[]{:S(2)}, u32[]{:S(2)}) %collective-permute-start.4) | collective-permute-done | bytes 262176 | tf_op jit(solution)/shard_map/ppermute | solution.py:48
  32.2 2.1 %collective-permute-start.7 = (bf16[4,64,128]{2,1,0:T(8,128)(2,1)S(1)}, bf16[4,64,128]{2,1,0:T(8,128)(2,1)S(1)}, u32[]{:S(2)}, u32[]{:S(2)}) collective-permute-start(bf16[4,64,128]{2,1,0:T(8,128)(2,1)S(1)} %shard_map.134.queries.x0), channel_id=1, source_target_pairs={{0,16},{1,65},{2,18},{3,67},{4,20},{5,69},{6,22},{7,71},{8,24},{9,... | collective-permute-start | bytes 196616 | tf_op jit(solution)/shard_map/ppermute | solution.py:48
  35.2 2.4 %shard_map.135 = (f32[128,128]{1,0:T(8,128)S(1)}, f32[128,128]{1,0:T(8,128)S(1)}) custom-call(s32[64]{0:T(128)S(1)} %copy-done.3, bf16[4,64,128]{2,1,0:T(8,128)(2,1)S(1)} %shard_map.134.queries.x0, bf16[2,64,256,128]{3,2,1,0:T(8,128)(2,1)S(1)} %bitcast.9), custom_call_target="tpu_custom_call" | custom-call | flops 134217728 | bytes 4194304 | tf_op jit(solution)/shard_map/pallas_call | solution.py:86
  40.5 2.4 %shard_map.137 = (f32[128,128]{1,0:T(8,128)S(1)}, f32[128,128]{1,0:T(8,128)S(1)}) custom-call(s32[64]{0:T(128)S(1)} %copy-done.3, bf16[4,64,128]{2,1,0:T(8,128)(2,1)S(1)} %shard_map.134.queries.x0, bf16[2,64,256,128]{3,2,1,0:T(8,128)(2,1)S(1)} %bitcast.9), custom_call_target="tpu_custom_call" | custom-call | flops 134217728 | bytes 4194304 | tf_op jit(solution)/shard_map/pallas_call | solution.py:86
  43.7 3.0 %shard_map.138.x0 = bf16[4,80,128]{2,1,0:T(8,128)(2,1)S(1)} custom-call(s32[64]{0:T(128)S(1)} %get-tuple-element.53.index.table, bf16[4,64,128]{2,1,0:T(8,128)(2,1)S(1)} %get-tuple-element.73.r0, bf16[4,64,128]{2,1,0:T(8,128)(2,1)S(1)} %collective-permute-done.9.r1, bf16[4,64,128]{2,1,0:T(8,128)(2,1)S(1)} %collective-permute-done.10.r2, ...), custom_call_target="tpu_custom_call" | custom-call | flops 536870912 | bytes 8388608 | tf_op jit(solution)/shard_map/pallas_call | solution.py:86
  46.7 1.6 %collective-permute-start.12 = (bf16[4,80,128]{2,1,0:T(8,128)(2,1)S(1)}, bf16[4,80,128]{2,1,0:T(8,128)(2,1)S(1)}, u32[]{:S(2)}, u32[]{:S(2)}) collective-permute-start(bf16[4,80,128]{2,1,0:T(8,128)(2,1)S(1)} %shard_map.138.x0), channel_id=1, source_target_pairs={{0,8},{1,33},{2,10},{3,35},{4,12},{5,37},{6,14},{7,39},{8,16},{9,4... | collective-permute-start | bytes 245768 | tf_op jit(solution)/shard_map/ppermute | solution.py:48
  48.3 3.6 %collective-permute-start.13 = (bf16[4,80,128]{2,1,0:T(8,128)(2,1)S(1)}, bf16[4,80,128]{2,1,0:T(8,128)(2,1)S(1)}, u32[]{:S(2)}, u32[]{:S(2)}) collective-permute-start(bf16[4,80,128]{2,1,0:T(8,128)(2,1)S(1)} %shard_map.138.x0), channel_id=1, source_target_pairs={{0,16},{1,65},{2,18},{3,67},{4,20},{5,69},{6,22},{7,71},{8,24},{9,... | collective-permute-start | bytes 245768 | tf_op jit(solution)/shard_map/ppermute | solution.py:48
  52.0 1.7 %shard_map.139 = (bf16[2,128,128]{2,1,0:T(8,128)(2,1)}, f32[256,128]{1,0:T(8,128)S(1)}, f32[256,128]{1,0:T(8,128)S(1)}) custom-call(s32[4]{0:T(128)S(1)} %pad_add_fusion.ids, bf16[16,128,128]{2,1,0:T(8,128)(2,1)S(1)} %shard_map.131.normed, bf16[4,128,512]{2,1,0:T(8,128)(2,1)S(1)} %get-tuple-element.77.w0, ...), custom_call_target="tpu_custom_call" | custom-call | flops 134217728 | bytes 3145728 | tf_op jit(solution)/shard_map/pallas_call | solution.py:86
  58.6 2.8 %collective-permute-done.18.c1 = bf16[4,80,128]{2,1,0:T(8,128)(2,1)S(1)} collective-permute-done((bf16[4,80,128]{2,1,0:T(8,128)(2,1)S(1)}, bf16[4,80,128]{2,1,0:T(8,128)(2,1)S(1)}, u32[]{:S(2)}, u32[]{:S(2)}) %collective-permute-start.18) | collective-permute-done | bytes 81952 | tf_op jit(solution)/shard_map/ppermute | solution.py:48
  61.9 1.6 %shard_map.141 = (f32[2,128]{1,0:T(2,128)}, f32[4,2,128,128]{3,2,1,0:T(8,128)S(1)}, bf16[4,2,128,128]{3,2,1,0:T(8,128)(2,1)S(1)}) custom-call(s32[4]{0:T(128)S(1)} %pad_add_fusion.ids, s32[64]{0:T(128)S(1)} %get-tuple-element.53.index.table, bf16[4,80,128]{2,1,0:T(8,128)(2,1)S(1)} %get-tuple-element.87.c0, ...), custom_call_target="tpu_custom_call" | custom-call | flops 134217728 | bytes 3145728 | tf_op jit(solution)/shard_map/pallas_call | solution.py:86
  63.5 8.7 %collective-permute-start.21 = (bf16[4,2,128,128]{3,2,1,0:T(8,128)(2,1)S(1)}, bf16[4,2,128,128]{3,2,1,0:T(8,128)(2,1)S(1)}, u32[]{:S(2)}, u32[]{:S(2)}) collective-permute-start(bf16[4,2,128,128]{3,2,1,0:T(8,128)(2,1)S(1)} %get-tuple-element.94), channel_id=1, source_target_pairs={{0,1},{1,0},{2,3},{3,2},{4,5},{5,4},{6,7},{7,6},{8,9},{9,8},{10,11... | collective-permute-start | bytes 786440 | tf_op jit(solution)/shard_map/ppermute | solution.py:69
  75.2 2.5 %collective-permute-start.23 = (bf16[2,128,128]{2,1,0:T(8,128)(2,1)S(1)}, bf16[2,128,128]{2,1,0:T(8,128)(2,1)S(1)}, u32[]{:S(2)}, u32[]{:S(2)}) collective-permute-start(bf16[2,128,128]{2,1,0:T(8,128)(2,1)S(1)} %get-tuple-element.97), channel_id=1, source_target_pairs={{0,4},{1,5},{2,6},{3,7},{4,0},{5,1},{6,2},{7,3},{8,12},{9,13},{10,... | collective-permute-start | bytes 196616 | tf_op jit(solution)/shard_map/ppermute | solution.py:65
  78.8 1.8 %collective-permute-done.23.g2 = bf16[2,128,128]{2,1,0:T(8,128)(2,1)S(1)} collective-permute-done((bf16[2,128,128]{2,1,0:T(8,128)(2,1)S(1)}, bf16[2,128,128]{2,1,0:T(8,128)(2,1)S(1)}, u32[]{:S(2)}, u32[]{:S(2)}) %collective-permute-start.23) | collective-permute-done | bytes 65568 | tf_op jit(solution)/shard_map/ppermute | solution.py:65
  81.7 3.2 %collective-permute-start.26 = (bf16[2,128,128]{2,1,0:T(8,128)(2,1)S(1)}, bf16[2,128,128]{2,1,0:T(8,128)(2,1)S(1)}, u32[]{:S(2)}, u32[]{:S(2)}) collective-permute-start(bf16[2,128,128]{2,1,0:T(8,128)(2,1)S(1)} %shard_map.143.refs_0_), channel_id=1, source_target_pairs={{0,4},{1,5},{2,6},{3,7},{4,0},{5,1},{6,2},{7,3},{8,12},{9,13},{10,... | collective-permute-start | bytes 196616 | tf_op jit(solution)/shard_map/ppermute | solution.py:65
  85.3 2.7 %collective-permute-start.28 = (bf16[2,128,128]{2,1,0:T(8,128)(2,1)S(1)}, bf16[2,128,128]{2,1,0:T(8,128)(2,1)S(1)}, u32[]{:S(2)}, u32[]{:S(2)}) collective-permute-start(bf16[2,128,128]{2,1,0:T(8,128)(2,1)S(1)} %shard_map.143.refs_0_), channel_id=1, source_target_pairs={{0,1},{1,0},{2,3},{3,2},{4,5},{5,4},{6,7},{7,6},{8,9},{9,8},{10,11... | collective-permute-start | bytes 196616 | tf_op jit(solution)/shard_map/ppermute | solution.py:69
  89.0 1.6 %collective-permute-start.30 = (bf16[2,128,128]{2,1,0:T(8,128)(2,1)S(1)}, bf16[2,128,128]{2,1,0:T(8,128)(2,1)S(1)}, u32[]{:S(2)}, u32[]{:S(2)}) collective-permute-start(bf16[2,128,128]{2,1,0:T(8,128)(2,1)S(1)} %collective-permute-done.26.refs_2_), channel_id=1, source_target_pairs={{0,1},{1,0},{2,3},{3,2},{4,5},{5,4},{6,7},{7,6},{8,9},{9,8},{10,11... | collective-permute-start | bytes 196616 | tf_op jit(solution)/shard_map/ppermute | solution.py:69
  (87 shorter events, 28.2 us)
Async XLA Ops:
  2.2 11.1 %collective-permute-start = (bf16[128,768]{1,0:T(8,128)(2,1)}, bf16[128,768]{1,0:T(8,128)(2,1)S(1)}, u32[]{:S(2)}, u32[]{:S(2)}) collective-permute-start(bf16[128,768]{1,0:T(8,128)(2,1)} %shard_map.130.w0), channel_id=1, source_target_pairs={{0,8},{1,33},{2,10},{3,35},{4,12},{5,37},{6,14},{7,39},{8,16},{9,4... | collective-permute-start | bytes 589832 | tf_op jit(solution)/shard_map/ppermute | solution.py:48
  4.8 9.0 %collective-permute-start.1 = (bf16[128,768]{1,0:T(8,128)(2,1)}, bf16[128,768]{1,0:T(8,128)(2,1)S(1)}, u32[]{:S(2)}, u32[]{:S(2)}) collective-permute-start(bf16[128,768]{1,0:T(8,128)(2,1)} %shard_map.130.w0), channel_id=1, source_target_pairs={{0,16},{1,65},{2,18},{3,67},{4,20},{5,69},{6,22},{7,71},{8,24},{9,... | collective-permute-start | bytes 589832 | tf_op jit(solution)/shard_map/ppermute | solution.py:48
  8.1 5.7 %collective-permute-start.2 = (bf16[128,768]{1,0:T(8,128)(2,1)}, bf16[128,768]{1,0:T(8,128)(2,1)S(1)}, u32[]{:S(2)}, u32[]{:S(2)}) collective-permute-start(bf16[128,768]{1,0:T(8,128)(2,1)} %shard_map.130.w0), channel_id=1, source_target_pairs={{0,24},{1,97},{2,26},{3,99},{4,28},{5,101},{6,30},{7,103},{8,0},{9... | collective-permute-start | bytes 589832 | tf_op jit(solution)/shard_map/ppermute | solution.py:48
  13.8 8.4 %collective-permute-start.15 = (bf16[4,128,512]{2,1,0:T(8,128)(2,1)S(1)}, bf16[4,128,512]{2,1,0:T(8,128)(2,1)S(1)}, u32[]{:S(2)}, u32[]{:S(2)}) collective-permute-start(bf16[4,128,512]{2,1,0:T(8,128)(2,1)S(1)} %get-tuple-element.77.w0), channel_id=1, source_target_pairs={{0,32},{1,9},{2,34},{3,11},{4,36},{5,13},{6,38},{7,15},{8,40},{9,1... | collective-permute-start | bytes 1572872 | tf_op jit(solution)/shard_map/ppermute | solution.py:61
  14.9 10.0 %collective-permute-start.3 = (bf16[4,128,256]{2,1,0:T(8,128)(2,1)S(1)}, bf16[4,128,256]{2,1,0:T(8,128)(2,1)S(1)}, u32[]{:S(2)}, u32[]{:S(2)}) collective-permute-start(bf16[4,128,256]{2,1,0:T(8,128)(2,1)S(1)} %get-tuple-element.59.w0), channel_id=1, source_target_pairs={{0,32},{1,9},{2,34},{3,11},{4,36},{5,13},{6,38},{7,15},{8,40},{9,1... | collective-permute-start | bytes 786440 | tf_op jit(solution)/shard_map/ppermute | solution.py:48
  15.4 14.7 %collective-permute-start.4 = (bf16[4,128,256]{2,1,0:T(8,128)(2,1)S(1)}, bf16[4,128,256]{2,1,0:T(8,128)(2,1)S(1)}, u32[]{:S(2)}, u32[]{:S(2)}) collective-permute-start(bf16[4,128,256]{2,1,0:T(8,128)(2,1)S(1)} %get-tuple-element.59.w0), channel_id=1, source_target_pairs={{0,64},{1,17},{2,66},{3,19},{4,68},{5,21},{6,70},{7,23},{8,72},{9,... | collective-permute-start | bytes 786440 | tf_op jit(solution)/shard_map/ppermute | solution.py:48
  18.0 12.1 %collective-permute-start.5 = (bf16[4,128,256]{2,1,0:T(8,128)(2,1)S(1)}, bf16[4,128,256]{2,1,0:T(8,128)(2,1)S(1)}, u32[]{:S(2)}, u32[]{:S(2)}) collective-permute-start(bf16[4,128,256]{2,1,0:T(8,128)(2,1)S(1)} %get-tuple-element.59.w0), channel_id=1, source_target_pairs={{0,96},{1,25},{2,98},{3,27},{4,100},{5,29},{6,102},{7,31},{8,104},... | collective-permute-start | bytes 786440 | tf_op jit(solution)/shard_map/ppermute | solution.py:48
  19.6 32.4 %collective-permute-start.16 = (bf16[4,128,512]{2,1,0:T(8,128)(2,1)S(1)}, bf16[4,128,512]{2,1,0:T(8,128)(2,1)S(1)}, u32[]{:S(2)}, u32[]{:S(2)}) collective-permute-start(bf16[4,128,512]{2,1,0:T(8,128)(2,1)S(1)} %get-tuple-element.77.w0), channel_id=1, source_target_pairs={{0,96},{1,25},{2,98},{3,27},{4,100},{5,29},{6,102},{7,31},{8,104},... | collective-permute-start | bytes 1572872 | tf_op jit(solution)/shard_map/ppermute | solution.py:61
  22.2 29.7 %collective-permute-start.17 = (bf16[4,128,512]{2,1,0:T(8,128)(2,1)S(1)}, bf16[4,128,512]{2,1,0:T(8,128)(2,1)S(1)}, u32[]{:S(2)}, u32[]{:S(2)}) collective-permute-start(bf16[4,128,512]{2,1,0:T(8,128)(2,1)S(1)} %collective-permute-done.15.w1), channel_id=1, source_target_pairs={{0,96},{1,25},{2,98},{3,27},{4,100},{5,29},{6,102},{7,31},{8,104},... | collective-permute-start | bytes 1572872 | tf_op jit(solution)/shard_map/ppermute | solution.py:61
  31.1 6.6 %collective-permute-start.6 = (bf16[4,64,128]{2,1,0:T(8,128)(2,1)S(1)}, bf16[4,64,128]{2,1,0:T(8,128)(2,1)S(1)}, u32[]{:S(2)}, u32[]{:S(2)}) collective-permute-start(bf16[4,64,128]{2,1,0:T(8,128)(2,1)S(1)} %shard_map.134.queries.x0), channel_id=1, source_target_pairs={{0,8},{1,33},{2,10},{3,35},{4,12},{5,37},{6,14},{7,39},{8,16},{9,4... | collective-permute-start | bytes 196616 | tf_op jit(solution)/shard_map/ppermute | solution.py:48
  32.2 5.5 %collective-permute-start.7 = (bf16[4,64,128]{2,1,0:T(8,128)(2,1)S(1)}, bf16[4,64,128]{2,1,0:T(8,128)(2,1)S(1)}, u32[]{:S(2)}, u32[]{:S(2)}) collective-permute-start(bf16[4,64,128]{2,1,0:T(8,128)(2,1)S(1)} %shard_map.134.queries.x0), channel_id=1, source_target_pairs={{0,16},{1,65},{2,18},{3,67},{4,20},{5,69},{6,22},{7,71},{8,24},{9,... | collective-permute-start | bytes 196616 | tf_op jit(solution)/shard_map/ppermute | solution.py:48
  38.3 4.7 %collective-permute-start.10 = (bf16[4,64,128]{2,1,0:T(8,128)(2,1)S(1)}, bf16[4,64,128]{2,1,0:T(8,128)(2,1)S(1)}, u32[]{:S(2)}, u32[]{:S(2)}) collective-permute-start(bf16[4,64,128]{2,1,0:T(8,128)(2,1)S(1)} %get-tuple-element.69), channel_id=1, source_target_pairs={{0,64},{1,17},{2,66},{3,19},{4,68},{5,21},{6,70},{7,23},{8,72},{9,... | collective-permute-start | bytes 196616 | tf_op jit(solution)/shard_map/ppermute | solution.py:48
  46.7 7.0 %collective-permute-start.12 = (bf16[4,80,128]{2,1,0:T(8,128)(2,1)S(1)}, bf16[4,80,128]{2,1,0:T(8,128)(2,1)S(1)}, u32[]{:S(2)}, u32[]{:S(2)}) collective-permute-start(bf16[4,80,128]{2,1,0:T(8,128)(2,1)S(1)} %shard_map.138.x0), channel_id=1, source_target_pairs={{0,8},{1,33},{2,10},{3,35},{4,12},{5,37},{6,14},{7,39},{8,16},{9,4... | collective-permute-start | bytes 245768 | tf_op jit(solution)/shard_map/ppermute | solution.py:48
  48.3 6.3 %collective-permute-start.13 = (bf16[4,80,128]{2,1,0:T(8,128)(2,1)S(1)}, bf16[4,80,128]{2,1,0:T(8,128)(2,1)S(1)}, u32[]{:S(2)}, u32[]{:S(2)}) collective-permute-start(bf16[4,80,128]{2,1,0:T(8,128)(2,1)S(1)} %shard_map.138.x0), channel_id=1, source_target_pairs={{0,16},{1,65},{2,18},{3,67},{4,20},{5,69},{6,22},{7,71},{8,24},{9,... | collective-permute-start | bytes 245768 | tf_op jit(solution)/shard_map/ppermute | solution.py:48
  55.8 5.6 %collective-permute-start.18 = (bf16[4,80,128]{2,1,0:T(8,128)(2,1)S(1)}, bf16[4,80,128]{2,1,0:T(8,128)(2,1)S(1)}, u32[]{:S(2)}, u32[]{:S(2)}) collective-permute-start(bf16[4,80,128]{2,1,0:T(8,128)(2,1)S(1)} %get-tuple-element.88), channel_id=1, source_target_pairs={{0,32},{1,9},{2,34},{3,11},{4,36},{5,13},{6,38},{7,15},{8,40},{9,1... | collective-permute-start | bytes 245768 | tf_op jit(solution)/shard_map/ppermute | solution.py:48
  55.9 5.5 %collective-permute-start.19 = (bf16[4,80,128]{2,1,0:T(8,128)(2,1)S(1)}, bf16[4,80,128]{2,1,0:T(8,128)(2,1)S(1)}, u32[]{:S(2)}, u32[]{:S(2)}) collective-permute-start(bf16[4,80,128]{2,1,0:T(8,128)(2,1)S(1)} %get-tuple-element.89), channel_id=1, source_target_pairs={{0,64},{1,17},{2,66},{3,19},{4,68},{5,21},{6,70},{7,23},{8,72},{9,... | collective-permute-start | bytes 245768 | tf_op jit(solution)/shard_map/ppermute | solution.py:48
  57.0 4.8 %collective-permute-start.20 = (bf16[4,80,128]{2,1,0:T(8,128)(2,1)S(1)}, bf16[4,80,128]{2,1,0:T(8,128)(2,1)S(1)}, u32[]{:S(2)}, u32[]{:S(2)}) collective-permute-start(bf16[4,80,128]{2,1,0:T(8,128)(2,1)S(1)} %get-tuple-element.90), channel_id=1, source_target_pairs={{0,96},{1,25},{2,98},{3,27},{4,100},{5,29},{6,102},{7,31},{8,104},... | collective-permute-start | bytes 245768 | tf_op jit(solution)/shard_map/ppermute | solution.py:48
  63.5 9.8 %collective-permute-start.21 = (bf16[4,2,128,128]{3,2,1,0:T(8,128)(2,1)S(1)}, bf16[4,2,128,128]{3,2,1,0:T(8,128)(2,1)S(1)}, u32[]{:S(2)}, u32[]{:S(2)}) collective-permute-start(bf16[4,2,128,128]{3,2,1,0:T(8,128)(2,1)S(1)} %get-tuple-element.94), channel_id=1, source_target_pairs={{0,1},{1,0},{2,3},{3,2},{4,5},{5,4},{6,7},{7,6},{8,9},{9,8},{10,11... | collective-permute-start | bytes 786440 | tf_op jit(solution)/shard_map/ppermute | solution.py:69
  73.9 4.9 %collective-permute-start.22 = (bf16[2,128,128]{2,1,0:T(8,128)(2,1)S(1)}, bf16[2,128,128]{2,1,0:T(8,128)(2,1)S(1)}, u32[]{:S(2)}, u32[]{:S(2)}) collective-permute-start(bf16[2,128,128]{2,1,0:T(8,128)(2,1)S(1)} %get-tuple-element.96), channel_id=1, source_target_pairs={{0,2},{1,3},{2,4},{3,5},{4,6},{5,7},{6,0},{7,1},{8,10},{9,11},{10,... | collective-permute-start | bytes 196616 | tf_op jit(solution)/shard_map/ppermute | solution.py:65
  75.2 5.4 %collective-permute-start.23 = (bf16[2,128,128]{2,1,0:T(8,128)(2,1)S(1)}, bf16[2,128,128]{2,1,0:T(8,128)(2,1)S(1)}, u32[]{:S(2)}, u32[]{:S(2)}) collective-permute-start(bf16[2,128,128]{2,1,0:T(8,128)(2,1)S(1)} %get-tuple-element.97), channel_id=1, source_target_pairs={{0,4},{1,5},{2,6},{3,7},{4,0},{5,1},{6,2},{7,3},{8,12},{9,13},{10,... | collective-permute-start | bytes 196616 | tf_op jit(solution)/shard_map/ppermute | solution.py:65
  81.6 6.4 %collective-permute-start.25 = (bf16[2,128,128]{2,1,0:T(8,128)(2,1)S(1)}, bf16[2,128,128]{2,1,0:T(8,128)(2,1)S(1)}, u32[]{:S(2)}, u32[]{:S(2)}) collective-permute-start(bf16[2,128,128]{2,1,0:T(8,128)(2,1)S(1)} %shard_map.143.refs_0_), channel_id=1, source_target_pairs={{0,2},{1,3},{2,4},{3,5},{4,6},{5,7},{6,0},{7,1},{8,10},{9,11},{10,... | collective-permute-start | bytes 196616 | tf_op jit(solution)/shard_map/ppermute | solution.py:65
  81.7 7.3 %collective-permute-start.26 = (bf16[2,128,128]{2,1,0:T(8,128)(2,1)S(1)}, bf16[2,128,128]{2,1,0:T(8,128)(2,1)S(1)}, u32[]{:S(2)}, u32[]{:S(2)}) collective-permute-start(bf16[2,128,128]{2,1,0:T(8,128)(2,1)S(1)} %shard_map.143.refs_0_), channel_id=1, source_target_pairs={{0,4},{1,5},{2,6},{3,7},{4,0},{5,1},{6,2},{7,3},{8,12},{9,13},{10,... | collective-permute-start | bytes 196616 | tf_op jit(solution)/shard_map/ppermute | solution.py:65
  85.0 5.6 %collective-permute-start.27 = (bf16[2,128,128]{2,1,0:T(8,128)(2,1)S(1)}, bf16[2,128,128]{2,1,0:T(8,128)(2,1)S(1)}, u32[]{:S(2)}, u32[]{:S(2)}) collective-permute-start(bf16[2,128,128]{2,1,0:T(8,128)(2,1)S(1)} %shard_map.143.refs_0_), channel_id=1, source_target_pairs={{0,6},{1,7},{2,0},{3,1},{4,2},{5,3},{6,4},{7,5},{8,14},{9,15},{10,... | collective-permute-start | bytes 196616 | tf_op jit(solution)/shard_map/ppermute | solution.py:65
  85.3 6.5 %collective-permute-start.28 = (bf16[2,128,128]{2,1,0:T(8,128)(2,1)S(1)}, bf16[2,128,128]{2,1,0:T(8,128)(2,1)S(1)}, u32[]{:S(2)}, u32[]{:S(2)}) collective-permute-start(bf16[2,128,128]{2,1,0:T(8,128)(2,1)S(1)} %shard_map.143.refs_0_), channel_id=1, source_target_pairs={{0,1},{1,0},{2,3},{3,2},{4,5},{5,4},{6,7},{7,6},{8,9},{9,8},{10,11... | collective-permute-start | bytes 196616 | tf_op jit(solution)/shard_map/ppermute | solution.py:69
  (21 other events, 174.1 us)
